TPU v7x, 32 devices: a whole 2x2x4 slice. The times are simulated.
32 devices in a mesh: dp: 8 (over z, y), mp: 4 (over x, core).
Axes of the slice: x: 2, y: 2, z: 4, core: 2. Of those that a mesh axis runs over, the one named last changes fastest.
Arguments:
- grad_flat: bfloat16 [8, 5202320], P('dp', 'mp'), may hold values from -4 to 4
- error_flat: bfloat16 [8, 5202320], P('dp', 'mp'), may hold values from -2 to 2
- momentum_flat: float32 [5202320], P('mp'), may hold values from -2 to 2
- warm_x: float32 [3072, 32], replicated, may hold values from -6 to 6
- warm_b: float32 [128, 32], replicated, may hold values from -6 to 6
- warm_c: float32 [128, 32], replicated, may hold values from -6 to 6
- warm_dt: float32 [48, 32], replicated, may hold values from -6 to 6
- part_order: int32 [6], replicated, may hold values from 0 to 5, each once
Outputs:
- error_next: bfloat16 [8, 5202320], P('dp', 'mp')
- momentum_next: float32 [5202320], P('mp')
Inputs may be any that keep to these rules, and one draw needn't show every extreme that they name: `part_order`: each part number appears once.
All inputs are finite; a program needn't handle non-finite values.
Results may differ from a plain program's by a relative error of at most 0.0017.
Values sent between devices are 32-bit elements; how exact they have to be, the bound alone decides.
No kernel may reach another device: no remote copies, remote signals or barrier semaphores. Data moves between devices by JAX's collectives and lax.ppermute only.
A program may use at most 64 MiB of HBM per device.

v0:
```python
import functools

import jax
import jax.numpy as jnp
from jax import lax
from jax.experimental import pallas as pl
from jax.experimental.pallas import tpu as pltpu
from jax.sharding import PartitionSpec as P

D = 1536
DI = 3072
DS = 128
NH = 48
KW = 4
RANK = 32
NS_STEPS = 5
CONV_CH = 3328
VEC = 3472
LANES = 128

momentum_decay = 0.9
ns_first = 3.4445
ns_second = -4.775
ns_third = 2.0315

COL_B = DI
COL_C = DI + DS
COL_DT = DI + 2 * DS
COLS = DI + 3 * DS
GRAM = COLS
WIDE = COLS + LANES
CHUNKS = DI // LANES

f32 = jnp.float32
bf16 = jnp.bfloat16


class Plan:
    def __init__(self, blocks):
        self.rows = D // blocks
        self.sizes = [
            D * DI // blocks,
            D * DS // blocks,
            D * DS // blocks,
            D * NH // blocks,
            CONV_CH * KW // blocks,
            VEC // blocks,
        ]
        self.total = sum(self.sizes)
        self.flat_rows = -(-self.total // LANES)
        self.buf_rows = (self.flat_rows + 15) // 8 * 8 + 16
        self.dt_groups = self.rows // 8
        self.conv_rows = self.sizes[4] // LANES
        self.conv_pad = -(-self.conv_rows // 8) * 8
        self.vec_rows = -(-self.sizes[5] // LANES)
        self.vec_pad = -(-self.vec_rows // 8) * 8
        self.panel_rows = self.rows + self.conv_pad + self.vec_pad


def starts_of(order_ref, sizes):
    zero = jnp.int32(0)
    first = [zero] * 6
    run = zero
    for place in range(6):
        part = order_ref[place]
        size = zero
        for k in range(6):
            here = part == k
            first[k] = jnp.where(here, run, first[k])
            size = jnp.where(here, jnp.int32(sizes[k]), size)
        run = run + size
    return [lax.shift_right_logical(o, 7) for o in first], [jnp.bitwise_and(o, 127) for o in first]


def lane_of(shape):
    return lax.broadcasted_iota(jnp.int32, shape, len(shape) - 1)


def split2(x):
    hi = x.astype(bf16)
    return hi, (x - hi.astype(f32)).astype(bf16)


def split3(x):
    hi = x.astype(bf16)
    rest = x - hi.astype(f32)
    mid = rest.astype(bf16)
    return hi, mid, (rest - mid.astype(f32)).astype(bf16)


def dot_nt(a, b):
    return lax.dot_general(a, b, (((1,), (1,)), ((), ())), preferred_element_type=f32)


def dot_tn(a, b):
    return lax.dot_general(a, b, (((0,), (0,)), ((), ())), preferred_element_type=f32)


def dot_exact(a, b):
    return lax.dot_general(
        a, b, (((1,), (0,)), ((), ())), preferred_element_type=f32, precision=lax.Precision.HIGHEST
    )


def spread(x, group):
    x = jnp.where(lane_of(x.shape) // RANK == group, x, 0.0)
    x = x + pltpu.roll(x, 64, 1)
    return x + pltpu.roll(x, 32, 1)


def panel_kernel(plan, order_ref, g_ref, e_ref, wx_ref, wb_ref, wc_ref, wd_ref, pp_ref, mh_ref, ml_ref, m_ref, dt_ref, w_ref):
    rows = plan.rows
    total = plan.total

    def merged(at, width):
        return g_ref[0:1, pl.ds(at, width)].astype(f32) + e_ref[0:1, pl.ds(at, width)].astype(f32)

    full = total // 1024
    unroll = 8

    def merge(i, _):
        for u in range(unroll):
            at = pl.multiple_of(i * (1024 * unroll), 1024) + 1024 * u
            m_ref[pl.ds(pl.multiple_of(i * (8 * unroll), 8) + 8 * u, 8), :] = merged(at, 1024).reshape(8, LANES)
        return 0

    lax.fori_loop(0, full // unroll, merge, 0)
    for i in range(full // unroll * unroll, full):
        m_ref[8 * i : 8 * i + 8, :] = merged(1024 * i, 1024).reshape(8, LANES)
    for r in range(8 * full, total // LANES):
        m_ref[r : r + 1, :] = merged(LANES * r, LANES)
    rest = total % LANES
    if rest:
        r = total // LANES
        m_ref[r : r + 1, 0:rest] = merged(LANES * r, rest)

    row, lane = starts_of(order_ref, plan.sizes)

    def turn(x, s):
        return pltpu.roll(x, jnp.bitwise_and(LANES - s, 127), 1)

    def put(at, column, tile):
        hi, lo = split2(tile)
        mh_ref[pl.ds(at, 16), column : column + LANES] = hi
        ml_ref[pl.ds(at, 16), column : column + LANES] = lo

    keep16 = lane_of((16, LANES))

    def read_x(i, _):
        base = row[0] + i * (16 * CHUNKS)
        keep = keep16 < LANES - lane[0]
        now = turn(m_ref[pl.ds(base, 16, stride=CHUNKS), :], lane[0])
        for c in range(CHUNKS):
            after = turn(m_ref[pl.ds(base + (c + 1), 16, stride=CHUNKS), :], lane[0])
            put(pl.multiple_of(i * 16, 16), c * LANES, jnp.where(keep, now, after))
            now = after
        return 0

    lax.fori_loop(0, rows // 16, read_x, 0)

    def read_bc(i, _):
        for k, column in ((1, COL_B), (2, COL_C)):
            base = row[k] + i * 16
            now = turn(m_ref[pl.ds(base, 16), :], lane[k])
            after = turn(m_ref[pl.ds(base + 1, 16), :], lane[k])
            put(pl.multiple_of(i * 16, 16), column, jnp.where(keep16 < LANES - lane[k], now, after))
        return 0

    lax.fori_loop(0, rows // 16, read_bc, 0)

    groups = plan.dt_groups
    lanes_dt = lane_of((groups, LANES))
    thirds = [turn(m_ref[pl.ds(row[3] + q, groups, stride=3), :], lane[3]) for q in range(4)]
    thirds = [jnp.where(lanes_dt < LANES - lane[3], thirds[q], thirds[q + 1]) for q in range(3)]
    for b in range(8):
        q, s = divmod(NH * b, LANES)
        piece = thirds[q] if s == 0 else pltpu.roll(thirds[q], LANES - s, 1)
        if s + NH > LANES:
            piece = jnp.where(lanes_dt < LANES - s, piece, pltpu.roll(thirds[q + 1], LANES - s, 1))
        dt_ref[b * groups : (b + 1) * groups, :] = jnp.where(lanes_dt < NH, piece, 0.0)

    def read_dt(i, _):
        at = pl.multiple_of(i * 16, 16)
        put(at, COL_DT, dt_ref[pl.ds(at, 16), :])
        return 0

    lax.fori_loop(0, rows // 16, read_dt, 0)

    shape = (plan.conv_pad, LANES)
    now = turn(m_ref[pl.ds(row[4], plan.conv_pad), :], lane[4])
    after = turn(m_ref[pl.ds(row[4] + 1, plan.conv_pad), :], lane[4])
    conv = jnp.where(lane_of(shape) < LANES - lane[4], now, after)
    conv = jnp.where(lax.broadcasted_iota(jnp.int32, shape, 0) < plan.conv_rows, conv, 0.0)
    pp_ref[rows : rows + plan.conv_pad, :] = conv
    shape = (plan.vec_pad, LANES)
    place = lax.broadcasted_iota(jnp.int32, shape, 0) * LANES + lane_of(shape)
    vec = jnp.where(place < plan.sizes[5], m_ref[pl.ds(row[5], plan.vec_pad), :], 0.0)
    pp_ref[rows + plan.conv_pad :, :] = vec

    w_ref[...] = jnp.zeros_like(w_ref)
    w_ref[:, 0:NH] = wd_ref[...]
    panel = None
    lanes = lane_of((rows, LANES))
    for k, (w, column, width) in enumerate(
        ((wx_ref, 0, DI), (wb_ref, COL_B, DS), (wc_ref, COL_C, DS), (w_ref, COL_DT, LANES))
    ):
        hi, mid, lo = split3(w[...])
        none = jnp.zeros_like(hi)
        part = dot_nt(mh_ref[:, column : column + width], jnp.concatenate([hi, mid, lo, none], 0))
        part = part + dot_nt(ml_ref[:, column : column + width], jnp.concatenate([hi, mid, none, none], 0))
        part = part + pltpu.roll(part, 64, 1)
        part = part + pltpu.roll(part, 32, 1)
        panel = part if k == 0 else jnp.where(lanes >= RANK * k, part, panel)
    pp_ref[0:rows, :] = panel


def factor_kernel(plan, replicas, pp_ref, mh_ref, ml_ref, z_ref):
    rows = plan.rows
    panel = pp_ref[0:rows, :]
    group = lane_of((rows, LANES)) // RANK
    for k, column, width in ((0, 0, DI), (1, COL_B, DS), (2, COL_C, DS), (3, COL_DT, DS)):
        hi, mid, lo = (piece.astype(f32) for piece in split3(spread(panel, k)))
        two = jnp.where(group == 0, hi, jnp.where(group == 1, mid, 0.0))
        three = jnp.where(group == 2, lo, two).astype(bf16)
        two = two.astype(bf16)
        step = min(width, 512)

        def block(at):
            z = dot_tn(three, mh_ref[:, pl.ds(at, step)]) + dot_tn(two, ml_ref[:, pl.ds(at, step)])
            z_ref[:, pl.ds(at, step)] = z[0:32] + z[32:64] + z[64:96]

        if width == step:
            block(column)
        else:
            lax.fori_loop(0, width // step, lambda i, _: (block(pl.multiple_of(i * step, step)), 0)[1], 0)
    gram = lax.dot_general(
        panel, panel, (((0,), (0,)), ((), ())), preferred_element_type=f32, precision=lax.Precision.HIGHEST
    )
    group = lane_of((RANK, LANES)) // RANK
    out = gram[0:RANK]
    for k in range(1, 4):
        out = jnp.where(group == k, gram[RANK * k : RANK * (k + 1)], out)
    z_ref[:, GRAM : GRAM + LANES] = out * (1.0 / replicas)


def output_kernel(plan, replicas, order_ref, z_ref, pp_ref, m_ref, mom_ref, err_ref, next_ref, a_ref, x_ref, s_ref):
    rows = plan.rows
    row, lane = starts_of(order_ref, plan.sizes)

    square = (LANES, LANES)
    down = lax.broadcasted_iota(jnp.int32, square, 0)
    along = lane_of(square)
    same = down // RANK == along // RANK
    eye = jnp.where(down == along, 1.0, 0.0)
    ones = jnp.where(same, 1.0, 0.0)
    gram = z_ref[:, GRAM : GRAM + LANES]
    gram = jnp.where(same, jnp.concatenate([gram] * 4, 0), 0.0)
    trace = dot_exact(dot_exact(ones, gram * eye), ones)
    scale = 1.0 / (jnp.sqrt(trace) + 1e-06)
    scale = jnp.where(same, scale * scale, 0.0)
    gram = gram * scale
    turned = eye
    for step in range(NS_STEPS):
        mixing = ns_first * eye + ns_second * gram + ns_third * dot_exact(gram, gram)
        turned = dot_exact(turned, mixing)
        if step + 1 < NS_STEPS:
            gram = dot_exact(mixing, dot_exact(gram, mixing))
    both = lax.dot_general(
        turned, turned, (((1,), (1,)), ((), ())), preferred_element_type=f32, precision=lax.Precision.HIGHEST
    )
    left = dot_exact(pp_ref[0:rows, :], both * (scale * (1.0 / replicas)))

    group = lane_of((rows, LANES)) // RANK
    for k, column, width in ((0, 0, DI), (1, COL_B, DS), (2, COL_C, DS), (3, COL_DT, DS)):
        hi, mid = (piece.astype(f32) for piece in split2(spread(left, k)))
        lhs = jnp.where(group % 2 == 0, hi, mid).astype(bf16)
        step = min(width, 512)

        def block(at):
            hi, mid = split2(z_ref[:, pl.ds(at, step)])
            rhs = jnp.concatenate([hi, hi, mid, mid], 0)
            x_ref[:, pl.ds(at, step)] = lax.dot_general(
                lhs, rhs, (((1,), (0,)), ((), ())), preferred_element_type=f32
            )

        if width == step:
            block(column)
        else:
            lax.fori_loop(0, width // step, lambda i, _: (block(pl.multiple_of(i * step, step)), 0)[1], 0)

    lanes8 = lane_of((8, LANES))
    first8 = lax.broadcasted_iota(jnp.int32, (8, LANES), 0) == 0
    lanes1 = lane_of((1, LANES))

    def write_x(i, last):
        at = pl.multiple_of(i * 8, 8)
        base = row[0] + i * (8 * CHUNKS)
        keep = lanes8 >= lane[0]
        head = turned0 = pltpu.roll(x_ref[pl.ds(at, 8), 0:LANES], lane[0], 1)
        for c in range(1, CHUNKS):
            now = pltpu.roll(x_ref[pl.ds(at, 8), c * LANES : (c + 1) * LANES], lane[0], 1)
            a_ref[pl.ds(base + c, 8, stride=CHUNKS), :] = jnp.where(keep, now, head)
            head = now
        tail = pltpu.roll(head, 1, 0)
        a_ref[pl.ds(base, 8, stride=CHUNKS), :] = jnp.where(keep, turned0, jnp.where(first8, last, tail))
        return tail

    lax.fori_loop(0, rows // 8, write_x, jnp.zeros((8, LANES), f32))
    last_x = pltpu.roll(x_ref[rows - 8 : rows, DI - LANES : DI], lane[0], 1)[7:8]
    end_x = row[0] + rows * CHUNKS
    a_ref[pl.ds(end_x, 1), :] = jnp.where(lanes1 < lane[0], last_x, a_ref[pl.ds(end_x, 1), :])

    def place(k, count, valid):
        s = lane[k]
        head = pltpu.roll(s_ref[8:16, :], s, 1)[0:1]
        end = pltpu.roll(s_ref[count : count + 8, :], s, 1)[7:8]
        if valid == LANES:
            a_ref[pl.ds(row[k], 1), :] = jnp.where(lanes1 >= s, head, a_ref[pl.ds(row[k], 1), :])
            final = row[k] + count
            a_ref[pl.ds(final, 1), :] = jnp.where(lanes1 < s, end, a_ref[pl.ds(final, 1), :])
            for r in range(1, count, 64):
                n = min(64, count - r)
                now = pltpu.roll(s_ref[8 + r : 8 + r + n, :], s, 1)
                before = pltpu.roll(s_ref[7 + r : 7 + r + n, :], s, 1)
                a_ref[pl.ds(row[k] + r, n), :] = jnp.where(lane_of((n, LANES)) >= s, now, before)
        else:
            a_ref[pl.ds(row[k], count - 1), :] = s_ref[8 : 8 + count - 1, :]
            final = row[k] + count - 1
            end = s_ref[8 + count - 1 : 8 + count, :]
            a_ref[pl.ds(final, 1), :] = jnp.where(lanes1 < valid, end, a_ref[pl.ds(final, 1), :])

    s_ref[8 : 8 + rows, :] = x_ref[:, COL_B : COL_B + DS]
    place(1, rows, LANES)
    s_ref[8 : 8 + rows, :] = x_ref[:, COL_C : COL_C + DS]
    place(2, rows, LANES)
    groups = plan.dt_groups
    lanes_dt = lane_of((groups, LANES))
    for q in range(3):
        third = jnp.zeros((groups, LANES), f32)
        for b in range(8):
            lo = NH * b - LANES * q
            if lo <= -NH or lo >= LANES:
                continue
            piece = x_ref[b * groups : (b + 1) * groups, COL_DT : COL_DT + LANES]
            if lo % LANES:
                piece = pltpu.roll(piece, lo % LANES, 1)
            third = jnp.where((lanes_dt >= lo) & (lanes_dt < lo + NH), piece, third)
        s_ref[pl.ds(8 + q, groups, stride=3), :] = third
    place(3, 3 * groups, LANES)
    s_ref[8 : 8 + plan.conv_pad, :] = pp_ref[rows : rows + plan.conv_pad, :] * (1.0 / replicas)
    place(4, plan.conv_rows, LANES)
    s_ref[8 : 8 + plan.vec_pad, :] = pp_ref[rows + plan.conv_pad :, :] * (1.0 / replicas)
    place(5, plan.vec_rows, plan.sizes[5] - (plan.vec_rows - 1) * LANES)

    total = plan.total
    begin4 = row[4] * LANES + lane[4]
    begin5 = row[5] * LANES + lane[5]

    def finish(at_row, count, width):
        n = count * LANES if count > 1 else width
        at = at_row * LANES
        m = m_ref[pl.ds(at_row, count), 0 : n // count]
        a = a_ref[pl.ds(at_row, count), 0 : n // count]
        index = lax.broadcasted_iota(jnp.int32, m.shape, 0) * LANES + lane_of(m.shape) + at
        in4 = (index >= begin4) & (index < begin4 + plan.sizes[4])
        in5 = (index >= begin5) & (index < begin5 + plan.sizes[5])
        err = jnp.where(in4 | in5, 0.0, m - a)
        err_ref[0:1, pl.ds(at, n)] = err.reshape(1, n).astype(bf16)
        next_ref[pl.ds(at, n)] = momentum_decay * mom_ref[pl.ds(at, n)] + a.reshape(n)

    full = total // 1024
    unroll = 4

    def step(i, _):
        for u in range(unroll):
            finish(pl.multiple_of(i * (8 * unroll), 8) + 8 * u, 8, LANES)
        return 0

    lax.fori_loop(0, full // unroll, step, 0)
    for i in range(full // unroll * unroll, full):
        finish(8 * i, 8, LANES)
    for r in range(8 * full, total // LANES):
        finish(r, 1, LANES)
    if total % LANES:
        finish(total // LANES, 1, total % LANES)


def vmem(count):
    return [pl.BlockSpec(memory_space=pltpu.VMEM)] * count


def call(kernel, order, out_shape, ins, scratch, limit, flops, size):
    specs = ([pl.BlockSpec(memory_space=pltpu.SMEM)] if order is not None else []) + vmem(len(ins))
    args = ([order] if order is not None else []) + list(ins)
    return pl.pallas_call(
        kernel,
        out_shape=out_shape,
        in_specs=specs,
        out_specs=tuple(vmem(len(out_shape))),
        scratch_shapes=scratch,
        compiler_params=pltpu.CompilerParams(vmem_limit_bytes=limit),
        cost_estimate=pl.CostEstimate(flops=flops, bytes_accessed=size, transcendentals=0),
    )(*args)


def exchange(x, axis, bit):
    n = lax.axis_size(axis)
    return lax.ppermute(x, axis, [(i, i ^ bit) for i in range(n)])


def bits(n):
    return [1 << b for b in range((n - 1).bit_length())]


def body(grad_flat, error_flat, momentum_flat, warm_x, warm_b, warm_c, warm_dt, part_order):
    plan = Plan(lax.axis_size("mp"))
    replicas = lax.axis_size("dp")
    rows = plan.rows
    shape = jax.ShapeDtypeStruct
    pp, mh, ml, m = call(
        functools.partial(panel_kernel, plan),
        part_order,
        (
            shape((plan.panel_rows, LANES), f32),
            shape((rows, COLS), bf16),
            shape((rows, COLS), bf16),
            shape((plan.buf_rows, LANES), f32),
        ),
        (grad_flat, error_flat, warm_x.T, warm_b.T, warm_c.T, warm_dt.T),
        [pltpu.VMEM((rows, LANES), f32), pltpu.VMEM((RANK, LANES), f32)],
        40 << 20,
        4 * rows * COLS * LANES,
        6 * plan.total * 4,
    )
    for bit in bits(replicas):
        pp = pp + exchange(pp, "dp", bit)
    (z,) = call(
        functools.partial(factor_kernel, plan, replicas),
        None,
        (shape((RANK, WIDE), f32),),
        (pp, mh, ml),
        [],
        32 << 20,
        4 * rows * COLS * LANES,
        plan.total * 4,
    )
    for bit in bits(lax.axis_size("mp")):
        z = z + exchange(z, "mp", bit)
    for bit in bits(replicas):
        z = z + exchange(z, "dp", bit)
    err, following = call(
        functools.partial(output_kernel, plan, replicas),
        part_order,
        (shape((1, plan.total), bf16), shape((plan.total,), f32)),
        (z, pp, m, momentum_flat),
        [
            pltpu.VMEM((plan.buf_rows, LANES), f32),
            pltpu.VMEM((rows, COLS), f32),
            pltpu.VMEM((rows + 24, LANES), f32),
        ],
        40 << 20,
        2 * rows * COLS * LANES,
        4 * plan.total * 4,
    )
    return err, following


def solution(mesh):
    placed = (P("dp", "mp"), P("dp", "mp"), P("mp"), P(), P(), P(), P(), P())
    return jax.shard_map(
        body, mesh=mesh, in_specs=placed, out_specs=(P("dp", "mp"), P("mp")), check_vma=False
    )
```

profile of v0, /device:TPU:0, one launch (start us, length us, event | category | flops | bytes accessed | tf_op | source)
XLA Modules:
  0.0 134.6 jit_solution(16002326238330152361)
XLA Ops:
  0.6 0.0 copy-start
  0.6 2.5 %copy-done = bf16[1,1300580]{1,0:T(2,128)(2,1)S(1)} copy-done((bf16[1,1300580]{1,0:T(2,128)(2,1)S(1)}, bf16[1,1300580]{1,0:T(2,128)(2,1)}, u32[]{:S(2)}) %copy-start) | copy-done | bytes 2601184
  3.1 0.0 copy-start.1
  3.1 1.0 copy-done.1
  4.1 0.0 copy-start.2
  4.1 0.7 copy-done.2
  4.8 0.0 copy-start.3
  4.8 0.7 copy-done.3
  5.5 0.0 copy-start.4
  5.5 0.7 copy-done.4
  6.3 0.0 copy-start.5
  6.3 0.7 copy-done.5
  6.9 14.0 %shard_map.95 = (f32[424,128]{1,0:T(8,128)S(1)}, bf16[384,3456]{1,0:T(8,128)(2,1)S(1)}, bf16[384,3456]{1,0:T(8,128)(2,1)S(1)}, f32[10192,128]{1,0:T(8,128)}) custom-call(s32[6]{0:T(128)S(1)} %copy-done.5, bf16[1,1300580]{1,0:T(2,128)(2,1)S(1)} %copy-done, bf16[1,1300580]{1,0:T(2,128)(2,1)} %e_ref.1, f32[32,3072]{1,0:T(8,128)S(1)} %bitcast.8, ...), custom_call_target="tpu_custom_call" | custom-call | flops 679477248 | bytes 31213920 | tf_op jit(solution)/shard_map/pallas_call | solution.py:395
  20.9 3.0 %collective-permute-start = (f32[424,128]{1,0:T(8,128)S(1)}, f32[424,128]{1,0:T(8,128)S(1)}, u32[]{:S(2)}, u32[]{:S(2)}) collective-permute-start(f32[424,128]{1,0:T(8,128)S(1)} %get-tuple-element.6), channel_id=1, source_target_pairs={{0,4},{4,0},{8,12},{12,8},{16,20},{20,16},{24,28},{28,24},{1,5},{5... | collective-permute-start | bytes 651272 | tf_op jit(solution)/shard_map/ppermute | solution.py:408
  23.9 5.3 %collective-permute-done = f32[424,128]{1,0:T(8,128)S(1)} collective-permute-done((f32[424,128]{1,0:T(8,128)S(1)}, f32[424,128]{1,0:T(8,128)S(1)}, u32[]{:S(2)}, u32[]{:S(2)}) %collective-permute-start) | collective-permute-done | bytes 217120 | tf_op jit(solution)/shard_map/ppermute | solution.py:408
  29.2 0.0 slice-start.2
  29.2 1.9 %collective-permute-start.1 = (f32[424,128]{1,0:T(8,128)S(1)}, f32[424,128]{1,0:T(8,128)S(1)}, u32[]{:S(2)}, u32[]{:S(2)}) collective-permute-start(f32[424,128]{1,0:T(8,128)S(1)} %add.24), channel_id=1, source_target_pairs={{0,8},{4,12},{8,0},{12,4},{16,24},{20,28},{24,16},{28,20},{1,9},{5... | collective-permute-start | bytes 651272 | tf_op jit(solution)/shard_map/ppermute | solution.py:408
  31.1 4.7 %collective-permute-done.1 = f32[424,128]{1,0:T(8,128)S(1)} collective-permute-done((f32[424,128]{1,0:T(8,128)S(1)}, f32[424,128]{1,0:T(8,128)S(1)}, u32[]{:S(2)}, u32[]{:S(2)}) %collective-permute-start.1) | collective-permute-done | bytes 217120 | tf_op jit(solution)/shard_map/ppermute | solution.py:408
  35.8 0.0 slice-start
  35.8 2.6 %collective-permute-start.2 = (f32[424,128]{1,0:T(8,128)S(1)}, f32[424,128]{1,0:T(8,128)S(1)}, u32[]{:S(2)}, u32[]{:S(2)}) collective-permute-start(f32[424,128]{1,0:T(8,128)S(1)} %add.25), channel_id=1, source_target_pairs={{0,16},{4,20},{8,24},{12,28},{16,0},{20,4},{24,8},{28,12},{1,17},{... | collective-permute-start | bytes 651272 | tf_op jit(solution)/shard_map/ppermute | solution.py:408
  38.4 8.7 %collective-permute-done.2 = f32[424,128]{1,0:T(8,128)S(1)} collective-permute-done((f32[424,128]{1,0:T(8,128)S(1)}, f32[424,128]{1,0:T(8,128)S(1)}, u32[]{:S(2)}, u32[]{:S(2)}) %collective-permute-start.2) | collective-permute-done | bytes 217120 | tf_op jit(solution)/shard_map/ppermute | solution.py:408
  47.1 0.0 slice-start.1
  47.1 0.0 slice-start.3
  47.1 3.2 %shard_map.96 = f32[32,3584]{1,0:T(8,128)S(1)} custom-call(f32[424,128]{1,0:T(8,128)S(1)} %add.26.pp_ref, bf16[384,3456]{1,0:T(8,128)(2,1)S(1)} %get-tuple-element.7.mh_ref, bf16[384,3456]{1,0:T(8,128)(2,1)S(1)} %get-tuple-element.8.ml_ref), custom_call_target="tpu_custom_call" | custom-call | flops 679477248 | bytes 5202320 | tf_op jit(solution)/shard_map/pallas_call | solution.py:395
  50.3 0.1 collective-permute-start.3
  50.4 1.8 %collective-permute-done.3 = f32[32,3584]{1,0:T(8,128)S(1)} collective-permute-done((f32[32,3584]{1,0:T(8,128)S(1)}, f32[32,3584]{1,0:T(8,128)S(1)}, u32[]{:S(2)}, u32[]{:S(2)}) %collective-permute-start.3) | collective-permute-done | bytes 458784 | tf_op jit(solution)/shard_map/ppermute | solution.py:408
  52.2 1.1 collective-permute-start.4
  53.4 11.5 %collective-permute-done.4 = f32[32,3584]{1,0:T(8,128)S(1)} collective-permute-done((f32[32,3584]{1,0:T(8,128)S(1)}, f32[32,3584]{1,0:T(8,128)S(1)}, u32[]{:S(2)}, u32[]{:S(2)}) %collective-permute-start.4) | collective-permute-done | bytes 458784 | tf_op jit(solution)/shard_map/ppermute | solution.py:408
  64.9 1.2 collective-permute-start.5
  66.1 10.6 %collective-permute-done.5 = f32[32,3584]{1,0:T(8,128)S(1)} collective-permute-done((f32[32,3584]{1,0:T(8,128)S(1)}, f32[32,3584]{1,0:T(8,128)S(1)}, u32[]{:S(2)}, u32[]{:S(2)}) %collective-permute-start.5) | collective-permute-done | bytes 458784 | tf_op jit(solution)/shard_map/ppermute | solution.py:408
  76.8 0.3 collective-permute-start.6
  77.1 10.5 %collective-permute-done.6 = f32[32,3584]{1,0:T(8,128)S(1)} collective-permute-done((f32[32,3584]{1,0:T(8,128)S(1)}, f32[32,3584]{1,0:T(8,128)S(1)}, u32[]{:S(2)}, u32[]{:S(2)}) %collective-permute-start.6) | collective-permute-done | bytes 458784 | tf_op jit(solution)/shard_map/ppermute | solution.py:408
  87.7 2.0 %collective-permute-start.7 = (f32[32,3584]{1,0:T(8,128)S(1)}, f32[32,3584]{1,0:T(8,128)S(1)}, u32[]{:S(2)}, u32[]{:S(2)}) collective-permute-start(f32[32,3584]{1,0:T(8,128)S(1)} %add.30), channel_id=1, source_target_pairs={{0,16},{4,20},{8,24},{12,28},{16,0},{20,4},{24,8},{28,12},{1,17},{... | collective-permute-start | bytes 1376264 | tf_op jit(solution)/shard_map/ppermute | solution.py:408
  89.7 18.7 %collective-permute-done.7 = f32[32,3584]{1,0:T(8,128)S(1)} collective-permute-done((f32[32,3584]{1,0:T(8,128)S(1)}, f32[32,3584]{1,0:T(8,128)S(1)}, u32[]{:S(2)}, u32[]{:S(2)}) %collective-permute-start.7) | collective-permute-done | bytes 458784 | tf_op jit(solution)/shard_map/ppermute | solution.py:408
  108.4 0.0 slice-done.2
  108.5 0.0 slice-done
  108.5 0.0 slice-done.1
  108.5 0.0 slice-done.3
  108.5 26.1 %shard_map.97 = (bf16[1,1300580]{1,0:T(2,128)(2,1)}, f32[1300580]{0:T(1024)}) custom-call(s32[6]{0:T(128)S(1)} %copy-done.5, f32[32,3584]{1,0:T(8,128)S(1)} %add.31.z_ref, f32[424,128]{1,0:T(8,128)S(1)} %add.26.pp_ref, f32[10192,128]{1,0:T(8,128)S(1)} %bitcast.5, f32[1300580]{0:T(1024)S(1)} %bitcast.7), custom_call_target="tpu_custom_call" | custom-call | flops 339738624 | bytes 20809280 | tf_op jit(solution)/shard_map/pallas_call | solution.py:395
  (10 shorter events, 0.3 us)
Async XLA Ops:
  0.6 2.5 %copy-start = (bf16[1,1300580]{1,0:T(2,128)(2,1)S(1)}, bf16[1,1300580]{1,0:T(2,128)(2,1)}, u32[]{:S(2)}) copy-start(bf16[1,1300580]{1,0:T(2,128)(2,1)} %g_ref.1) | copy-start | bytes 7803484
  3.1 1.0 copy-start.1
  4.1 0.7 copy-start.2
  4.8 0.7 copy-start.3
  5.5 0.7 copy-start.4
  6.3 0.7 copy-start.5
  20.9 8.3 %collective-permute-start = (f32[424,128]{1,0:T(8,128)S(1)}, f32[424,128]{1,0:T(8,128)S(1)}, u32[]{:S(2)}, u32[]{:S(2)}) collective-permute-start(f32[424,128]{1,0:T(8,128)S(1)} %get-tuple-element.6), channel_id=1, source_target_pairs={{0,4},{4,0},{8,12},{12,8},{16,20},{20,16},{24,28},{28,24},{1,5},{5... | collective-permute-start | bytes 651272 | tf_op jit(solution)/shard_map/ppermute | solution.py:408
  29.2 79.3 %slice-start.2 = ((s8[5206016]{0:T(1024)(128)(4,1)}), s8[4194304]{0:T(1024)(128)(4,1)S(1)}, s32[]{:S(2)}) async-start(s8[5206016]{0:T(1024)(128)(4,1)} %bitcast.6), calls=%async_computation.2 | async-start | bytes 8388608
  29.2 6.6 %collective-permute-start.1 = (f32[424,128]{1,0:T(8,128)S(1)}, f32[424,128]{1,0:T(8,128)S(1)}, u32[]{:S(2)}, u32[]{:S(2)}) collective-permute-start(f32[424,128]{1,0:T(8,128)S(1)} %add.24), channel_id=1, source_target_pairs={{0,8},{4,12},{8,0},{12,4},{16,24},{20,28},{24,16},{28,20},{1,9},{5... | collective-permute-start | bytes 651272 | tf_op jit(solution)/shard_map/ppermute | solution.py:408
  35.8 72.6 %slice-start = ((s8[5218304]{0:T(1024)(128)(4,1)}), s8[4194304]{0:T(1024)(128)(4,1)S(1)}, s32[]{:S(2)}) async-start(s8[5218304]{0:T(1024)(128)(4,1)} %bitcast.4), calls=%async_computation | async-start | bytes 8388608
  35.8 11.2 %collective-permute-start.2 = (f32[424,128]{1,0:T(8,128)S(1)}, f32[424,128]{1,0:T(8,128)S(1)}, u32[]{:S(2)}, u32[]{:S(2)}) collective-permute-start(f32[424,128]{1,0:T(8,128)S(1)} %add.25), channel_id=1, source_target_pairs={{0,16},{4,20},{8,24},{12,28},{16,0},{20,4},{24,8},{28,12},{1,17},{... | collective-permute-start | bytes 651272 | tf_op jit(solution)/shard_map/ppermute | solution.py:408
  47.1 61.4 %slice-start.1 = ((s8[5218304]{0:T(1024)(128)(4,1)}), s8[1024000]{0:T(1024)(128)(4,1)S(1)}, s32[]{:S(2)}) async-start(s8[5218304]{0:T(1024)(128)(4,1)} %bitcast.4), calls=%async_computation.1 | async-start | bytes 2048000
  47.1 61.4 %slice-start.3 = ((s8[5206016]{0:T(1024)(128)(4,1)}), s8[1011712]{0:T(1024)(128)(4,1)S(1)}, s32[]{:S(2)}) async-start(s8[5206016]{0:T(1024)(128)(4,1)} %bitcast.6), calls=%async_computation.3 | async-start | bytes 2023424
  50.3 1.9 %collective-permute-start.3 = (f32[32,3584]{1,0:T(8,128)S(1)}, f32[32,3584]{1,0:T(8,128)S(1)}, u32[]{:S(2)}, u32[]{:S(2)}) collective-permute-start(f32[32,3584]{1,0:T(8,128)S(1)} %shard_map.96), channel_id=1, source_target_pairs={{0,1},{1,0},{2,3},{3,2},{4,5},{5,4},{6,7},{7,6},{8,9},{9,8},{10,11... | collective-permute-start | bytes 1376264 | tf_op jit(solution)/shard_map/ppermute | solution.py:408
  52.2 12.6 %collective-permute-start.4 = (f32[32,3584]{1,0:T(8,128)S(1)}, f32[32,3584]{1,0:T(8,128)S(1)}, u32[]{:S(2)}, u32[]{:S(2)}) collective-permute-start(f32[32,3584]{1,0:T(8,128)S(1)} %add.27), channel_id=1, source_target_pairs={{0,2},{1,3},{2,0},{3,1},{4,6},{5,7},{6,4},{7,5},{8,10},{9,11},{10,... | collective-permute-start | bytes 1376264 | tf_op jit(solution)/shard_map/ppermute | solution.py:408
  64.9 11.8 %collective-permute-start.5 = (f32[32,3584]{1,0:T(8,128)S(1)}, f32[32,3584]{1,0:T(8,128)S(1)}, u32[]{:S(2)}, u32[]{:S(2)}) collective-permute-start(f32[32,3584]{1,0:T(8,128)S(1)} %add.28), channel_id=1, source_target_pairs={{0,4},{4,0},{8,12},{12,8},{16,20},{20,16},{24,28},{28,24},{1,5},{5... | collective-permute-start | bytes 1376264 | tf_op jit(solution)/shard_map/ppermute | solution.py:408
  76.8 10.9 %collective-permute-start.6 = (f32[32,3584]{1,0:T(8,128)S(1)}, f32[32,3584]{1,0:T(8,128)S(1)}, u32[]{:S(2)}, u32[]{:S(2)}) collective-permute-start(f32[32,3584]{1,0:T(8,128)S(1)} %add.29), channel_id=1, source_target_pairs={{0,8},{4,12},{8,0},{12,4},{16,24},{20,28},{24,16},{28,20},{1,9},{5... | collective-permute-start | bytes 1376264 | tf_op jit(solution)/shard_map/ppermute | solution.py:408
  87.7 20.7 %collective-permute-start.7 = (f32[32,3584]{1,0:T(8,128)S(1)}, f32[32,3584]{1,0:T(8,128)S(1)}, u32[]{:S(2)}, u32[]{:S(2)}) collective-permute-start(f32[32,3584]{1,0:T(8,128)S(1)} %add.30), channel_id=1, source_target_pairs={{0,16},{4,20},{8,24},{12,28},{16,0},{20,4},{24,8},{28,12},{1,17},{... | collective-permute-start | bytes 1376264 | tf_op jit(solution)/shard_map/ppermute | solution.py:408
where the time goes:
time: 135 us
  waiting for transfers between devices  71.9 us (53%)
  Pallas kernels  43.2 us (32%)
  starting transfers between devices  12.1 us (9%)
  local copies, waits for them, and re-layouts  6.29 us (5%)
    ppermute x8, waiting for transfers between devices, exchange(): return lax.ppermute(x, axis, [(i, i ^ bit) for i in range(n)])  71.9 us
    pallas_call x3, Pallas kernels, call(): pl.pallas_call(kernel, out_shape=out_shape, in_specs=specs, out_specs=tup...  43.2 us
    ppermute x8, starting transfers between devices, exchange(): return lax.ppermute(x, axis, [(i, i ^ bit) for i in range(n)])  12.1 us
    unnamed x20, local copies, waits for them, and re-layouts  6.29 us
  transfers between devices with their start and end apart: 8, of which 8 were waited for; matrix products, arithmetic and copies ran while one was open for 0% of the time, Pallas kernels for 0%

commit v1 on v0

v1 whole, which is shorter than its diff:
```python
import functools

import jax
import jax.numpy as jnp
from jax import lax
from jax.experimental import pallas as pl
from jax.experimental.pallas import tpu as pltpu
from jax.sharding import PartitionSpec as P

D = 1536
DI = 3072
DS = 128
NH = 48
KW = 4
RANK = 32
NS_STEPS = 5
CONV_CH = 3328
VEC = 3472
LANES = 128

momentum_decay = 0.9
ns_first = 3.4445
ns_second = -4.775
ns_third = 2.0315

COL_B = DI
COL_C = DI + DS
COL_DT = DI + 2 * DS
COLS = DI + 3 * DS
GRAM = COLS
WIDE = COLS + LANES
CHUNKS = DI // LANES

MERGE = 256
FINISH = 128
PIECES = 8

f32 = jnp.float32
bf16 = jnp.bfloat16
HBM = pltpu.MemorySpace.HBM
VMEM = pltpu.MemorySpace.VMEM


class Plan:
    def __init__(self, blocks):
        self.rows = D // blocks
        self.sizes = [
            D * DI // blocks,
            D * DS // blocks,
            D * DS // blocks,
            D * NH // blocks,
            CONV_CH * KW // blocks,
            VEC // blocks,
        ]
        self.total = sum(self.sizes)
        self.flat_rows = -(-self.total // LANES)
        self.buf_rows = (self.flat_rows + 15) // 8 * 8 + 16
        self.dt_groups = self.rows // 8
        self.conv_rows = self.sizes[4] // LANES
        self.conv_pad = -(-self.conv_rows // 8) * 8
        self.vec_rows = -(-self.sizes[5] // LANES)
        self.vec_pad = -(-self.vec_rows // 8) * 8
        self.panel_rows = self.rows + self.conv_pad + self.vec_pad
        self.shift = self.sizes[5] % LANES
        self.half = -(-self.panel_rows // 16) * 8
        step = -(-self.flat_rows // (PIECES * MERGE)) * MERGE
        cuts = list(range(0, self.flat_rows, step)) + [self.flat_rows]
        self.pieces = list(zip(cuts, cuts[1:]))


def starts_of(order_ref, sizes):
    zero = jnp.int32(0)
    first = [zero] * 6
    run = zero
    for place in range(6):
        part = order_ref[place]
        size = zero
        for k in range(6):
            here = part == k
            first[k] = jnp.where(here, run, first[k])
            size = jnp.where(here, jnp.int32(sizes[k]), size)
        run = run + size
    return [lax.shift_right_logical(o, 7) for o in first], [jnp.bitwise_and(o, 127) for o in first]


def lane_of(shape):
    return lax.broadcasted_iota(jnp.int32, shape, len(shape) - 1)


def split2(x):
    hi = x.astype(bf16)
    return hi, (x - hi.astype(f32)).astype(bf16)


def split3(x):
    hi = x.astype(bf16)
    rest = x - hi.astype(f32)
    mid = rest.astype(bf16)
    return hi, mid, (rest - mid.astype(f32)).astype(bf16)


def dot_nt(a, b):
    return lax.dot_general(a, b, (((1,), (1,)), ((), ())), preferred_element_type=f32)


def dot_tn(a, b):
    return lax.dot_general(a, b, (((0,), (0,)), ((), ())), preferred_element_type=f32)


def dot_exact(a, b):
    return lax.dot_general(
        a, b, (((1,), (0,)), ((), ())), preferred_element_type=f32, precision=lax.Precision.HIGHEST
    )


def spread(x, group):
    x = jnp.where(lane_of(x.shape) // RANK == group, x, 0.0)
    x = x + pltpu.roll(x, 64, 1)
    return x + pltpu.roll(x, 32, 1)


def panel_kernel(plan, order_hbm, g_hbm, e_hbm, wx_hbm, wb_hbm, wc_hbm, wd_hbm, top_ref, low_ref, mh_ref, ml_ref, m_ref, order_ref, g_ref, e_ref, wx_ref, wb_ref, wc_ref, wd_ref, dt_ref, w_ref, sems):
    rows = plan.rows
    total = plan.total
    shift = plan.shift

    small = [
        pltpu.make_async_copy(src, dst, sems.at[i])
        for i, (src, dst) in enumerate(
            ((order_hbm, order_ref), (wx_hbm, wx_ref), (wb_hbm, wb_ref), (wc_hbm, wc_ref), (wd_hbm, wd_ref))
        )
    ]
    big = []
    for i, (begin, end) in enumerate(plan.pieces):
        part = (slice(0, 1), slice(begin * LANES, min(end * LANES, total)))
        big.append(
            [
                pltpu.make_async_copy(src.at[part], dst.at[part], sems.at[5 + 2 * i + j])
                for j, (src, dst) in enumerate(((g_hbm, g_ref), (e_hbm, e_ref)))
            ]
        )
    for i, pair in enumerate(big):
        for copy in pair:
            copy.start()
        if i == 0:
            for copy in small:
                copy.start()

    def merged(at, width):
        return g_ref[0:1, pl.ds(at, width)].astype(f32) + e_ref[0:1, pl.ds(at, width)].astype(f32)

    for (begin, end), pair in zip(plan.pieces, big):
        for copy in pair:
            copy.wait()
        whole = min(end, total // LANES)

        def merge(i, _):
            r = pl.multiple_of(begin + i * MERGE, 8)
            m_ref[pl.ds(r, MERGE), :] = merged(pl.multiple_of(r * LANES, 1024), MERGE * LANES).reshape(MERGE, LANES)
            return 0

        count = (whole - begin) // MERGE
        lax.fori_loop(0, count, merge, 0)
        r = begin + count * MERGE
        n = (whole - r) // 8 * 8
        if n:
            m_ref[r : r + n, :] = merged(r * LANES, n * LANES).reshape(n, LANES)
        for r in range(r + n, whole):
            m_ref[r : r + 1, :] = merged(LANES * r, LANES)
        if end > whole:
            m_ref[whole : whole + 1, 0 : total % LANES] = merged(LANES * whole, total % LANES)

    for copy in small:
        copy.wait()
    row, lane = starts_of(order_ref, plan.sizes)

    def fetch(base, count, stride, moved):
        step = {} if stride == 1 else {"stride": stride}
        now = m_ref[pl.ds(base, count, **step), :]
        return pltpu.roll(now, LANES - shift, 1) if moved else now

    def joined(base, count, stride, moved):
        now = fetch(base, count, stride, moved)
        if not moved:
            return now
        return jnp.where(lane_of((count, LANES)) < LANES - shift, now, fetch(base + 1, count, stride, moved))

    def either(k, work):
        for moved in (False, True):
            pl.when((lane[k] != 0) == moved)(functools.partial(work, moved))

    def put(at, count, column, tile):
        hi, lo = split2(tile)
        mh_ref[pl.ds(at, count), column : column + LANES] = hi
        ml_ref[pl.ds(at, count), column : column + LANES] = lo

    high = 32

    def read_x(moved):
        keep = lane_of((high, LANES)) < LANES - shift

        def block(i, _):
            base = row[0] + i * (high * CHUNKS)
            at = pl.multiple_of(i * high, high)
            now = fetch(base, high, CHUNKS, moved)
            for c in range(CHUNKS):
                tile = now
                if moved or c + 1 < CHUNKS:
                    now = fetch(base + (c + 1), high, CHUNKS, moved)
                if moved:
                    tile = jnp.where(keep, tile, now)
                put(at, high, c * LANES, tile)
            return 0

        lax.fori_loop(0, rows // high, block, 0)

    either(0, read_x)
    for k, column in ((1, COL_B), (2, COL_C)):
        either(k, lambda moved, k=k, column=column: put(0, rows, column, joined(row[k], rows, 1, moved)))

    groups = plan.dt_groups
    lanes_dt = lane_of((groups, LANES))

    def read_dt(moved):
        thirds = [joined(row[3] + q, groups, 3, moved) for q in range(3)]
        for b in range(8):
            q, s = divmod(NH * b, LANES)
            piece = thirds[q] if s == 0 else pltpu.roll(thirds[q], LANES - s, 1)
            if s + NH > LANES:
                piece = jnp.where(lanes_dt < LANES - s, piece, pltpu.roll(thirds[q + 1], LANES - s, 1))
            dt_ref[b * groups : (b + 1) * groups, :] = jnp.where(lanes_dt < NH, piece, 0.0)

    either(3, read_dt)
    put(0, rows, COL_DT, dt_ref[...])

    low = rows - plan.half

    def read_conv(moved):
        shape = (plan.conv_pad, LANES)
        conv = joined(row[4], plan.conv_pad, 1, moved)
        conv = jnp.where(lax.broadcasted_iota(jnp.int32, shape, 0) < plan.conv_rows, conv, 0.0)
        low_ref[low : low + plan.conv_pad, :] = conv

    either(4, read_conv)
    shape = (plan.vec_pad, LANES)
    place = lax.broadcasted_iota(jnp.int32, shape, 0) * LANES + lane_of(shape)
    vec = jnp.where(place < plan.sizes[5], m_ref[pl.ds(row[5], plan.vec_pad), :], 0.0)
    low_ref[low + plan.conv_pad :, :] = vec

    w_ref[...] = jnp.zeros_like(w_ref)
    w_ref[:, 0:NH] = wd_ref[...]
    panel = None
    lanes = lane_of((rows, LANES))
    for k, (w, column, width) in enumerate(
        ((wx_ref, 0, DI), (wb_ref, COL_B, DS), (wc_ref, COL_C, DS), (w_ref, COL_DT, LANES))
    ):
        hi, mid, lo = split3(w[...])
        none = jnp.zeros_like(hi)
        part = dot_nt(mh_ref[:, column : column + width], jnp.concatenate([hi, mid, lo, none], 0))
        part = part + dot_nt(ml_ref[:, column : column + width], jnp.concatenate([hi, mid, none, none], 0))
        part = part + pltpu.roll(part, 64, 1)
        part = part + pltpu.roll(part, 32, 1)
        panel = part if k == 0 else jnp.where(lanes >= RANK * k, part, panel)
    top_ref[...] = panel[0 : plan.half]
    low_ref[0:low, :] = panel[plan.half :]


def factor_kernel(plan, replicas, top_ref, low_ref, mh_ref, ml_ref, mine0_ref, mine1_ref, other_ref, z_ref):
    rows = plan.rows
    panel = jnp.concatenate([top_ref[...], low_ref[0 : rows - plan.half, :]], 0)
    group = lane_of((rows, LANES)) // RANK
    for k, column, width in ((0, 0, DI), (1, COL_B, DS), (2, COL_C, DS), (3, COL_DT, DS)):
        hi, mid, lo = (piece.astype(f32) for piece in split3(spread(panel, k)))
        two = jnp.where(group == 0, hi, jnp.where(group == 1, mid, 0.0))
        three = jnp.where(group == 2, lo, two).astype(bf16)
        two = two.astype(bf16)
        z = dot_tn(three, mh_ref[:, column : column + width]) + dot_tn(two, ml_ref[:, column : column + width])
        z_ref[:, column : column + width] = z[0:32] + z[32:64] + z[64:96]
    gram = lax.dot_general(
        panel, panel, (((0,), (0,)), ((), ())), preferred_element_type=f32, precision=lax.Precision.HIGHEST
    )
    group = lane_of((RANK, LANES)) // RANK
    out = gram[0:RANK]
    for k in range(1, 4):
        out = jnp.where(group == k, gram[RANK * k : RANK * (k + 1)], out)
    z_ref[:, GRAM : GRAM + LANES] = out * (1.0 / replicas)
    half = RANK // 2
    core = jnp.bitwise_and(lax.axis_index("mp"), 1)
    for mine in (0, 1):

        @pl.when(core == mine)
        def _():
            mine0_ref[...] = z_ref[half * mine : half * mine + half // 2, :]
            mine1_ref[...] = z_ref[half * mine + half // 2 : half * (mine + 1), :]
            other_ref[...] = z_ref[half * (1 - mine) : half * (2 - mine), :]


def output_kernel(plan, replicas, order_ref, mine0_ref, mine1_ref, other0_ref, other1_ref, top_ref, low_ref, m_ref, mom_ref, err_hbm, next_hbm, z_ref, a_ref, x_ref, s_ref, err_ref, next_ref, sems):
    rows = plan.rows
    shift = plan.shift
    row, lane = starts_of(order_ref, plan.sizes)

    quarter = RANK // 4
    core = jnp.bitwise_and(lax.axis_index("mp"), 1)
    for mine in (0, 1):

        @pl.when(core == mine)
        def _():
            for i, ref in enumerate((mine0_ref, mine1_ref, other0_ref, other1_ref)):
                at = (2 * mine + i) % 4 * quarter
                z_ref[at : at + quarter, :] = ref[...]

    square = (LANES, LANES)
    down = lax.broadcasted_iota(jnp.int32, square, 0)
    along = lane_of(square)
    same = down // RANK == along // RANK
    eye = jnp.where(down == along, 1.0, 0.0)
    ones = jnp.where(same, 1.0, 0.0)
    gram = z_ref[:, GRAM : GRAM + LANES]
    gram = jnp.where(same, jnp.concatenate([gram] * 4, 0), 0.0)
    trace = dot_exact(dot_exact(ones, gram * eye), ones)
    scale = 1.0 / (jnp.sqrt(trace) + 1e-06)
    scale = jnp.where(same, scale * scale, 0.0)
    gram = gram * scale
    turned = eye
    for step in range(NS_STEPS):
        mixing = ns_first * eye + ns_second * gram + ns_third * dot_exact(gram, gram)
        turned = dot_exact(turned, mixing)
        if step + 1 < NS_STEPS:
            gram = dot_exact(mixing, dot_exact(gram, mixing))
    both = lax.dot_general(
        turned, turned, (((1,), (1,)), ((), ())), preferred_element_type=f32, precision=lax.Precision.HIGHEST
    )
    panel = jnp.concatenate([top_ref[...], low_ref[0 : rows - plan.half, :]], 0)
    left = dot_exact(panel, both * (scale * (1.0 / replicas)))

    group = lane_of((rows, LANES)) // RANK
    for k, column, width in ((0, 0, DI), (1, COL_B, DS), (2, COL_C, DS), (3, COL_DT, DS)):
        hi, mid = (piece.astype(f32) for piece in split2(spread(left, k)))
        lhs = jnp.where(group % 2 == 0, hi, mid).astype(bf16)
        hi, mid = split2(z_ref[:, column : column + width])
        rhs = jnp.concatenate([hi, hi, mid, mid], 0)
        x_ref[8 : 8 + rows, column : column + width] = lax.dot_general(
            lhs, rhs, (((1,), (0,)), ((), ())), preferred_element_type=f32
        )

    high = 32
    lanes1 = lane_of((1, LANES))

    def right(x):
        return pltpu.roll(x, shift, 1)

    def either(k, work):
        for moved in (False, True):
            pl.when((lane[k] != 0) == moved)(functools.partial(work, moved))

    def write_x(moved):
        keep = lane_of((high, LANES)) >= shift
        if moved:
            s_ref[8 : 8 + rows, :] = right(x_ref[8 : 8 + rows, DI - LANES : DI])

        def block(i, _):
            at = pl.multiple_of(8 + i * high, 8)
            base = row[0] + i * (high * CHUNKS)
            if moved:
                before = s_ref[pl.ds(at - 1, high), :]
            for c in range(CHUNKS):
                now = x_ref[pl.ds(at, high), c * LANES : (c + 1) * LANES]
                if moved:
                    now = right(now)
                    now, before = jnp.where(keep, now, before), now
                a_ref[pl.ds(base + c, high, stride=CHUNKS), :] = now
            return 0

        lax.fori_loop(0, rows // high, block, 0)
        if moved:
            final = row[0] + rows * CHUNKS
            end = s_ref[rows + 7 : rows + 8, :]
            a_ref[pl.ds(final, 1), :] = jnp.where(lanes1 < shift, end, a_ref[pl.ds(final, 1), :])

    either(0, write_x)

    def place(k, ref, column, count):
        columns = slice(column, column + LANES)

        def work(moved):
            if not moved:
                a_ref[pl.ds(row[k], count), :] = ref[8 : 8 + count, columns]
                return
            head = right(ref[8:16, columns])[0:1]
            end = right(ref[count : count + 8, columns])[7:8]
            a_ref[pl.ds(row[k], 1), :] = jnp.where(lanes1 >= shift, head, a_ref[pl.ds(row[k], 1), :])
            final = row[k] + count
            a_ref[pl.ds(final, 1), :] = jnp.where(lanes1 < shift, end, a_ref[pl.ds(final, 1), :])
            n = count - 1
            now = right(ref[9 : 9 + n, columns])
            before = right(ref[8 : 8 + n, columns])
            a_ref[pl.ds(row[k] + 1, n), :] = jnp.where(lane_of((n, LANES)) >= shift, now, before)

        either(k, work)

    place(1, x_ref, COL_B, rows)
    place(2, x_ref, COL_C, rows)
    groups = plan.dt_groups
    lanes_dt = lane_of((groups, LANES))
    for q in range(3):
        third = jnp.zeros((groups, LANES), f32)
        for b in range(8):
            lo = NH * b - LANES * q
            if lo <= -NH or lo >= LANES:
                continue
            piece = x_ref[8 + b * groups : 8 + (b + 1) * groups, COL_DT : COL_DT + LANES]
            if lo % LANES:
                piece = pltpu.roll(piece, lo % LANES, 1)
            third = jnp.where((lanes_dt >= lo) & (lanes_dt < lo + NH), piece, third)
        s_ref[pl.ds(8 + q, groups, stride=3), :] = third
    place(3, s_ref, 0, 3 * groups)
    low = rows - plan.half
    s_ref[8 : 8 + plan.conv_pad, :] = low_ref[low : low + plan.conv_pad, :] * (1.0 / replicas)
    place(4, s_ref, 0, plan.conv_rows)
    vec = low_ref[low + plan.conv_pad :, :] * (1.0 / replicas)
    last = plan.vec_rows - 1
    a_ref[pl.ds(row[5], last), :] = vec[0:last]
    final = row[5] + last
    valid = plan.sizes[5] - last * LANES
    a_ref[pl.ds(final, 1), :] = jnp.where(lanes1 < valid, vec[last : last + 1], a_ref[pl.ds(final, 1), :])

    total = plan.total
    spans = [(row[k] * LANES + lane[k], row[k] * LANES + lane[k] + plan.sizes[k]) for k in (4, 5)]

    def finish(at_row, count, width=LANES):
        n = count * width
        at = at_row * LANES
        a = a_ref[pl.ds(at_row, count), 0:width]
        next_ref[pl.ds(at, n)] = momentum_decay * mom_ref[pl.ds(at, n)] + a.reshape(n)
        near = [(at < end) & (at + n > begin) for begin, end in spans]
        near = near[0] | near[1]

        @pl.when(jnp.logical_not(near))
        def _():
            err = m_ref[pl.ds(at_row, count), 0:width] - a_ref[pl.ds(at_row, count), 0:width]
            err_ref[0:1, pl.ds(at, n)] = err.astype(bf16).reshape(1, n)

        @pl.when(near)
        def _():
            err = m_ref[pl.ds(at_row, count), 0:width] - a_ref[pl.ds(at_row, count), 0:width]
            index = lax.broadcasted_iota(jnp.int32, err.shape, 0) * LANES + lane_of(err.shape) + at
            for begin, end in spans:
                err = jnp.where((index >= begin) & (index < end), 0.0, err)
            err_ref[0:1, pl.ds(at, n)] = err.astype(bf16).reshape(1, n)

    copies = []
    for i, (begin, end) in enumerate(plan.pieces):
        whole = min(end, total // LANES)
        count = (whole - begin) // FINISH
        lax.fori_loop(0, count, lambda j, _: (finish(pl.multiple_of(begin + j * FINISH, 8), FINISH), 0)[1], 0)
        r = begin + count * FINISH
        n = (whole - r) // 8 * 8
        if n:
            finish(r, n)
        for r in range(r + n, whole):
            finish(r, 1)
        if end > whole:
            finish(whole, 1, total % LANES)
        part = slice(begin * LANES, min(end * LANES, total))
        copies.append(pltpu.make_async_copy(err_ref.at[0:1, part], err_hbm.at[0:1, part], sems.at[2 * i]))
        copies.append(pltpu.make_async_copy(next_ref.at[part], next_hbm.at[part], sems.at[2 * i + 1]))
        for copy in copies[-2:]:
            copy.start()
    for copy in copies:
        copy.wait()


def specs(*spaces):
    return [pl.BlockSpec(memory_space=space) for space in spaces]


def pairwise(x, first, second):
    n = lax.axis_size("dp") * lax.axis_size("mp")
    return lax.ppermute(x, ("dp", "mp"), [(i, i ^ (second if i % 2 else first)) for i in range(n)])


def butterfly(halves, steps, turns):
    n = len(steps)
    order = [[steps[(i + t) % n] for i in range(n)] for t in turns]
    for i in range(n):
        got = [pairwise(halves[h], order[2 * h][i], order[2 * h + 1][i]) for h in (0, 1)]
        halves = [mine + other for mine, other in zip(halves, got)]
    return halves


def body(grad_flat, error_flat, momentum_flat, warm_x, warm_b, warm_c, warm_dt, part_order):
    blocks = lax.axis_size("mp")
    replicas = lax.axis_size("dp")
    plan = Plan(blocks)
    rows = plan.rows
    total = plan.total
    shape = jax.ShapeDtypeStruct
    pieces = len(plan.pieces)
    dma = pltpu.SemaphoreType.DMA
    top, low, mh, ml, m = pl.pallas_call(
        functools.partial(panel_kernel, plan),
        out_shape=(
            shape((plan.half, LANES), f32),
            shape((plan.panel_rows - plan.half, LANES), f32),
            shape((rows, COLS), bf16),
            shape((rows, COLS), bf16),
            shape((plan.buf_rows, LANES), f32),
        ),
        in_specs=specs(*[HBM] * 7),
        out_specs=tuple(specs(*[VMEM] * 5)),
        scratch_shapes=[
            pltpu.SMEM((6,), jnp.int32),
            pltpu.VMEM((1, total), bf16),
            pltpu.VMEM((1, total), bf16),
            pltpu.VMEM((RANK, DI), f32),
            pltpu.VMEM((RANK, DS), f32),
            pltpu.VMEM((RANK, DS), f32),
            pltpu.VMEM((RANK, NH), f32),
            pltpu.VMEM((rows, LANES), f32),
            pltpu.VMEM((RANK, LANES), f32),
            dma((5 + 2 * pieces,)),
        ],
        compiler_params=pltpu.CompilerParams(vmem_limit_bytes=36 << 20),
        cost_estimate=pl.CostEstimate(flops=4 * rows * COLS * LANES, bytes_accessed=8 * total, transcendentals=0),
    )(*(pltpu.with_memory_space_constraint(x, HBM) for x in (part_order, grad_flat, error_flat, warm_x.T, warm_b.T, warm_c.T, warm_dt.T)))

    inner = [1 << b for b in range(1, (blocks - 1).bit_length())]
    outer = [blocks << b for b in range((replicas - 1).bit_length())]
    n = len(outer)
    top, low = butterfly([top, low], outer, (0, n - 1, 1, 0))

    mine0, mine1, other = pl.pallas_call(
        functools.partial(factor_kernel, plan, replicas),
        out_shape=(shape((RANK // 4, WIDE), f32), shape((RANK // 4, WIDE), f32), shape((RANK // 2, WIDE), f32)),
        in_specs=specs(*[VMEM] * 4),
        out_specs=tuple(specs(*[VMEM] * 3)),
        scratch_shapes=[pltpu.VMEM((RANK, WIDE), f32)],
        compiler_params=pltpu.CompilerParams(vmem_limit_bytes=24 << 20),
        cost_estimate=pl.CostEstimate(flops=4 * rows * COLS * LANES, bytes_accessed=4 * total, transcendentals=0),
    )(top, low, mh, ml)
    got = pairwise(other, 1, 1)
    steps = inner + outer
    n = len(steps)
    halves = butterfly(
        [mine0 + got[: RANK // 4], mine1 + got[RANK // 4 :]], steps, (0, n // 2, 1, 1 + n // 2)
    )
    others = [pairwise(half, 1, 1) for half in halves]

    return pl.pallas_call(
        functools.partial(output_kernel, plan, replicas),
        out_shape=(shape((1, total), bf16), shape((total,), f32)),
        in_specs=specs(pltpu.SMEM, *[VMEM] * 8),
        out_specs=tuple(specs(HBM, HBM)),
        scratch_shapes=[
            pltpu.VMEM((RANK, WIDE), f32),
            pltpu.VMEM((plan.buf_rows, LANES), f32),
            pltpu.VMEM((rows + 8, COLS), f32),
            pltpu.VMEM((rows + 24, LANES), f32),
            pltpu.VMEM((1, total), bf16),
            pltpu.VMEM((total,), f32),
            dma((2 * pieces,)),
        ],
        compiler_params=pltpu.CompilerParams(vmem_limit_bytes=36 << 20),
        cost_estimate=pl.CostEstimate(flops=2 * rows * COLS * LANES, bytes_accessed=16 * total, transcendentals=0),
    )(part_order, *halves, *others, top, low, m, momentum_flat)


def solution(mesh):
    placed = (P("dp", "mp"), P("dp", "mp"), P("mp"), P(), P(), P(), P(), P())
    return jax.shard_map(
        body, mesh=mesh, in_specs=placed, out_specs=(P("dp", "mp"), P("mp")), check_vma=False
    )
```

time: 135 us -> 72.3 us (0.54)
  waiting for transfers between devices: 71.9 us -> 18.3 us
  Pallas kernels: 43.2 us -> 23.6 us
  starting transfers between devices: 12.1 us -> 30.3 us
  local copies, waits for them, and re-layouts: 6.29 us -> 0.02 us
    ppermute x8 -> x17, waiting for transfers between devices: 71.9 us -> 18.3 us  [pairwise(): lax.ppermute(x, ('dp', 'mp'), [(i, i ^ (second if i % 2 else first)) for...]
    pallas_call x3, Pallas kernels: 43.2 us -> 23.6 us  [the longest x1 13 us: body(): pl.pallas_call(functools.partial(output_kernel, plan, replicas), out_shap...]
    ppermute x8 -> x17, starting transfers between devices: 12.1 us -> 30.3 us  [pairwise(): lax.ppermute(x, ('dp', 'mp'), [(i, i ^ (second if i % 2 else first)) for...]
    unnamed x20 -> x6, local copies, waits for them, and re-layouts: 6.29 us -> 0.02 us
  transfers between devices with their start and end apart: 8 -> 17, of which waited for: 8 -> 13; matrix products, arithmetic and copies ran while one was open for 0% -> 0% of each run, Pallas kernels for 0% -> 0%
where the time goes in v1:
time: 72.3 us; the launch traced here: 73.2 us
  starting transfers between devices  30.3 us (42%)
  Pallas kernels  23.6 us (33%)
  waiting for transfers between devices  18.3 us (25%)
  between operations  0.77 us (1%)
    ppermute x17, starting transfers between devices, pairwise(): lax.ppermute(x, ('dp', 'mp'), [(i, i ^ (second if i % 2 else first)) for...  30.3 us
    ppermute x17, waiting for transfers between devices, pairwise(): lax.ppermute(x, ('dp', 'mp'), [(i, i ^ (second if i % 2 else first)) for...  18.3 us
    pallas_call x1, Pallas kernels, body(): pl.pallas_call(functools.partial(output_kernel, plan, replicas), out_shap...  13 us
    pallas_call x1, Pallas kernels, body(): pl.pallas_call(functools.partial(panel_kernel, plan), out_shape=(shape((p...  8.92 us
    pallas_call x1, Pallas kernels, body(): pl.pallas_call(functools.partial(factor_kernel, plan, replicas), out_shap...  1.64 us
  transfers between devices with their start and end apart: 17, of which 13 were waited for; matrix products, arithmetic and copies ran while one was open for 0% of the time, Pallas kernels for 0%

profile of v1, /device:TPU:0, one launch (start us, length us, event | category | flops | bytes accessed | tf_op | source)
XLA Modules:
  0.0 73.2 jit_solution(5988569135217381651)
XLA Ops:
  0.6 8.9 %shard_map.95 = (f32[216,128]{1,0:T(8,128)S(1)}, f32[208,128]{1,0:T(8,128)S(1)}, bf16[384,3456]{1,0:T(8,128)(2,1)S(1)}, bf16[384,3456]{1,0:T(8,128)(2,1)S(1)}, f32[10192,128]{1,0:T(8,128)S(1)}) custom-call(s32[6]{0:T(128)} %order_ref.1, bf16[1,1300580]{1,0:T(2,128)(2,1)} %g_hbm.1, bf16[1,1300580]{1,0:T(2,128)(2,1)} %e_hbm.1, f32[32,3072]{1,0:T(8,128)} %bitcast.6, ...), custom_call_target="tpu_custom_call" | custom-call | flops 679477248 | bytes 10404640 | tf_op jit(solution)/shard_map/pallas_call | solution.py:501
  9.6 3.0 %collective-permute-start = (f32[216,128]{1,0:T(8,128)S(1)}, f32[216,128]{1,0:T(8,128)S(1)}, u32[]{:S(2)}, u32[]{:S(2)}) collective-permute-start(f32[216,128]{1,0:T(8,128)S(1)} %get-tuple-element.10), channel_id=1, source_target_pairs={{0,4},{1,17},{2,6},{3,19},{4,0},{5,21},{6,2},{7,23},{8,12},{9,25},... | collective-permute-start | bytes 331784 | tf_op jit(solution)/shard_map/ppermute | solution.py:480
  12.6 1.6 %collective-permute-start.3 = (f32[208,128]{1,0:T(8,128)S(1)}, f32[208,128]{1,0:T(8,128)S(1)}, u32[]{:S(2)}, u32[]{:S(2)}) collective-permute-start(f32[208,128]{1,0:T(8,128)S(1)} %get-tuple-element.11), channel_id=1, source_target_pairs={{0,8},{1,5},{2,10},{3,7},{4,12},{5,1},{6,14},{7,3},{8,0},{9,13},{1... | collective-permute-start | bytes 319496 | tf_op jit(solution)/shard_map/ppermute | solution.py:480
  14.2 1.1 %collective-permute-done = f32[216,128]{1,0:T(8,128)S(1)} collective-permute-done((f32[216,128]{1,0:T(8,128)S(1)}, f32[216,128]{1,0:T(8,128)S(1)}, u32[]{:S(2)}, u32[]{:S(2)}) %collective-permute-start) | collective-permute-done | bytes 110624 | tf_op jit(solution)/shard_map/ppermute | solution.py:480
  15.3 2.1 %collective-permute-start.1 = (f32[216,128]{1,0:T(8,128)S(1)}, f32[216,128]{1,0:T(8,128)S(1)}, u32[]{:S(2)}, u32[]{:S(2)}) collective-permute-start(f32[216,128]{1,0:T(8,128)S(1)} %add.48), channel_id=1, source_target_pairs={{0,8},{1,5},{2,10},{3,7},{4,12},{5,1},{6,14},{7,3},{8,0},{9,13},{1... | collective-permute-start | bytes 331784 | tf_op jit(solution)/shard_map/ppermute | solution.py:480
  17.5 0.0 collective-permute-done.3
  17.5 0.0 slice-start
  17.5 0.0 copy-start
  17.5 2.7 %collective-permute-start.4 = (f32[208,128]{1,0:T(8,128)S(1)}, f32[208,128]{1,0:T(8,128)S(1)}, u32[]{:S(2)}, u32[]{:S(2)}) collective-permute-start(f32[208,128]{1,0:T(8,128)S(1)} %add.51), channel_id=1, source_target_pairs={{0,16},{1,9},{2,18},{3,11},{4,20},{5,13},{6,22},{7,15},{8,24},{9,1... | collective-permute-start | bytes 319496 | tf_op jit(solution)/shard_map/ppermute | solution.py:480
  20.3 0.2 collective-permute-done.1
  20.5 3.2 %collective-permute-start.2 = (f32[216,128]{1,0:T(8,128)S(1)}, f32[216,128]{1,0:T(8,128)S(1)}, u32[]{:S(2)}, u32[]{:S(2)}) collective-permute-start(f32[216,128]{1,0:T(8,128)S(1)} %add.49), channel_id=1, source_target_pairs={{0,16},{1,9},{2,18},{3,11},{4,20},{5,13},{6,22},{7,15},{8,24},{9,1... | collective-permute-start | bytes 331784 | tf_op jit(solution)/shard_map/ppermute | solution.py:480
  23.7 0.0 collective-permute-done.4
  23.7 2.2 %collective-permute-start.5 = (f32[208,128]{1,0:T(8,128)S(1)}, f32[208,128]{1,0:T(8,128)S(1)}, u32[]{:S(2)}, u32[]{:S(2)}) collective-permute-start(f32[208,128]{1,0:T(8,128)S(1)} %add.52), channel_id=1, source_target_pairs={{0,4},{1,17},{2,6},{3,19},{4,0},{5,21},{6,2},{7,23},{8,12},{9,25},... | collective-permute-start | bytes 319496 | tf_op jit(solution)/shard_map/ppermute | solution.py:480
  26.0 2.7 %collective-permute-done.5 = f32[208,128]{1,0:T(8,128)S(1)} collective-permute-done((f32[208,128]{1,0:T(8,128)S(1)}, f32[208,128]{1,0:T(8,128)S(1)}, u32[]{:S(2)}, u32[]{:S(2)}) %collective-permute-start.5) | collective-permute-done | bytes 106528 | tf_op jit(solution)/shard_map/ppermute | solution.py:480
  28.7 0.2 collective-permute-done.2
  28.9 0.0 slice-start.1
  28.9 1.6 %shard_map.96 = (f32[8,3584]{1,0:T(8,128)S(1)}, f32[8,3584]{1,0:T(8,128)S(1)}, f32[16,3584]{1,0:T(8,128)S(1)}) custom-call(f32[216,128]{1,0:T(8,128)S(1)} %add.50.top_ref, f32[208,128]{1,0:T(8,128)S(1)} %add.53.low_ref, bf16[384,3456]{1,0:T(8,128)(2,1)S(1)} %get-tuple-element.12.mh_ref, bf16[384,3456]{1,0:T(8,128)(2,1)S(1)} %get-tuple-element.13.ml_ref), custom_call_target="tpu_custom_call" | custom-call | flops 679477248 | bytes 5202320 | tf_op jit(solution)/shard_map/pallas_call | solution.py:533
  30.5 1.0 %collective-permute-start.6 = (f32[16,3584]{1,0:T(8,128)S(1)}, f32[16,3584]{1,0:T(8,128)S(1)}, u32[]{:S(2)}, u32[]{:S(2)}) collective-permute-start(f32[16,3584]{1,0:T(8,128)S(1)} %get-tuple-element.15), channel_id=1, source_target_pairs={{0,1},{1,0},{2,3},{3,2},{4,5},{5,4},{6,7},{7,6},{8,9},{9,8},{10,11... | collective-permute-start | bytes 688136 | tf_op jit(solution)/shard_map/ppermute | solution.py:480
  31.5 1.1 %collective-permute-done.6 = f32[16,3584]{1,0:T(8,128)S(1)} collective-permute-done((f32[16,3584]{1,0:T(8,128)S(1)}, f32[16,3584]{1,0:T(8,128)S(1)}, u32[]{:S(2)}, u32[]{:S(2)}) %collective-permute-start.6) | collective-permute-done | bytes 229408 | tf_op jit(solution)/shard_map/ppermute | solution.py:480
  32.7 2.3 %collective-permute-start.11 = (f32[8,3584]{1,0:T(8,128)S(1)}, f32[8,3584]{1,0:T(8,128)S(1)}, u32[]{:S(2)}, u32[]{:S(2)}) collective-permute-start(f32[8,3584]{1,0:T(8,128)S(1)} %get-tuple-element.18), channel_id=1, source_target_pairs={{0,4},{1,17},{2,6},{3,19},{4,0},{5,21},{6,2},{7,23},{8,12},{9,25},... | collective-permute-start | bytes 344072 | tf_op jit(solution)/shard_map/ppermute | solution.py:480
  35.0 1.5 %collective-permute-start.7 = (f32[8,3584]{1,0:T(8,128)S(1)}, f32[8,3584]{1,0:T(8,128)S(1)}, u32[]{:S(2)}, u32[]{:S(2)}) collective-permute-start(f32[8,3584]{1,0:T(8,128)S(1)} %get-tuple-element.19), channel_id=1, source_target_pairs={{0,2},{1,9},{2,0},{3,11},{4,6},{5,13},{6,4},{7,15},{8,10},{9,1},{1... | collective-permute-start | bytes 344072 | tf_op jit(solution)/shard_map/ppermute | solution.py:480
  36.5 1.3 %collective-permute-done.11 = f32[8,3584]{1,0:T(8,128)S(1)} collective-permute-done((f32[8,3584]{1,0:T(8,128)S(1)}, f32[8,3584]{1,0:T(8,128)S(1)}, u32[]{:S(2)}, u32[]{:S(2)}) %collective-permute-start.11) | collective-permute-done | bytes 114720 | tf_op jit(solution)/shard_map/ppermute | solution.py:480
  37.8 1.2 %collective-permute-start.12 = (f32[8,3584]{1,0:T(8,128)S(1)}, f32[8,3584]{1,0:T(8,128)S(1)}, u32[]{:S(2)}, u32[]{:S(2)}) collective-permute-start(f32[8,3584]{1,0:T(8,128)S(1)} %add.60), channel_id=1, source_target_pairs={{0,8},{1,3},{2,10},{3,1},{4,12},{5,7},{6,14},{7,5},{8,0},{9,11},{1... | collective-permute-start | bytes 344072 | tf_op jit(solution)/shard_map/ppermute | solution.py:480
  38.9 0.8 %collective-permute-done.7 = f32[8,3584]{1,0:T(8,128)S(1)} collective-permute-done((f32[8,3584]{1,0:T(8,128)S(1)}, f32[8,3584]{1,0:T(8,128)S(1)}, u32[]{:S(2)}, u32[]{:S(2)}) %collective-permute-start.7) | collective-permute-done | bytes 114720 | tf_op jit(solution)/shard_map/ppermute | solution.py:480
  39.8 1.0 %collective-permute-start.8 = (f32[8,3584]{1,0:T(8,128)S(1)}, f32[8,3584]{1,0:T(8,128)S(1)}, u32[]{:S(2)}, u32[]{:S(2)}) collective-permute-start(f32[8,3584]{1,0:T(8,128)S(1)} %add.55), channel_id=1, source_target_pairs={{0,4},{1,17},{2,6},{3,19},{4,0},{5,21},{6,2},{7,23},{8,12},{9,25},... | collective-permute-start | bytes 344072 | tf_op jit(solution)/shard_map/ppermute | solution.py:480
  40.7 1.9 %collective-permute-done.12 = f32[8,3584]{1,0:T(8,128)S(1)} collective-permute-done((f32[8,3584]{1,0:T(8,128)S(1)}, f32[8,3584]{1,0:T(8,128)S(1)}, u32[]{:S(2)}, u32[]{:S(2)}) %collective-permute-start.12) | collective-permute-done | bytes 114720 | tf_op jit(solution)/shard_map/ppermute | solution.py:480
  42.6 3.1 %collective-permute-start.13 = (f32[8,3584]{1,0:T(8,128)S(1)}, f32[8,3584]{1,0:T(8,128)S(1)}, u32[]{:S(2)}, u32[]{:S(2)}) collective-permute-start(f32[8,3584]{1,0:T(8,128)S(1)} %add.61), channel_id=1, source_target_pairs={{0,16},{1,5},{2,18},{3,7},{4,20},{5,1},{6,22},{7,3},{8,24},{9,13},... | collective-permute-start | bytes 344072 | tf_op jit(solution)/shard_map/ppermute | solution.py:480
  45.7 0.0 collective-permute-done.8
  45.7 1.6 %collective-permute-start.9 = (f32[8,3584]{1,0:T(8,128)S(1)}, f32[8,3584]{1,0:T(8,128)S(1)}, u32[]{:S(2)}, u32[]{:S(2)}) collective-permute-start(f32[8,3584]{1,0:T(8,128)S(1)} %add.56), channel_id=1, source_target_pairs={{0,8},{1,3},{2,10},{3,1},{4,12},{5,7},{6,14},{7,5},{8,0},{9,11},{1... | collective-permute-start | bytes 344072 | tf_op jit(solution)/shard_map/ppermute | solution.py:480
  47.3 2.5 %collective-permute-done.13 = f32[8,3584]{1,0:T(8,128)S(1)} collective-permute-done((f32[8,3584]{1,0:T(8,128)S(1)}, f32[8,3584]{1,0:T(8,128)S(1)}, u32[]{:S(2)}, u32[]{:S(2)}) %collective-permute-start.13) | collective-permute-done | bytes 114720 | tf_op jit(solution)/shard_map/ppermute | solution.py:480
  49.8 1.6 %collective-permute-start.14 = (f32[8,3584]{1,0:T(8,128)S(1)}, f32[8,3584]{1,0:T(8,128)S(1)}, u32[]{:S(2)}, u32[]{:S(2)}) collective-permute-start(f32[8,3584]{1,0:T(8,128)S(1)} %add.62), channel_id=1, source_target_pairs={{0,2},{1,9},{2,0},{3,11},{4,6},{5,13},{6,4},{7,15},{8,10},{9,1},{1... | collective-permute-start | bytes 344072 | tf_op jit(solution)/shard_map/ppermute | solution.py:480
  51.5 0.3 collective-permute-done.9
  51.8 2.0 %collective-permute-start.10 = (f32[8,3584]{1,0:T(8,128)S(1)}, f32[8,3584]{1,0:T(8,128)S(1)}, u32[]{:S(2)}, u32[]{:S(2)}) collective-permute-start(f32[8,3584]{1,0:T(8,128)S(1)} %add.57), channel_id=1, source_target_pairs={{0,16},{1,5},{2,18},{3,7},{4,20},{5,1},{6,22},{7,3},{8,24},{9,13},... | collective-permute-start | bytes 344072 | tf_op jit(solution)/shard_map/ppermute | solution.py:480
  53.8 0.9 %collective-permute-done.14 = f32[8,3584]{1,0:T(8,128)S(1)} collective-permute-done((f32[8,3584]{1,0:T(8,128)S(1)}, f32[8,3584]{1,0:T(8,128)S(1)}, u32[]{:S(2)}, u32[]{:S(2)}) %collective-permute-start.14) | collective-permute-done | bytes 114720 | tf_op jit(solution)/shard_map/ppermute | solution.py:480
  54.7 0.1 collective-permute-start.16
  54.8 4.0 %collective-permute-done.10 = f32[8,3584]{1,0:T(8,128)S(1)} collective-permute-done((f32[8,3584]{1,0:T(8,128)S(1)}, f32[8,3584]{1,0:T(8,128)S(1)}, u32[]{:S(2)}, u32[]{:S(2)}) %collective-permute-start.10) | collective-permute-done | bytes 114720 | tf_op jit(solution)/shard_map/ppermute | solution.py:480
  58.8 0.1 collective-permute-start.15
  58.8 0.0 collective-permute-done.16.other1_ref
  58.9 1.3 %collective-permute-done.15.other0_ref = f32[8,3584]{1,0:T(8,128)S(1)} collective-permute-done((f32[8,3584]{1,0:T(8,128)S(1)}, f32[8,3584]{1,0:T(8,128)S(1)}, u32[]{:S(2)}, u32[]{:S(2)}) %collective-permute-start.15) | collective-permute-done | bytes 114720 | tf_op jit(solution)/shard_map/ppermute | solution.py:480
  60.2 0.0 slice-done
  60.2 0.0 copy-done
  60.2 0.0 slice-done.1
  60.2 13.0 %shard_map.97 = (bf16[1,1300580]{1,0:T(2,128)(2,1)}, f32[1300580]{0:T(1024)}) custom-call(s32[6]{0:T(128)S(1)} %copy-done, f32[8,3584]{1,0:T(8,128)S(1)} %add.58.mine0_ref, f32[8,3584]{1,0:T(8,128)S(1)} %add.63.mine1_ref, f32[8,3584]{1,0:T(8,128)S(1)} %collective-permute-done.15.other0_ref, f32[8,3584]{1,0:T(8,128)S(1)} %collective-permute-done.16.other1_ref, ...), custom_call_target="tpu_custom_call" | custom-call | flops 339738624 | bytes 20809280 | tf_op jit(solution)/shard_map/pallas_call | solution.py:550
  (16 shorter events, 0.2 us)
Async XLA Ops:
  9.6 5.8 %collective-permute-start = (f32[216,128]{1,0:T(8,128)S(1)}, f32[216,128]{1,0:T(8,128)S(1)}, u32[]{:S(2)}, u32[]{:S(2)}) collective-permute-start(f32[216,128]{1,0:T(8,128)S(1)} %get-tuple-element.10), channel_id=1, source_target_pairs={{0,4},{1,17},{2,6},{3,19},{4,0},{5,21},{6,2},{7,23},{8,12},{9,25},... | collective-permute-start | bytes 331784 | tf_op jit(solution)/shard_map/ppermute | solution.py:480
  12.6 4.9 %collective-permute-start.3 = (f32[208,128]{1,0:T(8,128)S(1)}, f32[208,128]{1,0:T(8,128)S(1)}, u32[]{:S(2)}, u32[]{:S(2)}) collective-permute-start(f32[208,128]{1,0:T(8,128)S(1)} %get-tuple-element.11), channel_id=1, source_target_pairs={{0,8},{1,5},{2,10},{3,7},{4,12},{5,1},{6,14},{7,3},{8,0},{9,13},{1... | collective-permute-start | bytes 319496 | tf_op jit(solution)/shard_map/ppermute | solution.py:480
  15.3 5.1 %collective-permute-start.1 = (f32[216,128]{1,0:T(8,128)S(1)}, f32[216,128]{1,0:T(8,128)S(1)}, u32[]{:S(2)}, u32[]{:S(2)}) collective-permute-start(f32[216,128]{1,0:T(8,128)S(1)} %add.48), channel_id=1, source_target_pairs={{0,8},{1,5},{2,10},{3,7},{4,12},{5,1},{6,14},{7,3},{8,0},{9,13},{1... | collective-permute-start | bytes 331784 | tf_op jit(solution)/shard_map/ppermute | solution.py:480
  17.5 42.7 %slice-start = ((s8[5206016]{0:T(1024)(128)(4,1)}), s8[4194304]{0:T(1024)(128)(4,1)S(1)}, s32[]{:S(2)}) async-start(s8[5206016]{0:T(1024)(128)(4,1)} %bitcast.4), calls=%async_computation | async-start | bytes 8388608
  17.5 42.7 %copy-start = (s32[6]{0:T(128)S(1)}, s32[6]{0:T(128)}, u32[]{:S(2)}) copy-start(s32[6]{0:T(128)} %order_ref.1) | copy-start | bytes 76
  17.5 6.2 %collective-permute-start.4 = (f32[208,128]{1,0:T(8,128)S(1)}, f32[208,128]{1,0:T(8,128)S(1)}, u32[]{:S(2)}, u32[]{:S(2)}) collective-permute-start(f32[208,128]{1,0:T(8,128)S(1)} %add.51), channel_id=1, source_target_pairs={{0,16},{1,9},{2,18},{3,11},{4,20},{5,13},{6,22},{7,15},{8,24},{9,1... | collective-permute-start | bytes 319496 | tf_op jit(solution)/shard_map/ppermute | solution.py:480
  20.5 8.4 %collective-permute-start.2 = (f32[216,128]{1,0:T(8,128)S(1)}, f32[216,128]{1,0:T(8,128)S(1)}, u32[]{:S(2)}, u32[]{:S(2)}) collective-permute-start(f32[216,128]{1,0:T(8,128)S(1)} %add.49), channel_id=1, source_target_pairs={{0,16},{1,9},{2,18},{3,11},{4,20},{5,13},{6,22},{7,15},{8,24},{9,1... | collective-permute-start | bytes 331784 | tf_op jit(solution)/shard_map/ppermute | solution.py:480
  23.7 4.9 %collective-permute-start.5 = (f32[208,128]{1,0:T(8,128)S(1)}, f32[208,128]{1,0:T(8,128)S(1)}, u32[]{:S(2)}, u32[]{:S(2)}) collective-permute-start(f32[208,128]{1,0:T(8,128)S(1)} %add.52), channel_id=1, source_target_pairs={{0,4},{1,17},{2,6},{3,19},{4,0},{5,21},{6,2},{7,23},{8,12},{9,25},... | collective-permute-start | bytes 319496 | tf_op jit(solution)/shard_map/ppermute | solution.py:480
  28.9 31.3 %slice-start.1 = ((s8[5206016]{0:T(1024)(128)(4,1)}), s8[1011712]{0:T(1024)(128)(4,1)S(1)}, s32[]{:S(2)}) async-start(s8[5206016]{0:T(1024)(128)(4,1)} %bitcast.4), calls=%async_computation.1 | async-start | bytes 2023424
  30.5 2.1 %collective-permute-start.6 = (f32[16,3584]{1,0:T(8,128)S(1)}, f32[16,3584]{1,0:T(8,128)S(1)}, u32[]{:S(2)}, u32[]{:S(2)}) collective-permute-start(f32[16,3584]{1,0:T(8,128)S(1)} %get-tuple-element.15), channel_id=1, source_target_pairs={{0,1},{1,0},{2,3},{3,2},{4,5},{5,4},{6,7},{7,6},{8,9},{9,8},{10,11... | collective-permute-start | bytes 688136 | tf_op jit(solution)/shard_map/ppermute | solution.py:480
  32.7 5.1 %collective-permute-start.11 = (f32[8,3584]{1,0:T(8,128)S(1)}, f32[8,3584]{1,0:T(8,128)S(1)}, u32[]{:S(2)}, u32[]{:S(2)}) collective-permute-start(f32[8,3584]{1,0:T(8,128)S(1)} %get-tuple-element.18), channel_id=1, source_target_pairs={{0,4},{1,17},{2,6},{3,19},{4,0},{5,21},{6,2},{7,23},{8,12},{9,25},... | collective-permute-start | bytes 344072 | tf_op jit(solution)/shard_map/ppermute | solution.py:480
  35.0 4.8 %collective-permute-start.7 = (f32[8,3584]{1,0:T(8,128)S(1)}, f32[8,3584]{1,0:T(8,128)S(1)}, u32[]{:S(2)}, u32[]{:S(2)}) collective-permute-start(f32[8,3584]{1,0:T(8,128)S(1)} %get-tuple-element.19), channel_id=1, source_target_pairs={{0,2},{1,9},{2,0},{3,11},{4,6},{5,13},{6,4},{7,15},{8,10},{9,1},{1... | collective-permute-start | bytes 344072 | tf_op jit(solution)/shard_map/ppermute | solution.py:480
  37.8 4.9 %collective-permute-start.12 = (f32[8,3584]{1,0:T(8,128)S(1)}, f32[8,3584]{1,0:T(8,128)S(1)}, u32[]{:S(2)}, u32[]{:S(2)}) collective-permute-start(f32[8,3584]{1,0:T(8,128)S(1)} %add.60), channel_id=1, source_target_pairs={{0,8},{1,3},{2,10},{3,1},{4,12},{5,7},{6,14},{7,5},{8,0},{9,11},{1... | collective-permute-start | bytes 344072 | tf_op jit(solution)/shard_map/ppermute | solution.py:480
  39.8 5.9 %collective-permute-start.8 = (f32[8,3584]{1,0:T(8,128)S(1)}, f32[8,3584]{1,0:T(8,128)S(1)}, u32[]{:S(2)}, u32[]{:S(2)}) collective-permute-start(f32[8,3584]{1,0:T(8,128)S(1)} %add.55), channel_id=1, source_target_pairs={{0,4},{1,17},{2,6},{3,19},{4,0},{5,21},{6,2},{7,23},{8,12},{9,25},... | collective-permute-start | bytes 344072 | tf_op jit(solution)/shard_map/ppermute | solution.py:480
  42.6 7.2 %collective-permute-start.13 = (f32[8,3584]{1,0:T(8,128)S(1)}, f32[8,3584]{1,0:T(8,128)S(1)}, u32[]{:S(2)}, u32[]{:S(2)}) collective-permute-start(f32[8,3584]{1,0:T(8,128)S(1)} %add.61), channel_id=1, source_target_pairs={{0,16},{1,5},{2,18},{3,7},{4,20},{5,1},{6,22},{7,3},{8,24},{9,13},... | collective-permute-start | bytes 344072 | tf_op jit(solution)/shard_map/ppermute | solution.py:480
  45.7 6.0 %collective-permute-start.9 = (f32[8,3584]{1,0:T(8,128)S(1)}, f32[8,3584]{1,0:T(8,128)S(1)}, u32[]{:S(2)}, u32[]{:S(2)}) collective-permute-start(f32[8,3584]{1,0:T(8,128)S(1)} %add.56), channel_id=1, source_target_pairs={{0,8},{1,3},{2,10},{3,1},{4,12},{5,7},{6,14},{7,5},{8,0},{9,11},{1... | collective-permute-start | bytes 344072 | tf_op jit(solution)/shard_map/ppermute | solution.py:480
  49.8 4.9 %collective-permute-start.14 = (f32[8,3584]{1,0:T(8,128)S(1)}, f32[8,3584]{1,0:T(8,128)S(1)}, u32[]{:S(2)}, u32[]{:S(2)}) collective-permute-start(f32[8,3584]{1,0:T(8,128)S(1)} %add.62), channel_id=1, source_target_pairs={{0,2},{1,9},{2,0},{3,11},{4,6},{5,13},{6,4},{7,15},{8,10},{9,1},{1... | collective-permute-start | bytes 344072 | tf_op jit(solution)/shard_map/ppermute | solution.py:480
  51.8 7.0 %collective-permute-start.10 = (f32[8,3584]{1,0:T(8,128)S(1)}, f32[8,3584]{1,0:T(8,128)S(1)}, u32[]{:S(2)}, u32[]{:S(2)}) collective-permute-start(f32[8,3584]{1,0:T(8,128)S(1)} %add.57), channel_id=1, source_target_pairs={{0,16},{1,5},{2,18},{3,7},{4,20},{5,1},{6,22},{7,3},{8,24},{9,13},... | collective-permute-start | bytes 344072 | tf_op jit(solution)/shard_map/ppermute | solution.py:480
  54.7 4.2 %collective-permute-start.16 = (f32[8,3584]{1,0:T(8,128)S(1)}, f32[8,3584]{1,0:T(8,128)S(1)}, u32[]{:S(2)}, u32[]{:S(2)}) collective-permute-start(f32[8,3584]{1,0:T(8,128)S(1)} %add.63.mine1_ref), channel_id=1, source_target_pairs={{0,1},{1,0},{2,3},{3,2},{4,5},{5,4},{6,7},{7,6},{8,9},{9,8},{10,11... | collective-permute-start | bytes 344072 | tf_op jit(solution)/shard_map/ppermute | solution.py:480
  58.8 1.4 %collective-permute-start.15 = (f32[8,3584]{1,0:T(8,128)S(1)}, f32[8,3584]{1,0:T(8,128)S(1)}, u32[]{:S(2)}, u32[]{:S(2)}) collective-permute-start(f32[8,3584]{1,0:T(8,128)S(1)} %add.58.mine0_ref), channel_id=1, source_target_pairs={{0,1},{1,0},{2,3},{3,2},{4,5},{5,4},{6,7},{7,6},{8,9},{9,8},{10,11... | collective-permute-start | bytes 344072 | tf_op jit(solution)/shard_map/ppermute | solution.py:480

commit v2 on v1

--- a/solution.py
+++ b/solution.py
@@ -27,8 +27,7 @@
 COL_C = DI + DS
 COL_DT = DI + 2 * DS
 COLS = DI + 3 * DS
-GRAM = COLS
-WIDE = COLS + LANES
+WITH_GRAM = COLS + 4 * LANES
 CHUNKS = DI // LANES
 
 MERGE = 256
@@ -139,40 +138,18 @@
                 for j, (src, dst) in enumerate(((g_hbm, g_ref), (e_hbm, e_ref)))
             ]
         )
+    small[0].start()
     for i, pair in enumerate(big):
         for copy in pair:
             copy.start()
         if i == 0:
-            for copy in small:
+            for copy in small[1:]:
                 copy.start()
+    small[0].wait()
+    row, lane = starts_of(order_ref, plan.sizes)
 
     def merged(at, width):
         return g_ref[0:1, pl.ds(at, width)].astype(f32) + e_ref[0:1, pl.ds(at, width)].astype(f32)
-
-    for (begin, end), pair in zip(plan.pieces, big):
-        for copy in pair:
-            copy.wait()
-        whole = min(end, total // LANES)
-
-        def merge(i, _):
-            r = pl.multiple_of(begin + i * MERGE, 8)
-            m_ref[pl.ds(r, MERGE), :] = merged(pl.multiple_of(r * LANES, 1024), MERGE * LANES).reshape(MERGE, LANES)
-            return 0
-
-        count = (whole - begin) // MERGE
-        lax.fori_loop(0, count, merge, 0)
-        r = begin + count * MERGE
-        n = (whole - r) // 8 * 8
-        if n:
-            m_ref[r : r + n, :] = merged(r * LANES, n * LANES).reshape(n, LANES)
-        for r in range(r + n, whole):
-            m_ref[r : r + 1, :] = merged(LANES * r, LANES)
-        if end > whole:
-            m_ref[whole : whole + 1, 0 : total % LANES] = merged(LANES * whole, total % LANES)
-
-    for copy in small:
-        copy.wait()
-    row, lane = starts_of(order_ref, plan.sizes)
 
     def fetch(base, count, stride, moved):
         step = {} if stride == 1 else {"stride": stride}
@@ -196,7 +173,7 @@
 
     high = 32
 
-    def read_x(moved):
+    def read_x(first, last, moved):
         keep = lane_of((high, LANES)) < LANES - shift
 
         def block(i, _):
@@ -212,9 +189,37 @@
                 put(at, high, c * LANES, tile)
             return 0
 
-        lax.fori_loop(0, rows // high, block, 0)
-
-    either(0, read_x)
+        lax.fori_loop(first, last, block, 0)
+
+    done = 0
+    for (begin, end), pair in zip(plan.pieces, big):
+        for copy in pair:
+            copy.wait()
+        whole = min(end, total // LANES)
+
+        def merge(i, _):
+            r = pl.multiple_of(begin + i * MERGE, 8)
+            m_ref[pl.ds(r, MERGE), :] = merged(pl.multiple_of(r * LANES, 1024), MERGE * LANES).reshape(MERGE, LANES)
+            return 0
+
+        count = (whole - begin) // MERGE
+        lax.fori_loop(0, count, merge, 0)
+        r = begin + count * MERGE
+        n = (whole - r) // 8 * 8
+        if n:
+            m_ref[r : r + n, :] = merged(r * LANES, n * LANES).reshape(n, LANES)
+        for r in range(r + n, whole):
+            m_ref[r : r + 1, :] = merged(LANES * r, LANES)
+        if end > whole:
+            m_ref[whole : whole + 1, 0 : total % LANES] = merged(LANES * whole, total % LANES)
+
+        ready = rows // high
+        if end < plan.flat_rows:
+            ready = jnp.minimum(lax.div(jnp.maximum(end - 1 - row[0], 0), jnp.int32(high * CHUNKS)), rows // high)
+        either(0, functools.partial(read_x, done, ready))
+        done = ready
+    for copy in small[1:]:
+        copy.wait()
     for k, column in ((1, COL_B), (2, COL_C)):
         either(k, lambda moved, k=k, column=column: put(0, rows, column, joined(row[k], rows, 1, moved)))
 
@@ -265,7 +270,7 @@
     low_ref[0:low, :] = panel[plan.half :]
 
 
-def factor_kernel(plan, replicas, top_ref, low_ref, mh_ref, ml_ref, mine0_ref, mine1_ref, other_ref, z_ref):
+def factor_kernel(plan, top_ref, low_ref, mh_ref, ml_ref, mine0_ref, mine1_ref, other_ref, z_ref):
     rows = plan.rows
     panel = jnp.concatenate([top_ref[...], low_ref[0 : rows - plan.half, :]], 0)
     group = lane_of((rows, LANES)) // RANK
@@ -283,19 +288,67 @@
     out = gram[0:RANK]
     for k in range(1, 4):
         out = jnp.where(group == k, gram[RANK * k : RANK * (k + 1)], out)
-    z_ref[:, GRAM : GRAM + LANES] = out * (1.0 / replicas)
     half = RANK // 2
     core = jnp.bitwise_and(lax.axis_index("mp"), 1)
     for mine in (0, 1):
 
         @pl.when(core == mine)
         def _():
-            mine0_ref[...] = z_ref[half * mine : half * mine + half // 2, :]
+            mine0_ref[:, 0:COLS] = z_ref[half * mine : half * mine + half // 2, :]
             mine1_ref[...] = z_ref[half * mine + half // 2 : half * (mine + 1), :]
-            other_ref[...] = z_ref[half * (1 - mine) : half * (2 - mine), :]
-
-
-def output_kernel(plan, replicas, order_ref, mine0_ref, mine1_ref, other0_ref, other1_ref, top_ref, low_ref, m_ref, mom_ref, err_hbm, next_hbm, z_ref, a_ref, x_ref, s_ref, err_ref, next_ref, sems):
+            other_ref[:, 0:COLS] = z_ref[half * (1 - mine) : half * (2 - mine), :]
+
+    other_ref[:, COLS:] = jnp.zeros((half, 4 * LANES), f32)
+    for b in range(4):
+        lanes = slice(COLS + b * LANES, COLS + (b + 1) * LANES)
+        mine0_ref[:, lanes] = out[8 * b : 8 * (b + 1)]
+        other_ref[0:8, lanes] = out[8 * b : 8 * (b + 1)]
+
+
+def block_masks():
+    square = (LANES, LANES)
+    down = lax.broadcasted_iota(jnp.int32, square, 0)
+    along = lane_of(square)
+    return jnp.where(down == along, 1.0, 0.0), jnp.where(down // RANK == along // RANK, 1.0, 0.0)
+
+
+def newton_schulz(eye, gram, turned, steps, last):
+    for step in range(steps):
+        mixing = ns_first * eye + ns_second * gram + ns_third * dot_exact(gram, gram)
+        turned = mixing if turned is None else dot_exact(turned, mixing)
+        if not (last and step + 1 == steps):
+            gram = dot_exact(mixing, dot_exact(gram, mixing))
+    return gram, turned
+
+
+def begin_kernel(sum_ref, gram_out, turned_out, scale_out):
+    eye, ones = block_masks()
+    gram = [sum_ref[:, b * LANES : (b + 1) * LANES] for b in range(4)]
+    gram = jnp.concatenate(gram * 4, 0) * ones
+    trace = jnp.sum(gram * eye, axis=0, keepdims=True)
+    trace = dot_exact(jnp.broadcast_to(trace, (8, LANES)), ones)
+    scale = 1.0 / (jnp.sqrt(trace) + 1e-06)
+    scale = scale * scale
+    scale_out[...] = scale
+    gram_out[...], turned_out[...] = newton_schulz(eye, gram * scale[0:1], None, NS_STEPS // 2, False)
+
+
+def frame_kernel(plan, replicas, gram_ref, turned_ref, scale_ref, top_ref, low_ref, lhs_ref):
+    rows = plan.rows
+    eye, _ = block_masks()
+    _, turned = newton_schulz(eye, gram_ref[...], turned_ref[...], NS_STEPS - NS_STEPS // 2, True)
+    both = lax.dot_general(
+        turned, turned, (((1,), (1,)), ((), ())), preferred_element_type=f32, precision=lax.Precision.HIGHEST
+    )
+    panel = jnp.concatenate([top_ref[...], low_ref[0 : rows - plan.half, :]], 0)
+    left = dot_exact(panel, both * (scale_ref[0:1] * (1.0 / replicas)))
+    group = lane_of((rows, LANES)) // RANK
+    for k in range(4):
+        hi, mid = (piece.astype(f32) for piece in split2(spread(left, k)))
+        lhs_ref[k * rows : (k + 1) * rows, :] = jnp.where(group % 2 == 0, hi, mid).astype(bf16)
+
+
+def output_kernel(plan, replicas, order_ref, mine0_ref, mine1_ref, other0_ref, other1_ref, lhs_ref, low_ref, m_ref, mom_ref, err_hbm, next_hbm, z_ref, a_ref, x_ref, s_ref, err_ref, next_ref, sems):
     rows = plan.rows
     shift = plan.shift
     row, lane = starts_of(order_ref, plan.sizes)
@@ -310,34 +363,8 @@
                 at = (2 * mine + i) % 4 * quarter
                 z_ref[at : at + quarter, :] = ref[...]
 
-    square = (LANES, LANES)
-    down = lax.broadcasted_iota(jnp.int32, square, 0)
-    along = lane_of(square)
-    same = down // RANK == along // RANK
-    eye = jnp.where(down == along, 1.0, 0.0)
-    ones = jnp.where(same, 1.0, 0.0)
-    gram = z_ref[:, GRAM : GRAM + LANES]
-    gram = jnp.where(same, jnp.concatenate([gram] * 4, 0), 0.0)
-    trace = dot_exact(dot_exact(ones, gram * eye), ones)
-    scale = 1.0 / (jnp.sqrt(trace) + 1e-06)
-    scale = jnp.where(same, scale * scale, 0.0)
-    gram = gram * scale
-    turned = eye
-    for step in range(NS_STEPS):
-        mixing = ns_first * eye + ns_second * gram + ns_third * dot_exact(gram, gram)
-        turned = dot_exact(turned, mixing)
-        if step + 1 < NS_STEPS:
-            gram = dot_exact(mixing, dot_exact(gram, mixing))
-    both = lax.dot_general(
-        turned, turned, (((1,), (1,)), ((), ())), preferred_element_type=f32, precision=lax.Precision.HIGHEST
-    )
-    panel = jnp.concatenate([top_ref[...], low_ref[0 : rows - plan.half, :]], 0)
-    left = dot_exact(panel, both * (scale * (1.0 / replicas)))
-
-    group = lane_of((rows, LANES)) // RANK
     for k, column, width in ((0, 0, DI), (1, COL_B, DS), (2, COL_C, DS), (3, COL_DT, DS)):
-        hi, mid = (piece.astype(f32) for piece in split2(spread(left, k)))
-        lhs = jnp.where(group % 2 == 0, hi, mid).astype(bf16)
+        lhs = lhs_ref[k * rows : (k + 1) * rows, :]
         hi, mid = split2(z_ref[:, column : column + width])
         rhs = jnp.concatenate([hi, hi, mid, mid], 0)
         x_ref[8 : 8 + rows, column : column + width] = lax.dot_general(
@@ -354,10 +381,8 @@
         for moved in (False, True):
             pl.when((lane[k] != 0) == moved)(functools.partial(work, moved))
 
-    def write_x(moved):
+    def write_x(first, last, moved):
         keep = lane_of((high, LANES)) >= shift
-        if moved:
-            s_ref[8 : 8 + rows, :] = right(x_ref[8 : 8 + rows, DI - LANES : DI])
 
         def block(i, _):
             at = pl.multiple_of(8 + i * high, 8)
@@ -372,13 +397,8 @@
                 a_ref[pl.ds(base + c, high, stride=CHUNKS), :] = now
             return 0
 
-        lax.fori_loop(0, rows // high, block, 0)
-        if moved:
-            final = row[0] + rows * CHUNKS
-            end = s_ref[rows + 7 : rows + 8, :]
-            a_ref[pl.ds(final, 1), :] = jnp.where(lanes1 < shift, end, a_ref[pl.ds(final, 1), :])
-
-    either(0, write_x)
+        lax.fori_loop(first, last, block, 0)
+
 
     def place(k, ref, column, count):
         columns = slice(column, column + LANES)
@@ -425,6 +445,14 @@
     valid = plan.sizes[5] - last * LANES
     a_ref[pl.ds(final, 1), :] = jnp.where(lanes1 < valid, vec[last : last + 1], a_ref[pl.ds(final, 1), :])
 
+    @pl.when(lane[0] != 0)
+    def _():
+        s_ref[8 : 8 + rows, :] = right(x_ref[8 : 8 + rows, DI - LANES : DI])
+        s_ref[7:8, :] = a_ref[pl.ds(row[0], 1), :]
+        final = row[0] + rows * CHUNKS
+        end = s_ref[rows + 7 : rows + 8, :]
+        a_ref[pl.ds(final, 1), :] = jnp.where(lanes1 < shift, end, a_ref[pl.ds(final, 1), :])
+
     total = plan.total
     spans = [(row[k] * LANES + lane[k], row[k] * LANES + lane[k] + plan.sizes[k]) for k in (4, 5)]
 
@@ -450,7 +478,14 @@
             err_ref[0:1, pl.ds(at, n)] = err.astype(bf16).reshape(1, n)
 
     copies = []
+    done = 0
     for i, (begin, end) in enumerate(plan.pieces):
+        step = high * CHUNKS
+        ready = rows // high
+        if end < plan.flat_rows:
+            ready = jnp.minimum(lax.div(jnp.maximum(end - row[0], 0) + (step - 1), jnp.int32(step)), rows // high)
+        either(0, functools.partial(write_x, done, ready))
+        done = ready
         whole = min(end, total // LANES)
         count = (whole - begin) // FINISH
         lax.fori_loop(0, count, lambda j, _: (finish(pl.multiple_of(begin + j * FINISH, 8), FINISH), 0)[1], 0)
@@ -480,11 +515,13 @@
     return lax.ppermute(x, ("dp", "mp"), [(i, i ^ (second if i % 2 else first)) for i in range(n)])
 
 
-def butterfly(halves, steps, turns):
-    n = len(steps)
-    order = [[steps[(i + t) % n] for i in range(n)] for t in turns]
-    for i in range(n):
-        got = [pairwise(halves[h], order[2 * h][i], order[2 * h + 1][i]) for h in (0, 1)]
+def turned(steps, by):
+    return steps[by:] + steps[:by]
+
+
+def butterfly(halves, orders, first, last):
+    for i in range(first, last):
+        got = [pairwise(halves[h], orders[2 * h][i], orders[2 * h + 1][i]) for h in (0, 1)]
         halves = [mine + other for mine, other in zip(halves, got)]
     return halves
 
@@ -527,24 +564,61 @@
 
     inner = [1 << b for b in range(1, (blocks - 1).bit_length())]
     outer = [blocks << b for b in range((replicas - 1).bit_length())]
-    n = len(outer)
-    top, low = butterfly([top, low], outer, (0, n - 1, 1, 0))
-
+    orders = [outer, turned(outer, len(outer) - 1), turned(outer, 1), outer]
+    top, low = butterfly([top, low], orders, 0, len(outer))
+    outer = outer[1:2] + outer[:1] + outer[2:]
+
+    quarter, half = RANK // 4, RANK // 2
     mine0, mine1, other = pl.pallas_call(
-        functools.partial(factor_kernel, plan, replicas),
-        out_shape=(shape((RANK // 4, WIDE), f32), shape((RANK // 4, WIDE), f32), shape((RANK // 2, WIDE), f32)),
+        functools.partial(factor_kernel, plan),
+        out_shape=(shape((quarter, WITH_GRAM), f32), shape((quarter, COLS), f32), shape((half, WITH_GRAM), f32)),
         in_specs=specs(*[VMEM] * 4),
         out_specs=tuple(specs(*[VMEM] * 3)),
-        scratch_shapes=[pltpu.VMEM((RANK, WIDE), f32)],
+        scratch_shapes=[pltpu.VMEM((RANK, COLS), f32)],
         compiler_params=pltpu.CompilerParams(vmem_limit_bytes=24 << 20),
         cost_estimate=pl.CostEstimate(flops=4 * rows * COLS * LANES, bytes_accessed=4 * total, transcendentals=0),
     )(top, low, mh, ml)
     got = pairwise(other, 1, 1)
-    steps = inner + outer
-    n = len(steps)
-    halves = butterfly(
-        [mine0 + got[: RANK // 4], mine1 + got[RANK // 4 :]], steps, (0, n // 2, 1, 1 + n // 2)
-    )
+    halves = [mine0 + got[:quarter], mine1 + got[quarter:, :COLS]]
+    square = shape((LANES, LANES), f32)
+
+    def begin(gram):
+        return pl.pallas_call(
+            begin_kernel,
+            out_shape=(square, square, shape((8, LANES), f32)),
+            in_specs=specs(VMEM),
+            out_specs=tuple(specs(*[VMEM] * 3)),
+            compiler_params=pltpu.CompilerParams(vmem_limit_bytes=4 << 20),
+            cost_estimate=pl.CostEstimate(flops=1500000000, bytes_accessed=200000, transcendentals=0),
+        )(gram)
+
+    def frame(made):
+        return pl.pallas_call(
+            functools.partial(frame_kernel, plan, replicas),
+            out_shape=shape((4 * rows, LANES), bf16),
+            in_specs=specs(*[VMEM] * 5),
+            out_specs=specs(VMEM)[0],
+            compiler_params=pltpu.CompilerParams(vmem_limit_bytes=8 << 20),
+            cost_estimate=pl.CostEstimate(flops=1500000000, bytes_accessed=600000, transcendentals=0),
+        )(*made, top, low)
+
+    gram, halves[0] = halves[0][:, COLS:], halves[0][:, :COLS]
+    for bit in inner:
+        gram = gram + pairwise(gram, bit, bit)
+    ring = inner + outer
+    n = len(ring)
+    orders = [turned(ring, by) for by in (0, n // 2, 1, 1 + n // 2)]
+    halves = butterfly(halves, orders, 0, 1)
+    halves[0], gram = lax.optimization_barrier((halves[0], gram))
+    halves = butterfly(halves, orders, 1, 2)
+    halves[1], gram = lax.optimization_barrier((halves[1], gram))
+    halves = butterfly(halves, orders, 2, 3)
+    made = begin(gram)
+    halves[0], made = lax.optimization_barrier((halves[0], made))
+    lhs = frame(made)
+    halves = butterfly(halves, orders, 3, n)
+    halves[0], lhs = lax.optimization_barrier((halves[0], lhs))
+    halves[1], lhs = lax.optimization_barrier((halves[1], lhs))
     others = [pairwise(half, 1, 1) for half in halves]
 
     return pl.pallas_call(
@@ -553,7 +627,7 @@
         in_specs=specs(pltpu.SMEM, *[VMEM] * 8),
         out_specs=tuple(specs(HBM, HBM)),
         scratch_shapes=[
-            pltpu.VMEM((RANK, WIDE), f32),
+            pltpu.VMEM((RANK, COLS), f32),
             pltpu.VMEM((plan.buf_rows, LANES), f32),
             pltpu.VMEM((rows + 8, COLS), f32),
             pltpu.VMEM((rows + 24, LANES), f32),
@@ -563,7 +637,7 @@
         ],
         compiler_params=pltpu.CompilerParams(vmem_limit_bytes=36 << 20),
         cost_estimate=pl.CostEstimate(flops=2 * rows * COLS * LANES, bytes_accessed=16 * total, transcendentals=0),
-    )(part_order, *halves, *others, top, low, m, momentum_flat)
+    )(part_order, *halves, *others, lhs, low, m, momentum_flat)
 
 
 def solution(mesh):

time: 72.3 us -> 65.6 us (0.907)
  waiting for transfers between devices: 18.3 us -> 14.8 us
  starting transfers between devices: 30.3 us -> 28.6 us
  Pallas kernels: 23.6 us -> 22.2 us
    pallas_call x1, Pallas kernels: 13 us -> 8.04 us  [body(): pl.pallas_call(functools.partial(output_kernel, plan, replicas), out_shap...]
    pallas_call x1 -> x3, Pallas kernels: 1.64 us -> 6.18 us  [the longest x1 2.94 us: frame(): pl.pallas_call(functools.partial(frame_kernel, plan, replicas), out_shape...]
    ppermute x17 -> x18, waiting for transfers between devices: 18.3 us -> 14.8 us  [pairwise(): lax.ppermute(x, ('dp', 'mp'), [(i, i ^ (second if i % 2 else first)) for...]
    ppermute x17 -> x18, starting transfers between devices: 30.3 us -> 28.6 us  [pairwise(): lax.ppermute(x, ('dp', 'mp'), [(i, i ^ (second if i % 2 else first)) for...]
    pallas_call x1, Pallas kernels: 8.92 us -> 7.97 us  [body(): pl.pallas_call(functools.partial(panel_kernel, plan), out_shape=(shape((p...]
  transfers between devices with their start and end apart: 17 -> 18, of which waited for: 13 -> 12; matrix products, arithmetic and copies ran while one was open for 0% -> 0% of each run, Pallas kernels for 0% -> 7%
where the time goes in v2:
time: 65.6 us; the launch traced here: 66.6 us
  starting transfers between devices  28.6 us (44%)
  Pallas kernels  22.2 us (34%)
  waiting for transfers between devices  14.8 us (23%)
  between operations  0.8 us (1%)
    ppermute x18, starting transfers between devices, pairwise(): lax.ppermute(x, ('dp', 'mp'), [(i, i ^ (second if i % 2 else first)) for...  28.6 us
    ppermute x18, waiting for transfers between devices, pairwise(): lax.ppermute(x, ('dp', 'mp'), [(i, i ^ (second if i % 2 else first)) for...  14.8 us
    pallas_call x1, Pallas kernels, body(): pl.pallas_call(functools.partial(output_kernel, plan, replicas), out_shap...  8.04 us
    pallas_call x1, Pallas kernels, body(): pl.pallas_call(functools.partial(panel_kernel, plan), out_shape=(shape((p...  7.97 us
    pallas_call x1, Pallas kernels, frame(): pl.pallas_call(functools.partial(frame_kernel, plan, replicas), out_shape...  2.94 us
    pallas_call x1, Pallas kernels, body(): pl.pallas_call(functools.partial(factor_kernel, plan), out_shape=(shape((...  1.64 us
    pallas_call x1, Pallas kernels, begin(): pl.pallas_call(begin_kernel, out_shape=(square, square, shape((8, LANES),...  1.6 us
  transfers between devices with their start and end apart: 18, of which 12 were waited for; matrix products, arithmetic and copies ran while one was open for 0% of the time, Pallas kernels for 7%

profile of v2, /device:TPU:0, one launch (start us, length us, event | category | flops | bytes accessed | tf_op | source)
XLA Modules:
  0.0 66.6 jit_solution(147406519968282033)
XLA Ops:
  0.6 8.0 %shard_map.95 = (f32[216,128]{1,0:T(8,128)S(1)}, f32[208,128]{1,0:T(8,128)S(1)}, bf16[384,3456]{1,0:T(8,128)(2,1)S(1)}, bf16[384,3456]{1,0:T(8,128)(2,1)S(1)}, f32[10192,128]{1,0:T(8,128)S(1)}) custom-call(s32[6]{0:T(128)} %order_ref.1, bf16[1,1300580]{1,0:T(2,128)(2,1)} %g_hbm.1, bf16[1,1300580]{1,0:T(2,128)(2,1)} %e_hbm.1, f32[32,3072]{1,0:T(8,128)} %bitcast.6, ...), custom_call_target="tpu_custom_call" | custom-call | flops 679477248 | bytes 10404640 | tf_op jit(solution)/shard_map/pallas_call | solution.py:538
  8.6 3.0 %collective-permute-start = (f32[216,128]{1,0:T(8,128)S(1)}, f32[216,128]{1,0:T(8,128)S(1)}, u32[]{:S(2)}, u32[]{:S(2)}) collective-permute-start(f32[216,128]{1,0:T(8,128)S(1)} %get-tuple-element.25), channel_id=1, source_target_pairs={{0,4},{1,17},{2,6},{3,19},{4,0},{5,21},{6,2},{7,23},{8,12},{9,25},... | collective-permute-start | bytes 331784 | tf_op jit(solution)/shard_map/ppermute | solution.py:515
  11.6 1.6 %collective-permute-start.3 = (f32[208,128]{1,0:T(8,128)S(1)}, f32[208,128]{1,0:T(8,128)S(1)}, u32[]{:S(2)}, u32[]{:S(2)}) collective-permute-start(f32[208,128]{1,0:T(8,128)S(1)} %get-tuple-element.26), channel_id=1, source_target_pairs={{0,8},{1,5},{2,10},{3,7},{4,12},{5,1},{6,14},{7,3},{8,0},{9,13},{1... | collective-permute-start | bytes 319496 | tf_op jit(solution)/shard_map/ppermute | solution.py:515
  13.2 1.2 %collective-permute-done = f32[216,128]{1,0:T(8,128)S(1)} collective-permute-done((f32[216,128]{1,0:T(8,128)S(1)}, f32[216,128]{1,0:T(8,128)S(1)}, u32[]{:S(2)}, u32[]{:S(2)}) %collective-permute-start) | collective-permute-done | bytes 110624 | tf_op jit(solution)/shard_map/ppermute | solution.py:515
  14.4 2.1 %collective-permute-start.1 = (f32[216,128]{1,0:T(8,128)S(1)}, f32[216,128]{1,0:T(8,128)S(1)}, u32[]{:S(2)}, u32[]{:S(2)}) collective-permute-start(f32[216,128]{1,0:T(8,128)S(1)} %add.51), channel_id=1, source_target_pairs={{0,8},{1,5},{2,10},{3,7},{4,12},{5,1},{6,14},{7,3},{8,0},{9,13},{1... | collective-permute-start | bytes 331784 | tf_op jit(solution)/shard_map/ppermute | solution.py:515
  16.5 0.0 collective-permute-done.3
  16.5 2.7 %collective-permute-start.4 = (f32[208,128]{1,0:T(8,128)S(1)}, f32[208,128]{1,0:T(8,128)S(1)}, u32[]{:S(2)}, u32[]{:S(2)}) collective-permute-start(f32[208,128]{1,0:T(8,128)S(1)} %add.54), channel_id=1, source_target_pairs={{0,16},{1,9},{2,18},{3,11},{4,20},{5,13},{6,22},{7,15},{8,24},{9,1... | collective-permute-start | bytes 319496 | tf_op jit(solution)/shard_map/ppermute | solution.py:515
  19.3 0.2 collective-permute-done.1
  19.5 3.2 %collective-permute-start.2 = (f32[216,128]{1,0:T(8,128)S(1)}, f32[216,128]{1,0:T(8,128)S(1)}, u32[]{:S(2)}, u32[]{:S(2)}) collective-permute-start(f32[216,128]{1,0:T(8,128)S(1)} %add.52), channel_id=1, source_target_pairs={{0,16},{1,9},{2,18},{3,11},{4,20},{5,13},{6,22},{7,15},{8,24},{9,1... | collective-permute-start | bytes 331784 | tf_op jit(solution)/shard_map/ppermute | solution.py:515
  22.8 0.0 collective-permute-done.4
  22.8 2.2 %collective-permute-start.5 = (f32[208,128]{1,0:T(8,128)S(1)}, f32[208,128]{1,0:T(8,128)S(1)}, u32[]{:S(2)}, u32[]{:S(2)}) collective-permute-start(f32[208,128]{1,0:T(8,128)S(1)} %add.55), channel_id=1, source_target_pairs={{0,4},{1,17},{2,6},{3,19},{4,0},{5,21},{6,2},{7,23},{8,12},{9,25},... | collective-permute-start | bytes 319496 | tf_op jit(solution)/shard_map/ppermute | solution.py:515
  25.0 2.7 %collective-permute-done.5 = f32[208,128]{1,0:T(8,128)S(1)} collective-permute-done((f32[208,128]{1,0:T(8,128)S(1)}, f32[208,128]{1,0:T(8,128)S(1)}, u32[]{:S(2)}, u32[]{:S(2)}) %collective-permute-start.5) | collective-permute-done | bytes 106528 | tf_op jit(solution)/shard_map/ppermute | solution.py:515
  27.7 0.3 collective-permute-done.2
  28.0 1.6 %shard_map.96 = (f32[8,3968]{1,0:T(8,128)S(1)}, f32[8,3456]{1,0:T(8,128)S(1)}, f32[16,3968]{1,0:T(8,128)S(1)}) custom-call(f32[216,128]{1,0:T(8,128)S(1)} %add.53.top_ref, f32[208,128]{1,0:T(8,128)S(1)} %add.56.low_ref, bf16[384,3456]{1,0:T(8,128)(2,1)S(1)} %get-tuple-element.27.mh_ref, bf16[384,3456]{1,0:T(8,128)(2,1)S(1)} %get-tuple-element.28.ml_ref), custom_call_target="tpu_custom_call" | custom-call | flops 679477248 | bytes 5202320 | tf_op jit(solution)/shard_map/pallas_call | solution.py:572
  29.7 0.9 %collective-permute-start.6 = (f32[16,3968]{1,0:T(8,128)S(1)}, f32[16,3968]{1,0:T(8,128)S(1)}, u32[]{:S(2)}, u32[]{:S(2)}) collective-permute-start(f32[16,3968]{1,0:T(8,128)S(1)} %get-tuple-element.30), channel_id=1, source_target_pairs={{0,1},{1,0},{2,3},{3,2},{4,5},{5,4},{6,7},{7,6},{8,9},{9,8},{10,11... | collective-permute-start | bytes 761864 | tf_op jit(solution)/shard_map/ppermute | solution.py:515
  30.6 1.2 %collective-permute-done.6 = f32[16,3968]{1,0:T(8,128)S(1)} collective-permute-done((f32[16,3968]{1,0:T(8,128)S(1)}, f32[16,3968]{1,0:T(8,128)S(1)}, u32[]{:S(2)}, u32[]{:S(2)}) %collective-permute-start.6) | collective-permute-done | bytes 253984 | tf_op jit(solution)/shard_map/ppermute | solution.py:515
  31.8 1.6 %collective-permute-start.8 = (f32[8,512]{1,0:T(8,128)S(1)}, f32[8,512]{1,0:T(8,128)S(1)}, u32[]{:S(2)}, u32[]{:S(2)}) collective-permute-start(f32[8,512]{1,0:T(8,128)S(1)} %slice.18), channel_id=1, source_target_pairs={{0,2},{1,3},{2,0},{3,1},{4,6},{5,7},{6,4},{7,5},{8,10},{9,11},{10,... | collective-permute-start | bytes 49160 | tf_op jit(solution)/shard_map/ppermute | solution.py:515
  33.4 0.5 collective-permute-start.7
  33.9 0.0 slice-start
  33.9 1.3 %collective-permute-start.11 = (f32[8,3456]{1,0:T(8,128)S(1)}, f32[8,3456]{1,0:T(8,128)S(1)}, u32[]{:S(2)}, u32[]{:S(2)}) collective-permute-start(f32[8,3456]{1,0:T(8,128)S(1)} %slice_add_fusion.1), channel_id=1, source_target_pairs={{0,8},{1,17},{2,10},{3,19},{4,12},{5,21},{6,14},{7,23},{8,0},{9,25... | collective-permute-start | bytes 331784 | tf_op jit(solution)/shard_map/ppermute | solution.py:515
  35.2 0.4 collective-permute-done.8
  35.6 2.5 %collective-permute-done.7 = f32[8,3456]{1,0:T(8,128)S(1)} collective-permute-done((f32[8,3456]{1,0:T(8,128)S(1)}, f32[8,3456]{1,0:T(8,128)S(1)}, u32[]{:S(2)}, u32[]{:S(2)}) %collective-permute-start.7) | collective-permute-done | bytes 110624 | tf_op jit(solution)/shard_map/ppermute | solution.py:515
  38.1 1.3 %collective-permute-start.9 = (f32[8,3456]{1,0:T(8,128)S(1)}, f32[8,3456]{1,0:T(8,128)S(1)}, u32[]{:S(2)}, u32[]{:S(2)}) collective-permute-start(f32[8,3456]{1,0:T(8,128)S(1)} %slice_add_fusion.3), channel_id=1, source_target_pairs={{0,8},{1,17},{2,10},{3,19},{4,12},{5,21},{6,14},{7,23},{8,0},{9,25... | collective-permute-start | bytes 331784 | tf_op jit(solution)/shard_map/ppermute | solution.py:515
  39.4 0.0 collective-permute-done.11
  39.5 1.9 %collective-permute-start.12 = (f32[8,3456]{1,0:T(8,128)S(1)}, f32[8,3456]{1,0:T(8,128)S(1)}, u32[]{:S(2)}, u32[]{:S(2)}) collective-permute-start(f32[8,3456]{1,0:T(8,128)S(1)} %add.63), channel_id=1, source_target_pairs={{0,4},{1,3},{2,6},{3,1},{4,0},{5,7},{6,2},{7,5},{8,12},{9,11},{10,... | collective-permute-start | bytes 331784 | tf_op jit(solution)/shard_map/ppermute | solution.py:515
  41.3 1.9 %collective-permute-done.9 = f32[8,3456]{1,0:T(8,128)S(1)} collective-permute-done((f32[8,3456]{1,0:T(8,128)S(1)}, f32[8,3456]{1,0:T(8,128)S(1)}, u32[]{:S(2)}, u32[]{:S(2)}) %collective-permute-start.9) | collective-permute-done | bytes 110624 | tf_op jit(solution)/shard_map/ppermute | solution.py:515
  43.3 1.9 %collective-permute-start.10 = (f32[8,3456]{1,0:T(8,128)S(1)}, f32[8,3456]{1,0:T(8,128)S(1)}, u32[]{:S(2)}, u32[]{:S(2)}) collective-permute-start(f32[8,3456]{1,0:T(8,128)S(1)} %add.60), channel_id=1, source_target_pairs={{0,4},{1,3},{2,6},{3,1},{4,0},{5,7},{6,2},{7,5},{8,12},{9,11},{10,... | collective-permute-start | bytes 331784 | tf_op jit(solution)/shard_map/ppermute | solution.py:515
  45.2 0.0 collective-permute-done.12
  45.2 0.0 slice-start.1
  45.3 0.0 copy-start
  45.3 2.5 %collective-permute-start.14 = (f32[8,3456]{1,0:T(8,128)S(1)}, f32[8,3456]{1,0:T(8,128)S(1)}, u32[]{:S(2)}, u32[]{:S(2)}) collective-permute-start(f32[8,3456]{1,0:T(8,128)S(1)} %add.64), channel_id=1, source_target_pairs={{0,16},{1,9},{2,18},{3,11},{4,20},{5,13},{6,22},{7,15},{8,24},{9,1... | collective-permute-start | bytes 331784 | tf_op jit(solution)/shard_map/ppermute | solution.py:515
  47.8 1.6 %shard_map.97 = (f32[128,128]{1,0:T(8,128)S(1)}, f32[128,128]{1,0:T(8,128)S(1)}, f32[8,128]{1,0:T(8,128)S(1)}) custom-call(f32[8,512]{1,0:T(8,128)S(1)} %slice_add_fusion.2.sum_ref), custom_call_target="tpu_custom_call" | custom-call | flops 1500000000 | bytes 200000 | tf_op jit(solution)/shard_map/pallas_call | solution.py:586
  49.4 0.0 collective-permute-done.10
  49.4 1.1 %collective-permute-start.13 = (f32[8,3456]{1,0:T(8,128)S(1)}, f32[8,3456]{1,0:T(8,128)S(1)}, u32[]{:S(2)}, u32[]{:S(2)}) collective-permute-start(f32[8,3456]{1,0:T(8,128)S(1)} %add.61), channel_id=1, source_target_pairs={{0,16},{1,9},{2,18},{3,11},{4,20},{5,13},{6,22},{7,15},{8,24},{9,1... | collective-permute-start | bytes 331784 | tf_op jit(solution)/shard_map/ppermute | solution.py:515
  50.5 1.7 %collective-permute-done.14 = f32[8,3456]{1,0:T(8,128)S(1)} collective-permute-done((f32[8,3456]{1,0:T(8,128)S(1)}, f32[8,3456]{1,0:T(8,128)S(1)}, u32[]{:S(2)}, u32[]{:S(2)}) %collective-permute-start.14) | collective-permute-done | bytes 110624 | tf_op jit(solution)/shard_map/ppermute | solution.py:515
  52.2 0.1 collective-permute-start.15
  52.3 2.9 %shard_map.98.lhs_ref = bf16[1536,128]{1,0:T(8,128)(2,1)S(1)} custom-call(f32[128,128]{1,0:T(8,128)S(1)} %get-tuple-element.39.gram_ref, f32[128,128]{1,0:T(8,128)S(1)} %get-tuple-element.40.turned_ref, f32[8,128]{1,0:T(8,128)S(1)} %get-tuple-element.41.scale_ref, f32[216,128]{1,0:T(8,128)S(1)} %add.53.top_ref, f32[208,128]{1,0:T(8,128)S(1)} %add.56.low_ref), custom_call_target="tpu_custom_call" | custom-call | flops 1500000000 | bytes 600000 | tf_op jit(solution)/shard_map/pallas_call | solution.py:596
  55.2 0.0 collective-permute-done.13
  55.2 1.8 %collective-permute-done.15 = f32[8,3456]{1,0:T(8,128)S(1)} collective-permute-done((f32[8,3456]{1,0:T(8,128)S(1)}, f32[8,3456]{1,0:T(8,128)S(1)}, u32[]{:S(2)}, u32[]{:S(2)}) %collective-permute-start.15) | collective-permute-done | bytes 110624 | tf_op jit(solution)/shard_map/ppermute | solution.py:515
  57.0 0.1 collective-permute-start.17
  57.1 0.5 collective-permute-start.16
  57.6 0.8 %collective-permute-done.17.other1_ref = f32[8,3456]{1,0:T(8,128)S(1)} collective-permute-done((f32[8,3456]{1,0:T(8,128)S(1)}, f32[8,3456]{1,0:T(8,128)S(1)}, u32[]{:S(2)}, u32[]{:S(2)}) %collective-permute-start.17) | collective-permute-done | bytes 110624 | tf_op jit(solution)/shard_map/ppermute | solution.py:515
  58.4 0.2 collective-permute-done.16.other0_ref
  58.6 0.0 slice-done
  58.6 0.0 slice-done.1
  58.6 0.0 copy-done
  58.6 8.0 %shard_map.99 = (bf16[1,1300580]{1,0:T(2,128)(2,1)}, f32[1300580]{0:T(1024)}) custom-call(s32[6]{0:T(128)S(1)} %copy-done, f32[8,3456]{1,0:T(8,128)S(1)} %add.65.mine0_ref, f32[8,3456]{1,0:T(8,128)S(1)} %add.67.mine1_ref, f32[8,3456]{1,0:T(8,128)S(1)} %collective-permute-done.16.other0_ref, f32[8,3456]{1,0:T(8,128)S(1)} %collective-permute-done.17.other1_ref, ...), custom_call_target="tpu_custom_call" | custom-call | flops 339738624 | bytes 20809280 | tf_op jit(solution)/shard_map/pallas_call | solution.py:624
  (20 shorter events, 0.3 us)
Async XLA Ops:
  8.6 5.8 %collective-permute-start = (f32[216,128]{1,0:T(8,128)S(1)}, f32[216,128]{1,0:T(8,128)S(1)}, u32[]{:S(2)}, u32[]{:S(2)}) collective-permute-start(f32[216,128]{1,0:T(8,128)S(1)} %get-tuple-element.25), channel_id=1, source_target_pairs={{0,4},{1,17},{2,6},{3,19},{4,0},{5,21},{6,2},{7,23},{8,12},{9,25},... | collective-permute-start | bytes 331784 | tf_op jit(solution)/shard_map/ppermute | solution.py:515
  11.6 4.9 %collective-permute-start.3 = (f32[208,128]{1,0:T(8,128)S(1)}, f32[208,128]{1,0:T(8,128)S(1)}, u32[]{:S(2)}, u32[]{:S(2)}) collective-permute-start(f32[208,128]{1,0:T(8,128)S(1)} %get-tuple-element.26), channel_id=1, source_target_pairs={{0,8},{1,5},{2,10},{3,7},{4,12},{5,1},{6,14},{7,3},{8,0},{9,13},{1... | collective-permute-start | bytes 319496 | tf_op jit(solution)/shard_map/ppermute | solution.py:515
  14.4 5.1 %collective-permute-start.1 = (f32[216,128]{1,0:T(8,128)S(1)}, f32[216,128]{1,0:T(8,128)S(1)}, u32[]{:S(2)}, u32[]{:S(2)}) collective-permute-start(f32[216,128]{1,0:T(8,128)S(1)} %add.51), channel_id=1, source_target_pairs={{0,8},{1,5},{2,10},{3,7},{4,12},{5,1},{6,14},{7,3},{8,0},{9,13},{1... | collective-permute-start | bytes 331784 | tf_op jit(solution)/shard_map/ppermute | solution.py:515
  16.5 6.2 %collective-permute-start.4 = (f32[208,128]{1,0:T(8,128)S(1)}, f32[208,128]{1,0:T(8,128)S(1)}, u32[]{:S(2)}, u32[]{:S(2)}) collective-permute-start(f32[208,128]{1,0:T(8,128)S(1)} %add.54), channel_id=1, source_target_pairs={{0,16},{1,9},{2,18},{3,11},{4,20},{5,13},{6,22},{7,15},{8,24},{9,1... | collective-permute-start | bytes 319496 | tf_op jit(solution)/shard_map/ppermute | solution.py:515
  19.5 8.5 %collective-permute-start.2 = (f32[216,128]{1,0:T(8,128)S(1)}, f32[216,128]{1,0:T(8,128)S(1)}, u32[]{:S(2)}, u32[]{:S(2)}) collective-permute-start(f32[216,128]{1,0:T(8,128)S(1)} %add.52), channel_id=1, source_target_pairs={{0,16},{1,9},{2,18},{3,11},{4,20},{5,13},{6,22},{7,15},{8,24},{9,1... | collective-permute-start | bytes 331784 | tf_op jit(solution)/shard_map/ppermute | solution.py:515
  22.8 4.9 %collective-permute-start.5 = (f32[208,128]{1,0:T(8,128)S(1)}, f32[208,128]{1,0:T(8,128)S(1)}, u32[]{:S(2)}, u32[]{:S(2)}) collective-permute-start(f32[208,128]{1,0:T(8,128)S(1)} %add.55), channel_id=1, source_target_pairs={{0,4},{1,17},{2,6},{3,19},{4,0},{5,21},{6,2},{7,23},{8,12},{9,25},... | collective-permute-start | bytes 319496 | tf_op jit(solution)/shard_map/ppermute | solution.py:515
  29.7 2.1 %collective-permute-start.6 = (f32[16,3968]{1,0:T(8,128)S(1)}, f32[16,3968]{1,0:T(8,128)S(1)}, u32[]{:S(2)}, u32[]{:S(2)}) collective-permute-start(f32[16,3968]{1,0:T(8,128)S(1)} %get-tuple-element.30), channel_id=1, source_target_pairs={{0,1},{1,0},{2,3},{3,2},{4,5},{5,4},{6,7},{7,6},{8,9},{9,8},{10,11... | collective-permute-start | bytes 761864 | tf_op jit(solution)/shard_map/ppermute | solution.py:515
  31.8 3.8 %collective-permute-start.8 = (f32[8,512]{1,0:T(8,128)S(1)}, f32[8,512]{1,0:T(8,128)S(1)}, u32[]{:S(2)}, u32[]{:S(2)}) collective-permute-start(f32[8,512]{1,0:T(8,128)S(1)} %slice.18), channel_id=1, source_target_pairs={{0,2},{1,3},{2,0},{3,1},{4,6},{5,7},{6,4},{7,5},{8,10},{9,11},{10,... | collective-permute-start | bytes 49160 | tf_op jit(solution)/shard_map/ppermute | solution.py:515
  33.4 4.7 %collective-permute-start.7 = (f32[8,3456]{1,0:T(8,128)S(1)}, f32[8,3456]{1,0:T(8,128)S(1)}, u32[]{:S(2)}, u32[]{:S(2)}) collective-permute-start(f32[8,3456]{1,0:T(8,128)S(1)} %slice.17), channel_id=1, source_target_pairs={{0,2},{1,5},{2,0},{3,7},{4,6},{5,1},{6,4},{7,3},{8,10},{9,13},{10,... | collective-permute-start | bytes 331784 | tf_op jit(solution)/shard_map/ppermute | solution.py:515
  33.9 24.7 %slice-start = ((s8[5206016]{0:T(1024)(128)(4,1)}), s8[4194304]{0:T(1024)(128)(4,1)S(1)}, s32[]{:S(2)}) async-start(s8[5206016]{0:T(1024)(128)(4,1)} %bitcast.4), calls=%async_computation | async-start | bytes 8388608
  33.9 5.5 %collective-permute-start.11 = (f32[8,3456]{1,0:T(8,128)S(1)}, f32[8,3456]{1,0:T(8,128)S(1)}, u32[]{:S(2)}, u32[]{:S(2)}) collective-permute-start(f32[8,3456]{1,0:T(8,128)S(1)} %slice_add_fusion.1), channel_id=1, source_target_pairs={{0,8},{1,17},{2,10},{3,19},{4,12},{5,21},{6,14},{7,23},{8,0},{9,25... | collective-permute-start | bytes 331784 | tf_op jit(solution)/shard_map/ppermute | solution.py:515
  38.1 5.2 %collective-permute-start.9 = (f32[8,3456]{1,0:T(8,128)S(1)}, f32[8,3456]{1,0:T(8,128)S(1)}, u32[]{:S(2)}, u32[]{:S(2)}) collective-permute-start(f32[8,3456]{1,0:T(8,128)S(1)} %slice_add_fusion.3), channel_id=1, source_target_pairs={{0,8},{1,17},{2,10},{3,19},{4,12},{5,21},{6,14},{7,23},{8,0},{9,25... | collective-permute-start | bytes 331784 | tf_op jit(solution)/shard_map/ppermute | solution.py:515
  39.5 5.7 %collective-permute-start.12 = (f32[8,3456]{1,0:T(8,128)S(1)}, f32[8,3456]{1,0:T(8,128)S(1)}, u32[]{:S(2)}, u32[]{:S(2)}) collective-permute-start(f32[8,3456]{1,0:T(8,128)S(1)} %add.63), channel_id=1, source_target_pairs={{0,4},{1,3},{2,6},{3,1},{4,0},{5,7},{6,2},{7,5},{8,12},{9,11},{10,... | collective-permute-start | bytes 331784 | tf_op jit(solution)/shard_map/ppermute | solution.py:515
  43.3 6.1 %collective-permute-start.10 = (f32[8,3456]{1,0:T(8,128)S(1)}, f32[8,3456]{1,0:T(8,128)S(1)}, u32[]{:S(2)}, u32[]{:S(2)}) collective-permute-start(f32[8,3456]{1,0:T(8,128)S(1)} %add.60), channel_id=1, source_target_pairs={{0,4},{1,3},{2,6},{3,1},{4,0},{5,7},{6,2},{7,5},{8,12},{9,11},{10,... | collective-permute-start | bytes 331784 | tf_op jit(solution)/shard_map/ppermute | solution.py:515
  45.2 13.3 %slice-start.1 = ((s8[5206016]{0:T(1024)(128)(4,1)}), s8[1011712]{0:T(1024)(128)(4,1)S(1)}, s32[]{:S(2)}) async-start(s8[5206016]{0:T(1024)(128)(4,1)} %bitcast.4), calls=%async_computation.1 | async-start | bytes 2023424
  45.3 13.3 %copy-start = (s32[6]{0:T(128)S(1)}, s32[6]{0:T(128)}, u32[]{:S(2)}) copy-start(s32[6]{0:T(128)} %order_ref.1) | copy-start | bytes 76
  45.3 6.9 %collective-permute-start.14 = (f32[8,3456]{1,0:T(8,128)S(1)}, f32[8,3456]{1,0:T(8,128)S(1)}, u32[]{:S(2)}, u32[]{:S(2)}) collective-permute-start(f32[8,3456]{1,0:T(8,128)S(1)} %add.64), channel_id=1, source_target_pairs={{0,16},{1,9},{2,18},{3,11},{4,20},{5,13},{6,22},{7,15},{8,24},{9,1... | collective-permute-start | bytes 331784 | tf_op jit(solution)/shard_map/ppermute | solution.py:515
  49.4 5.8 %collective-permute-start.13 = (f32[8,3456]{1,0:T(8,128)S(1)}, f32[8,3456]{1,0:T(8,128)S(1)}, u32[]{:S(2)}, u32[]{:S(2)}) collective-permute-start(f32[8,3456]{1,0:T(8,128)S(1)} %add.61), channel_id=1, source_target_pairs={{0,16},{1,9},{2,18},{3,11},{4,20},{5,13},{6,22},{7,15},{8,24},{9,1... | collective-permute-start | bytes 331784 | tf_op jit(solution)/shard_map/ppermute | solution.py:515
  52.2 4.8 %collective-permute-start.15 = (f32[8,3456]{1,0:T(8,128)S(1)}, f32[8,3456]{1,0:T(8,128)S(1)}, u32[]{:S(2)}, u32[]{:S(2)}) collective-permute-start(f32[8,3456]{1,0:T(8,128)S(1)} %add.66), channel_id=1, source_target_pairs={{0,2},{1,5},{2,0},{3,7},{4,6},{5,1},{6,4},{7,3},{8,10},{9,13},{10,... | collective-permute-start | bytes 331784 | tf_op jit(solution)/shard_map/ppermute | solution.py:515
  57.0 1.4 %collective-permute-start.17 = (f32[8,3456]{1,0:T(8,128)S(1)}, f32[8,3456]{1,0:T(8,128)S(1)}, u32[]{:S(2)}, u32[]{:S(2)}) collective-permute-start(f32[8,3456]{1,0:T(8,128)S(1)} %add.67.mine1_ref), channel_id=1, source_target_pairs={{0,1},{1,0},{2,3},{3,2},{4,5},{5,4},{6,7},{7,6},{8,9},{9,8},{10,11... | collective-permute-start | bytes 331784 | tf_op jit(solution)/shard_map/ppermute | solution.py:515
  57.1 1.5 %collective-permute-start.16 = (f32[8,3456]{1,0:T(8,128)S(1)}, f32[8,3456]{1,0:T(8,128)S(1)}, u32[]{:S(2)}, u32[]{:S(2)}) collective-permute-start(f32[8,3456]{1,0:T(8,128)S(1)} %add.65.mine0_ref), channel_id=1, source_target_pairs={{0,1},{1,0},{2,3},{3,2},{4,5},{5,4},{6,7},{7,6},{8,9},{9,8},{10,11... | collective-permute-start | bytes 331784 | tf_op jit(solution)/shard_map/ppermute | solution.py:515

commit v3 on v2

--- a/solution.py
+++ b/solution.py
@@ -348,7 +348,7 @@
         lhs_ref[k * rows : (k + 1) * rows, :] = jnp.where(group % 2 == 0, hi, mid).astype(bf16)
 
 
-def output_kernel(plan, replicas, order_ref, mine0_ref, mine1_ref, other0_ref, other1_ref, lhs_ref, low_ref, m_ref, mom_ref, err_hbm, next_hbm, z_ref, a_ref, x_ref, s_ref, err_ref, next_ref, sems):
+def output_kernel(plan, replicas, order_ref, mine0_ref, mine1_ref, other0_ref, other1_ref, lhs_ref, low_ref, m_ref, mom_ref, err_hbm, next_hbm, z_ref, t_ref, a_ref, x_ref, s_ref, err_ref, next_ref, sems):
     rows = plan.rows
     shift = plan.shift
     row, lane = starts_of(order_ref, plan.sizes)
@@ -363,13 +363,27 @@
                 at = (2 * mine + i) % 4 * quarter
                 z_ref[at : at + quarter, :] = ref[...]
 
+    @pl.when(lane[0] != 0)
+    def _():
+        keep = lane_of((RANK, LANES)) >= shift
+        before = jnp.zeros((RANK, LANES), f32)
+        for c in range(CHUNKS):
+            columns = slice(c * LANES, (c + 1) * LANES)
+            now = pltpu.roll(z_ref[:, columns], shift, 1)
+            z_ref[:, columns] = jnp.where(keep, now, before)
+            before = now
+        t_ref[...] = before
+
+    def product(k, factor):
+        hi, mid = split2(factor)
+        return jnp.dot(
+            lhs_ref[k * rows : (k + 1) * rows, :],
+            jnp.concatenate([hi, hi, mid, mid], 0),
+            preferred_element_type=f32,
+        )
+
     for k, column, width in ((0, 0, DI), (1, COL_B, DS), (2, COL_C, DS), (3, COL_DT, DS)):
-        lhs = lhs_ref[k * rows : (k + 1) * rows, :]
-        hi, mid = split2(z_ref[:, column : column + width])
-        rhs = jnp.concatenate([hi, hi, mid, mid], 0)
-        x_ref[8 : 8 + rows, column : column + width] = lax.dot_general(
-            lhs, rhs, (((1,), (0,)), ((), ())), preferred_element_type=f32
-        )
+        x_ref[8 : 8 + rows, column : column + width] = product(k, z_ref[:, column : column + width])
 
     high = 32
     lanes1 = lane_of((1, LANES))
@@ -387,13 +401,10 @@
         def block(i, _):
             at = pl.multiple_of(8 + i * high, 8)
             base = row[0] + i * (high * CHUNKS)
-            if moved:
-                before = s_ref[pl.ds(at - 1, high), :]
             for c in range(CHUNKS):
                 now = x_ref[pl.ds(at, high), c * LANES : (c + 1) * LANES]
-                if moved:
-                    now = right(now)
-                    now, before = jnp.where(keep, now, before), now
+                if moved and c == 0:
+                    now = jnp.where(keep, now, s_ref[pl.ds(at - 1, high), :])
                 a_ref[pl.ds(base + c, high, stride=CHUNKS), :] = now
             return 0
 
@@ -447,7 +458,7 @@
 
     @pl.when(lane[0] != 0)
     def _():
-        s_ref[8 : 8 + rows, :] = right(x_ref[8 : 8 + rows, DI - LANES : DI])
+        s_ref[8 : 8 + rows, :] = product(0, t_ref[...])
         s_ref[7:8, :] = a_ref[pl.ds(row[0], 1), :]
         final = row[0] + rows * CHUNKS
         end = s_ref[rows + 7 : rows + 8, :]
@@ -603,13 +614,13 @@
         )(*made, top, low)
 
     gram, halves[0] = halves[0][:, COLS:], halves[0][:, :COLS]
-    for bit in inner:
-        gram = gram + pairwise(gram, bit, bit)
     ring = inner + outer
     n = len(ring)
     orders = [turned(ring, by) for by in (0, n // 2, 1, 1 + n // 2)]
     halves = butterfly(halves, orders, 0, 1)
     halves[0], gram = lax.optimization_barrier((halves[0], gram))
+    for bit in inner:
+        gram = gram + pairwise(gram, bit, bit)
     halves = butterfly(halves, orders, 1, 2)
     halves[1], gram = lax.optimization_barrier((halves[1], gram))
     halves = butterfly(halves, orders, 2, 3)
@@ -628,6 +639,7 @@
         out_specs=tuple(specs(HBM, HBM)),
         scratch_shapes=[
             pltpu.VMEM((RANK, COLS), f32),
+            pltpu.VMEM((RANK, LANES), f32),
             pltpu.VMEM((plan.buf_rows, LANES), f32),
             pltpu.VMEM((rows + 8, COLS), f32),
             pltpu.VMEM((rows + 24, LANES), f32),

time: 65.6 us -> 64.2 us (0.979); the launches traced: 66.6 us -> 64.2 us
  waiting for transfers between devices: 14.8 us -> 12.6 us
  Pallas kernels: 22.2 us -> 20.1 us
  starting transfers between devices: 28.6 us -> 30.4 us
    ppermute x18, waiting for transfers between devices: 14.8 us -> 12.6 us  [pairwise(): lax.ppermute(x, ('dp', 'mp'), [(i, i ^ (second if i % 2 else first)) for...]
    ppermute x18, starting transfers between devices: 28.6 us -> 30.4 us  [pairwise(): lax.ppermute(x, ('dp', 'mp'), [(i, i ^ (second if i % 2 else first)) for...]
    pallas_call x1, Pallas kernels: 8.04 us -> 6.83 us  [body(): pl.pallas_call(functools.partial(output_kernel, plan, replicas), out_shap...]
    pallas_call x1, Pallas kernels: 7.97 us -> 7.15 us  [body(): pl.pallas_call(functools.partial(panel_kernel, plan), out_shape=(shape((p...]
where the time goes in v3:
time: 64.2 us
  starting transfers between devices  30.4 us (47%)
  Pallas kernels  20.1 us (31%)
  waiting for transfers between devices  12.6 us (20%)
  between operations  0.79 us (1%)
    ppermute x18, starting transfers between devices, pairwise(): lax.ppermute(x, ('dp', 'mp'), [(i, i ^ (second if i % 2 else first)) for...  30.4 us
    ppermute x18, waiting for transfers between devices, pairwise(): lax.ppermute(x, ('dp', 'mp'), [(i, i ^ (second if i % 2 else first)) for...  12.6 us
    pallas_call x1, Pallas kernels, body(): pl.pallas_call(functools.partial(panel_kernel, plan), out_shape=(shape((p...  7.15 us
    pallas_call x1, Pallas kernels, body(): pl.pallas_call(functools.partial(output_kernel, plan, replicas), out_shap...  6.83 us
    pallas_call x1, Pallas kernels, frame(): pl.pallas_call(functools.partial(frame_kernel, plan, replicas), out_shape...  2.93 us
    pallas_call x1, Pallas kernels, body(): pl.pallas_call(functools.partial(factor_kernel, plan), out_shape=(shape((...  1.64 us
    pallas_call x1, Pallas kernels, begin(): pl.pallas_call(begin_kernel, out_shape=(square, square, shape((8, LANES),...  1.6 us
  transfers between devices with their start and end apart: 18, of which 12 were waited for; matrix products, arithmetic and copies ran while one was open for 0% of the time, Pallas kernels for 7%

profile of v3, /device:TPU:0, one launch (start us, length us, event | category | flops | bytes accessed | tf_op | source)
XLA Modules:
  0.0 64.2 jit_solution(13346340261999124530)
XLA Ops:
  0.6 7.2 %shard_map.95 = (f32[216,128]{1,0:T(8,128)S(1)}, f32[208,128]{1,0:T(8,128)S(1)}, bf16[384,3456]{1,0:T(8,128)(2,1)S(1)}, bf16[384,3456]{1,0:T(8,128)(2,1)S(1)}, f32[10192,128]{1,0:T(8,128)S(1)}) custom-call(s32[6]{0:T(128)} %order_ref.1, bf16[1,1300580]{1,0:T(2,128)(2,1)} %g_hbm.1, bf16[1,1300580]{1,0:T(2,128)(2,1)} %e_hbm.1, f32[32,3072]{1,0:T(8,128)} %bitcast.6, ...), custom_call_target="tpu_custom_call" | custom-call | flops 679477248 | bytes 10404640 | tf_op jit(solution)/shard_map/pallas_call | solution.py:549
  7.8 3.0 %collective-permute-start = (f32[216,128]{1,0:T(8,128)S(1)}, f32[216,128]{1,0:T(8,128)S(1)}, u32[]{:S(2)}, u32[]{:S(2)}) collective-permute-start(f32[216,128]{1,0:T(8,128)S(1)} %get-tuple-element.25), channel_id=1, source_target_pairs={{0,4},{1,17},{2,6},{3,19},{4,0},{5,21},{6,2},{7,23},{8,12},{9,25},... | collective-permute-start | bytes 331784 | tf_op jit(solution)/shard_map/ppermute | solution.py:526
  10.8 1.6 %collective-permute-start.3 = (f32[208,128]{1,0:T(8,128)S(1)}, f32[208,128]{1,0:T(8,128)S(1)}, u32[]{:S(2)}, u32[]{:S(2)}) collective-permute-start(f32[208,128]{1,0:T(8,128)S(1)} %get-tuple-element.26), channel_id=1, source_target_pairs={{0,8},{1,5},{2,10},{3,7},{4,12},{5,1},{6,14},{7,3},{8,0},{9,13},{1... | collective-permute-start | bytes 319496 | tf_op jit(solution)/shard_map/ppermute | solution.py:526
  12.4 1.1 %collective-permute-done = f32[216,128]{1,0:T(8,128)S(1)} collective-permute-done((f32[216,128]{1,0:T(8,128)S(1)}, f32[216,128]{1,0:T(8,128)S(1)}, u32[]{:S(2)}, u32[]{:S(2)}) %collective-permute-start) | collective-permute-done | bytes 110624 | tf_op jit(solution)/shard_map/ppermute | solution.py:526
  13.6 2.1 %collective-permute-start.1 = (f32[216,128]{1,0:T(8,128)S(1)}, f32[216,128]{1,0:T(8,128)S(1)}, u32[]{:S(2)}, u32[]{:S(2)}) collective-permute-start(f32[216,128]{1,0:T(8,128)S(1)} %add.51), channel_id=1, source_target_pairs={{0,8},{1,5},{2,10},{3,7},{4,12},{5,1},{6,14},{7,3},{8,0},{9,13},{1... | collective-permute-start | bytes 331784 | tf_op jit(solution)/shard_map/ppermute | solution.py:526
  15.7 0.0 collective-permute-done.3
  15.7 2.7 %collective-permute-start.4 = (f32[208,128]{1,0:T(8,128)S(1)}, f32[208,128]{1,0:T(8,128)S(1)}, u32[]{:S(2)}, u32[]{:S(2)}) collective-permute-start(f32[208,128]{1,0:T(8,128)S(1)} %add.54), channel_id=1, source_target_pairs={{0,16},{1,9},{2,18},{3,11},{4,20},{5,13},{6,22},{7,15},{8,24},{9,1... | collective-permute-start | bytes 319496 | tf_op jit(solution)/shard_map/ppermute | solution.py:526
  18.5 0.3 collective-permute-done.1
  18.7 3.2 %collective-permute-start.2 = (f32[216,128]{1,0:T(8,128)S(1)}, f32[216,128]{1,0:T(8,128)S(1)}, u32[]{:S(2)}, u32[]{:S(2)}) collective-permute-start(f32[216,128]{1,0:T(8,128)S(1)} %add.52), channel_id=1, source_target_pairs={{0,16},{1,9},{2,18},{3,11},{4,20},{5,13},{6,22},{7,15},{8,24},{9,1... | collective-permute-start | bytes 331784 | tf_op jit(solution)/shard_map/ppermute | solution.py:526
  22.0 0.0 collective-permute-done.4
  22.0 2.2 %collective-permute-start.5 = (f32[208,128]{1,0:T(8,128)S(1)}, f32[208,128]{1,0:T(8,128)S(1)}, u32[]{:S(2)}, u32[]{:S(2)}) collective-permute-start(f32[208,128]{1,0:T(8,128)S(1)} %add.55), channel_id=1, source_target_pairs={{0,4},{1,17},{2,6},{3,19},{4,0},{5,21},{6,2},{7,23},{8,12},{9,25},... | collective-permute-start | bytes 319496 | tf_op jit(solution)/shard_map/ppermute | solution.py:526
  24.2 2.7 %collective-permute-done.5 = f32[208,128]{1,0:T(8,128)S(1)} collective-permute-done((f32[208,128]{1,0:T(8,128)S(1)}, f32[208,128]{1,0:T(8,128)S(1)}, u32[]{:S(2)}, u32[]{:S(2)}) %collective-permute-start.5) | collective-permute-done | bytes 106528 | tf_op jit(solution)/shard_map/ppermute | solution.py:526
  26.9 0.3 collective-permute-done.2
  27.2 1.6 %shard_map.96 = (f32[8,3968]{1,0:T(8,128)S(1)}, f32[8,3456]{1,0:T(8,128)S(1)}, f32[16,3968]{1,0:T(8,128)S(1)}) custom-call(f32[216,128]{1,0:T(8,128)S(1)} %add.53.top_ref, f32[208,128]{1,0:T(8,128)S(1)} %add.56.low_ref, bf16[384,3456]{1,0:T(8,128)(2,1)S(1)} %get-tuple-element.27.mh_ref, bf16[384,3456]{1,0:T(8,128)(2,1)S(1)} %get-tuple-element.28.ml_ref), custom_call_target="tpu_custom_call" | custom-call | flops 679477248 | bytes 5202320 | tf_op jit(solution)/shard_map/pallas_call | solution.py:583
  28.8 0.9 %collective-permute-start.6 = (f32[16,3968]{1,0:T(8,128)S(1)}, f32[16,3968]{1,0:T(8,128)S(1)}, u32[]{:S(2)}, u32[]{:S(2)}) collective-permute-start(f32[16,3968]{1,0:T(8,128)S(1)} %get-tuple-element.30), channel_id=1, source_target_pairs={{0,1},{1,0},{2,3},{3,2},{4,5},{5,4},{6,7},{7,6},{8,9},{9,8},{10,11... | collective-permute-start | bytes 761864 | tf_op jit(solution)/shard_map/ppermute | solution.py:526
  29.8 1.2 %collective-permute-done.6 = f32[16,3968]{1,0:T(8,128)S(1)} collective-permute-done((f32[16,3968]{1,0:T(8,128)S(1)}, f32[16,3968]{1,0:T(8,128)S(1)}, u32[]{:S(2)}, u32[]{:S(2)}) %collective-permute-start.6) | collective-permute-done | bytes 253984 | tf_op jit(solution)/shard_map/ppermute | solution.py:526
  30.9 1.6 %collective-permute-start.7 = (f32[8,3456]{1,0:T(8,128)S(1)}, f32[8,3456]{1,0:T(8,128)S(1)}, u32[]{:S(2)}, u32[]{:S(2)}) collective-permute-start(f32[8,3456]{1,0:T(8,128)S(1)} %slice.17), channel_id=1, source_target_pairs={{0,2},{1,5},{2,0},{3,7},{4,6},{5,1},{6,4},{7,3},{8,10},{9,13},{10,... | collective-permute-start | bytes 331784 | tf_op jit(solution)/shard_map/ppermute | solution.py:526
  32.5 1.3 %collective-permute-start.10 = (f32[8,3456]{1,0:T(8,128)S(1)}, f32[8,3456]{1,0:T(8,128)S(1)}, u32[]{:S(2)}, u32[]{:S(2)}) collective-permute-start(f32[8,3456]{1,0:T(8,128)S(1)} %slice_add_fusion.1), channel_id=1, source_target_pairs={{0,8},{1,17},{2,10},{3,19},{4,12},{5,21},{6,14},{7,23},{8,0},{9,25... | collective-permute-start | bytes 331784 | tf_op jit(solution)/shard_map/ppermute | solution.py:526
  33.9 1.9 %collective-permute-done.7 = f32[8,3456]{1,0:T(8,128)S(1)} collective-permute-done((f32[8,3456]{1,0:T(8,128)S(1)}, f32[8,3456]{1,0:T(8,128)S(1)}, u32[]{:S(2)}, u32[]{:S(2)}) %collective-permute-start.7) | collective-permute-done | bytes 110624 | tf_op jit(solution)/shard_map/ppermute | solution.py:526
  35.8 0.0 slice-start
  35.8 1.3 %collective-permute-start.8 = (f32[8,3456]{1,0:T(8,128)S(1)}, f32[8,3456]{1,0:T(8,128)S(1)}, u32[]{:S(2)}, u32[]{:S(2)}) collective-permute-start(f32[8,3456]{1,0:T(8,128)S(1)} %slice_add_fusion.2), channel_id=1, source_target_pairs={{0,8},{1,17},{2,10},{3,19},{4,12},{5,21},{6,14},{7,23},{8,0},{9,25... | collective-permute-start | bytes 331784 | tf_op jit(solution)/shard_map/ppermute | solution.py:526
  37.1 1.2 %collective-permute-done.10 = f32[8,3456]{1,0:T(8,128)S(1)} collective-permute-done((f32[8,3456]{1,0:T(8,128)S(1)}, f32[8,3456]{1,0:T(8,128)S(1)}, u32[]{:S(2)}, u32[]{:S(2)}) %collective-permute-start.10) | collective-permute-done | bytes 110624 | tf_op jit(solution)/shard_map/ppermute | solution.py:526
  38.4 1.4 %collective-permute-start.11 = (f32[8,3456]{1,0:T(8,128)S(1)}, f32[8,3456]{1,0:T(8,128)S(1)}, u32[]{:S(2)}, u32[]{:S(2)}) collective-permute-start(f32[8,3456]{1,0:T(8,128)S(1)} %add.62), channel_id=1, source_target_pairs={{0,4},{1,3},{2,6},{3,1},{4,0},{5,7},{6,2},{7,5},{8,12},{9,11},{10,... | collective-permute-start | bytes 331784 | tf_op jit(solution)/shard_map/ppermute | solution.py:526
  39.7 1.2 %collective-permute-start.12 = (f32[8,512]{1,0:T(8,128)S(1)}, f32[8,512]{1,0:T(8,128)S(1)}, u32[]{:S(2)}, u32[]{:S(2)}) collective-permute-start(f32[8,512]{1,0:T(8,128)S(1)} %slice.18), channel_id=1, source_target_pairs={{0,2},{1,3},{2,0},{3,1},{4,6},{5,7},{6,4},{7,5},{8,10},{9,11},{10,... | collective-permute-start | bytes 49160 | tf_op jit(solution)/shard_map/ppermute | solution.py:526
  40.9 2.6 %collective-permute-done.12 = f32[8,512]{1,0:T(8,128)S(1)} collective-permute-done((f32[8,512]{1,0:T(8,128)S(1)}, f32[8,512]{1,0:T(8,128)S(1)}, u32[]{:S(2)}, u32[]{:S(2)}) %collective-permute-start.12) | collective-permute-done | bytes 16416 | tf_op jit(solution)/shard_map/ppermute | solution.py:526
  43.5 0.0 collective-permute-done.8
  43.5 0.8 %collective-permute-start.9 = (f32[8,3456]{1,0:T(8,128)S(1)}, f32[8,3456]{1,0:T(8,128)S(1)}, u32[]{:S(2)}, u32[]{:S(2)}) collective-permute-start(f32[8,3456]{1,0:T(8,128)S(1)} %add.59), channel_id=1, source_target_pairs={{0,4},{1,3},{2,6},{3,1},{4,0},{5,7},{6,2},{7,5},{8,12},{9,11},{10,... | collective-permute-start | bytes 331784 | tf_op jit(solution)/shard_map/ppermute | solution.py:526
  44.3 0.0 collective-permute-done.11
  44.3 0.0 slice-start.1
  44.3 0.0 copy-start
  44.3 2.3 %collective-permute-start.14 = (f32[8,3456]{1,0:T(8,128)S(1)}, f32[8,3456]{1,0:T(8,128)S(1)}, u32[]{:S(2)}, u32[]{:S(2)}) collective-permute-start(f32[8,3456]{1,0:T(8,128)S(1)} %add.63), channel_id=1, source_target_pairs={{0,16},{1,9},{2,18},{3,11},{4,20},{5,13},{6,22},{7,15},{8,24},{9,1... | collective-permute-start | bytes 331784 | tf_op jit(solution)/shard_map/ppermute | solution.py:526
  46.6 1.6 %shard_map.97 = (f32[128,128]{1,0:T(8,128)S(1)}, f32[128,128]{1,0:T(8,128)S(1)}, f32[8,128]{1,0:T(8,128)S(1)}) custom-call(f32[8,512]{1,0:T(8,128)S(1)} %add.64.sum_ref), custom_call_target="tpu_custom_call" | custom-call | flops 1500000000 | bytes 200000 | tf_op jit(solution)/shard_map/pallas_call | solution.py:597
  48.2 0.1 collective-permute-done.9
  48.3 2.6 %collective-permute-start.13 = (f32[8,3456]{1,0:T(8,128)S(1)}, f32[8,3456]{1,0:T(8,128)S(1)}, u32[]{:S(2)}, u32[]{:S(2)}) collective-permute-start(f32[8,3456]{1,0:T(8,128)S(1)} %add.60), channel_id=1, source_target_pairs={{0,16},{1,9},{2,18},{3,11},{4,20},{5,13},{6,22},{7,15},{8,24},{9,1... | collective-permute-start | bytes 331784 | tf_op jit(solution)/shard_map/ppermute | solution.py:526
  50.9 0.0 collective-permute-done.14
  50.9 1.6 %collective-permute-start.15 = (f32[8,3456]{1,0:T(8,128)S(1)}, f32[8,3456]{1,0:T(8,128)S(1)}, u32[]{:S(2)}, u32[]{:S(2)}) collective-permute-start(f32[8,3456]{1,0:T(8,128)S(1)} %add.66), channel_id=1, source_target_pairs={{0,2},{1,5},{2,0},{3,7},{4,6},{5,1},{6,4},{7,3},{8,10},{9,13},{10,... | collective-permute-start | bytes 331784 | tf_op jit(solution)/shard_map/ppermute | solution.py:526
  52.5 2.9 %shard_map.98.lhs_ref = bf16[1536,128]{1,0:T(8,128)(2,1)S(1)} custom-call(f32[128,128]{1,0:T(8,128)S(1)} %get-tuple-element.39.gram_ref, f32[128,128]{1,0:T(8,128)S(1)} %get-tuple-element.40.turned_ref, f32[8,128]{1,0:T(8,128)S(1)} %get-tuple-element.41.scale_ref, f32[216,128]{1,0:T(8,128)S(1)} %add.53.top_ref, f32[208,128]{1,0:T(8,128)S(1)} %add.56.low_ref), custom_call_target="tpu_custom_call" | custom-call | flops 1500000000 | bytes 600000 | tf_op jit(solution)/shard_map/pallas_call | solution.py:607
  55.4 0.0 collective-permute-done.13
  55.5 0.3 collective-permute-done.15
  55.8 0.1 collective-permute-start.17
  55.8 0.5 collective-permute-start.16
  56.3 0.8 %collective-permute-done.17.other1_ref = f32[8,3456]{1,0:T(8,128)S(1)} collective-permute-done((f32[8,3456]{1,0:T(8,128)S(1)}, f32[8,3456]{1,0:T(8,128)S(1)}, u32[]{:S(2)}, u32[]{:S(2)}) %collective-permute-start.17) | collective-permute-done | bytes 110624 | tf_op jit(solution)/shard_map/ppermute | solution.py:526
  57.1 0.2 collective-permute-done.16.other0_ref
  57.3 0.0 slice-done
  57.3 0.0 slice-done.1
  57.3 0.0 copy-done
  57.3 6.8 %shard_map.99 = (bf16[1,1300580]{1,0:T(2,128)(2,1)}, f32[1300580]{0:T(1024)}) custom-call(s32[6]{0:T(128)S(1)} %copy-done, f32[8,3456]{1,0:T(8,128)S(1)} %add.65.mine0_ref, f32[8,3456]{1,0:T(8,128)S(1)} %add.67.mine1_ref, f32[8,3456]{1,0:T(8,128)S(1)} %collective-permute-done.16.other0_ref, f32[8,3456]{1,0:T(8,128)S(1)} %collective-permute-done.17.other1_ref, ...), custom_call_target="tpu_custom_call" | custom-call | flops 339738624 | bytes 20809280 | tf_op jit(solution)/shard_map/pallas_call | solution.py:635
  (20 shorter events, 0.3 us)
Async XLA Ops:
  7.8 5.8 %collective-permute-start = (f32[216,128]{1,0:T(8,128)S(1)}, f32[216,128]{1,0:T(8,128)S(1)}, u32[]{:S(2)}, u32[]{:S(2)}) collective-permute-start(f32[216,128]{1,0:T(8,128)S(1)} %get-tuple-element.25), channel_id=1, source_target_pairs={{0,4},{1,17},{2,6},{3,19},{4,0},{5,21},{6,2},{7,23},{8,12},{9,25},... | collective-permute-start | bytes 331784 | tf_op jit(solution)/shard_map/ppermute | solution.py:526
  10.8 4.9 %collective-permute-start.3 = (f32[208,128]{1,0:T(8,128)S(1)}, f32[208,128]{1,0:T(8,128)S(1)}, u32[]{:S(2)}, u32[]{:S(2)}) collective-permute-start(f32[208,128]{1,0:T(8,128)S(1)} %get-tuple-element.26), channel_id=1, source_target_pairs={{0,8},{1,5},{2,10},{3,7},{4,12},{5,1},{6,14},{7,3},{8,0},{9,13},{1... | collective-permute-start | bytes 319496 | tf_op jit(solution)/shard_map/ppermute | solution.py:526
  13.6 5.2 %collective-permute-start.1 = (f32[216,128]{1,0:T(8,128)S(1)}, f32[216,128]{1,0:T(8,128)S(1)}, u32[]{:S(2)}, u32[]{:S(2)}) collective-permute-start(f32[216,128]{1,0:T(8,128)S(1)} %add.51), channel_id=1, source_target_pairs={{0,8},{1,5},{2,10},{3,7},{4,12},{5,1},{6,14},{7,3},{8,0},{9,13},{1... | collective-permute-start | bytes 331784 | tf_op jit(solution)/shard_map/ppermute | solution.py:526
  15.7 6.2 %collective-permute-start.4 = (f32[208,128]{1,0:T(8,128)S(1)}, f32[208,128]{1,0:T(8,128)S(1)}, u32[]{:S(2)}, u32[]{:S(2)}) collective-permute-start(f32[208,128]{1,0:T(8,128)S(1)} %add.54), channel_id=1, source_target_pairs={{0,16},{1,9},{2,18},{3,11},{4,20},{5,13},{6,22},{7,15},{8,24},{9,1... | collective-permute-start | bytes 319496 | tf_op jit(solution)/shard_map/ppermute | solution.py:526
  18.7 8.4 %collective-permute-start.2 = (f32[216,128]{1,0:T(8,128)S(1)}, f32[216,128]{1,0:T(8,128)S(1)}, u32[]{:S(2)}, u32[]{:S(2)}) collective-permute-start(f32[216,128]{1,0:T(8,128)S(1)} %add.52), channel_id=1, source_target_pairs={{0,16},{1,9},{2,18},{3,11},{4,20},{5,13},{6,22},{7,15},{8,24},{9,1... | collective-permute-start | bytes 331784 | tf_op jit(solution)/shard_map/ppermute | solution.py:526
  22.0 4.9 %collective-permute-start.5 = (f32[208,128]{1,0:T(8,128)S(1)}, f32[208,128]{1,0:T(8,128)S(1)}, u32[]{:S(2)}, u32[]{:S(2)}) collective-permute-start(f32[208,128]{1,0:T(8,128)S(1)} %add.55), channel_id=1, source_target_pairs={{0,4},{1,17},{2,6},{3,19},{4,0},{5,21},{6,2},{7,23},{8,12},{9,25},... | collective-permute-start | bytes 319496 | tf_op jit(solution)/shard_map/ppermute | solution.py:526
  28.8 2.1 %collective-permute-start.6 = (f32[16,3968]{1,0:T(8,128)S(1)}, f32[16,3968]{1,0:T(8,128)S(1)}, u32[]{:S(2)}, u32[]{:S(2)}) collective-permute-start(f32[16,3968]{1,0:T(8,128)S(1)} %get-tuple-element.30), channel_id=1, source_target_pairs={{0,1},{1,0},{2,3},{3,2},{4,5},{5,4},{6,7},{7,6},{8,9},{9,8},{10,11... | collective-permute-start | bytes 761864 | tf_op jit(solution)/shard_map/ppermute | solution.py:526
  30.9 4.8 %collective-permute-start.7 = (f32[8,3456]{1,0:T(8,128)S(1)}, f32[8,3456]{1,0:T(8,128)S(1)}, u32[]{:S(2)}, u32[]{:S(2)}) collective-permute-start(f32[8,3456]{1,0:T(8,128)S(1)} %slice.17), channel_id=1, source_target_pairs={{0,2},{1,5},{2,0},{3,7},{4,6},{5,1},{6,4},{7,3},{8,10},{9,13},{10,... | collective-permute-start | bytes 331784 | tf_op jit(solution)/shard_map/ppermute | solution.py:526
  32.5 5.8 %collective-permute-start.10 = (f32[8,3456]{1,0:T(8,128)S(1)}, f32[8,3456]{1,0:T(8,128)S(1)}, u32[]{:S(2)}, u32[]{:S(2)}) collective-permute-start(f32[8,3456]{1,0:T(8,128)S(1)} %slice_add_fusion.1), channel_id=1, source_target_pairs={{0,8},{1,17},{2,10},{3,19},{4,12},{5,21},{6,14},{7,23},{8,0},{9,25... | collective-permute-start | bytes 331784 | tf_op jit(solution)/shard_map/ppermute | solution.py:526
  35.8 21.5 %slice-start = ((s8[5206016]{0:T(1024)(128)(4,1)}), s8[4194304]{0:T(1024)(128)(4,1)S(1)}, s32[]{:S(2)}) async-start(s8[5206016]{0:T(1024)(128)(4,1)} %bitcast.4), calls=%async_computation | async-start | bytes 8388608
  35.8 7.7 %collective-permute-start.8 = (f32[8,3456]{1,0:T(8,128)S(1)}, f32[8,3456]{1,0:T(8,128)S(1)}, u32[]{:S(2)}, u32[]{:S(2)}) collective-permute-start(f32[8,3456]{1,0:T(8,128)S(1)} %slice_add_fusion.2), channel_id=1, source_target_pairs={{0,8},{1,17},{2,10},{3,19},{4,12},{5,21},{6,14},{7,23},{8,0},{9,25... | collective-permute-start | bytes 331784 | tf_op jit(solution)/shard_map/ppermute | solution.py:526
  38.4 5.9 %collective-permute-start.11 = (f32[8,3456]{1,0:T(8,128)S(1)}, f32[8,3456]{1,0:T(8,128)S(1)}, u32[]{:S(2)}, u32[]{:S(2)}) collective-permute-start(f32[8,3456]{1,0:T(8,128)S(1)} %add.62), channel_id=1, source_target_pairs={{0,4},{1,3},{2,6},{3,1},{4,0},{5,7},{6,2},{7,5},{8,12},{9,11},{10,... | collective-permute-start | bytes 331784 | tf_op jit(solution)/shard_map/ppermute | solution.py:526
  39.7 3.7 %collective-permute-start.12 = (f32[8,512]{1,0:T(8,128)S(1)}, f32[8,512]{1,0:T(8,128)S(1)}, u32[]{:S(2)}, u32[]{:S(2)}) collective-permute-start(f32[8,512]{1,0:T(8,128)S(1)} %slice.18), channel_id=1, source_target_pairs={{0,2},{1,3},{2,0},{3,1},{4,6},{5,7},{6,4},{7,5},{8,10},{9,11},{10,... | collective-permute-start | bytes 49160 | tf_op jit(solution)/shard_map/ppermute | solution.py:526
  43.5 4.8 %collective-permute-start.9 = (f32[8,3456]{1,0:T(8,128)S(1)}, f32[8,3456]{1,0:T(8,128)S(1)}, u32[]{:S(2)}, u32[]{:S(2)}) collective-permute-start(f32[8,3456]{1,0:T(8,128)S(1)} %add.59), channel_id=1, source_target_pairs={{0,4},{1,3},{2,6},{3,1},{4,0},{5,7},{6,2},{7,5},{8,12},{9,11},{10,... | collective-permute-start | bytes 331784 | tf_op jit(solution)/shard_map/ppermute | solution.py:526
  44.3 13.0 %slice-start.1 = ((s8[5206016]{0:T(1024)(128)(4,1)}), s8[1011712]{0:T(1024)(128)(4,1)S(1)}, s32[]{:S(2)}) async-start(s8[5206016]{0:T(1024)(128)(4,1)} %bitcast.4), calls=%async_computation.1 | async-start | bytes 2023424
  44.3 13.0 %copy-start = (s32[6]{0:T(128)S(1)}, s32[6]{0:T(128)}, u32[]{:S(2)}) copy-start(s32[6]{0:T(128)} %order_ref.1) | copy-start | bytes 76
  44.3 6.6 %collective-permute-start.14 = (f32[8,3456]{1,0:T(8,128)S(1)}, f32[8,3456]{1,0:T(8,128)S(1)}, u32[]{:S(2)}, u32[]{:S(2)}) collective-permute-start(f32[8,3456]{1,0:T(8,128)S(1)} %add.63), channel_id=1, source_target_pairs={{0,16},{1,9},{2,18},{3,11},{4,20},{5,13},{6,22},{7,15},{8,24},{9,1... | collective-permute-start | bytes 331784 | tf_op jit(solution)/shard_map/ppermute | solution.py:526
  48.3 7.1 %collective-permute-start.13 = (f32[8,3456]{1,0:T(8,128)S(1)}, f32[8,3456]{1,0:T(8,128)S(1)}, u32[]{:S(2)}, u32[]{:S(2)}) collective-permute-start(f32[8,3456]{1,0:T(8,128)S(1)} %add.60), channel_id=1, source_target_pairs={{0,16},{1,9},{2,18},{3,11},{4,20},{5,13},{6,22},{7,15},{8,24},{9,1... | collective-permute-start | bytes 331784 | tf_op jit(solution)/shard_map/ppermute | solution.py:526
  50.9 4.8 %collective-permute-start.15 = (f32[8,3456]{1,0:T(8,128)S(1)}, f32[8,3456]{1,0:T(8,128)S(1)}, u32[]{:S(2)}, u32[]{:S(2)}) collective-permute-start(f32[8,3456]{1,0:T(8,128)S(1)} %add.66), channel_id=1, source_target_pairs={{0,2},{1,5},{2,0},{3,7},{4,6},{5,1},{6,4},{7,3},{8,10},{9,13},{10,... | collective-permute-start | bytes 331784 | tf_op jit(solution)/shard_map/ppermute | solution.py:526
  55.8 1.4 %collective-permute-start.17 = (f32[8,3456]{1,0:T(8,128)S(1)}, f32[8,3456]{1,0:T(8,128)S(1)}, u32[]{:S(2)}, u32[]{:S(2)}) collective-permute-start(f32[8,3456]{1,0:T(8,128)S(1)} %add.67.mine1_ref), channel_id=1, source_target_pairs={{0,1},{1,0},{2,3},{3,2},{4,5},{5,4},{6,7},{7,6},{8,9},{9,8},{10,11... | collective-permute-start | bytes 331784 | tf_op jit(solution)/shard_map/ppermute | solution.py:526
  55.8 1.5 %collective-permute-start.16 = (f32[8,3456]{1,0:T(8,128)S(1)}, f32[8,3456]{1,0:T(8,128)S(1)}, u32[]{:S(2)}, u32[]{:S(2)}) collective-permute-start(f32[8,3456]{1,0:T(8,128)S(1)} %add.65.mine0_ref), channel_id=1, source_target_pairs={{0,1},{1,0},{2,3},{3,2},{4,5},{5,4},{6,7},{7,6},{8,9},{9,8},{10,11... | collective-permute-start | bytes 331784 | tf_op jit(solution)/shard_map/ppermute | solution.py:526

commit v4 on v3

--- a/solution.py
+++ b/solution.py
@@ -31,7 +31,7 @@
 CHUNKS = DI // LANES
 
 MERGE = 256
-FINISH = 128
+FINISH = 256
 PIECES = 8
 
 f32 = jnp.float32
@@ -171,7 +171,7 @@
         mh_ref[pl.ds(at, count), column : column + LANES] = hi
         ml_ref[pl.ds(at, count), column : column + LANES] = lo
 
-    high = 32
+    high = 64
 
     def read_x(first, last, moved):
         keep = lane_of((high, LANES)) < LANES - shift

time: 64.2 us -> 63.9 us (level)
    pallas_call x1, Pallas kernels: 6.83 us -> 6.09 us  [body(): pl.pallas_call(functools.partial(output_kernel, plan, replicas), out_shap...]
where the time goes in v4:
time: 63.9 us; the launch traced here: 63.7 us
  starting transfers between devices  30.4 us (48%)
  Pallas kernels  19.5 us (31%)
  waiting for transfers between devices  12.6 us (20%)
  between operations  0.95 us (1%)
    ppermute x18, starting transfers between devices, pairwise(): lax.ppermute(x, ('dp', 'mp'), [(i, i ^ (second if i % 2 else first)) for...  30.4 us
    ppermute x18, waiting for transfers between devices, pairwise(): lax.ppermute(x, ('dp', 'mp'), [(i, i ^ (second if i % 2 else first)) for...  12.6 us
    pallas_call x1, Pallas kernels, body(): pl.pallas_call(functools.partial(panel_kernel, plan), out_shape=(shape((p...  7.06 us
    pallas_call x1, Pallas kernels, body(): pl.pallas_call(functools.partial(output_kernel, plan, replicas), out_shap...  6.09 us
    pallas_call x1, Pallas kernels, frame(): pl.pallas_call(functools.partial(frame_kernel, plan, replicas), out_shape...  2.93 us
    pallas_call x1, Pallas kernels, body(): pl.pallas_call(functools.partial(factor_kernel, plan), out_shape=(shape((...  1.82 us
    pallas_call x1, Pallas kernels, begin(): pl.pallas_call(begin_kernel, out_shape=(square, square, shape((8, LANES),...  1.6 us
  transfers between devices with their start and end apart: 18, of which 12 were waited for; matrix products, arithmetic and copies ran while one was open for 0% of the time, Pallas kernels for 7%

profile of v4, /device:TPU:0, one launch (start us, length us, event | category | flops | bytes accessed | tf_op | source)
XLA Modules:
  0.0 63.7 jit_solution(12879777206455281045)
XLA Ops:
  0.6 7.1 %shard_map.95 = (f32[216,128]{1,0:T(8,128)S(1)}, f32[208,128]{1,0:T(8,128)S(1)}, bf16[384,3456]{1,0:T(8,128)(2,1)S(1)}, bf16[384,3456]{1,0:T(8,128)(2,1)S(1)}, f32[10192,128]{1,0:T(8,128)S(1)}) custom-call(s32[6]{0:T(128)} %order_ref.1, bf16[1,1300580]{1,0:T(2,128)(2,1)} %g_hbm.1, bf16[1,1300580]{1,0:T(2,128)(2,1)} %e_hbm.1, f32[32,3072]{1,0:T(8,128)} %bitcast.6, ...), custom_call_target="tpu_custom_call" | custom-call | flops 679477248 | bytes 10404640 | tf_op jit(solution)/shard_map/pallas_call | solution.py:549
  7.7 3.0 %collective-permute-start = (f32[216,128]{1,0:T(8,128)S(1)}, f32[216,128]{1,0:T(8,128)S(1)}, u32[]{:S(2)}, u32[]{:S(2)}) collective-permute-start(f32[216,128]{1,0:T(8,128)S(1)} %get-tuple-element.25), channel_id=1, source_target_pairs={{0,4},{1,17},{2,6},{3,19},{4,0},{5,21},{6,2},{7,23},{8,12},{9,25},... | collective-permute-start | bytes 331784 | tf_op jit(solution)/shard_map/ppermute | solution.py:526
  10.7 1.6 %collective-permute-start.3 = (f32[208,128]{1,0:T(8,128)S(1)}, f32[208,128]{1,0:T(8,128)S(1)}, u32[]{:S(2)}, u32[]{:S(2)}) collective-permute-start(f32[208,128]{1,0:T(8,128)S(1)} %get-tuple-element.26), channel_id=1, source_target_pairs={{0,8},{1,5},{2,10},{3,7},{4,12},{5,1},{6,14},{7,3},{8,0},{9,13},{1... | collective-permute-start | bytes 319496 | tf_op jit(solution)/shard_map/ppermute | solution.py:526
  12.3 1.2 %collective-permute-done = f32[216,128]{1,0:T(8,128)S(1)} collective-permute-done((f32[216,128]{1,0:T(8,128)S(1)}, f32[216,128]{1,0:T(8,128)S(1)}, u32[]{:S(2)}, u32[]{:S(2)}) %collective-permute-start) | collective-permute-done | bytes 110624 | tf_op jit(solution)/shard_map/ppermute | solution.py:526
  13.5 2.1 %collective-permute-start.1 = (f32[216,128]{1,0:T(8,128)S(1)}, f32[216,128]{1,0:T(8,128)S(1)}, u32[]{:S(2)}, u32[]{:S(2)}) collective-permute-start(f32[216,128]{1,0:T(8,128)S(1)} %add.51), channel_id=1, source_target_pairs={{0,8},{1,5},{2,10},{3,7},{4,12},{5,1},{6,14},{7,3},{8,0},{9,13},{1... | collective-permute-start | bytes 331784 | tf_op jit(solution)/shard_map/ppermute | solution.py:526
  15.6 0.0 collective-permute-done.3
  15.6 2.7 %collective-permute-start.4 = (f32[208,128]{1,0:T(8,128)S(1)}, f32[208,128]{1,0:T(8,128)S(1)}, u32[]{:S(2)}, u32[]{:S(2)}) collective-permute-start(f32[208,128]{1,0:T(8,128)S(1)} %add.54), channel_id=1, source_target_pairs={{0,16},{1,9},{2,18},{3,11},{4,20},{5,13},{6,22},{7,15},{8,24},{9,1... | collective-permute-start | bytes 319496 | tf_op jit(solution)/shard_map/ppermute | solution.py:526
  18.4 0.2 collective-permute-done.1
  18.6 3.2 %collective-permute-start.2 = (f32[216,128]{1,0:T(8,128)S(1)}, f32[216,128]{1,0:T(8,128)S(1)}, u32[]{:S(2)}, u32[]{:S(2)}) collective-permute-start(f32[216,128]{1,0:T(8,128)S(1)} %add.52), channel_id=1, source_target_pairs={{0,16},{1,9},{2,18},{3,11},{4,20},{5,13},{6,22},{7,15},{8,24},{9,1... | collective-permute-start | bytes 331784 | tf_op jit(solution)/shard_map/ppermute | solution.py:526
  21.9 0.0 collective-permute-done.4
  21.9 2.2 %collective-permute-start.5 = (f32[208,128]{1,0:T(8,128)S(1)}, f32[208,128]{1,0:T(8,128)S(1)}, u32[]{:S(2)}, u32[]{:S(2)}) collective-permute-start(f32[208,128]{1,0:T(8,128)S(1)} %add.55), channel_id=1, source_target_pairs={{0,4},{1,17},{2,6},{3,19},{4,0},{5,21},{6,2},{7,23},{8,12},{9,25},... | collective-permute-start | bytes 319496 | tf_op jit(solution)/shard_map/ppermute | solution.py:526
  24.1 2.7 %collective-permute-done.5 = f32[208,128]{1,0:T(8,128)S(1)} collective-permute-done((f32[208,128]{1,0:T(8,128)S(1)}, f32[208,128]{1,0:T(8,128)S(1)}, u32[]{:S(2)}, u32[]{:S(2)}) %collective-permute-start.5) | collective-permute-done | bytes 106528 | tf_op jit(solution)/shard_map/ppermute | solution.py:526
  26.8 0.3 collective-permute-done.2
  27.1 1.8 %shard_map.96 = (f32[8,3968]{1,0:T(8,128)S(1)}, f32[8,3456]{1,0:T(8,128)S(1)}, f32[16,3968]{1,0:T(8,128)S(1)}) custom-call(f32[216,128]{1,0:T(8,128)S(1)} %add.53.top_ref, f32[208,128]{1,0:T(8,128)S(1)} %add.56.low_ref, bf16[384,3456]{1,0:T(8,128)(2,1)S(1)} %get-tuple-element.27.mh_ref, bf16[384,3456]{1,0:T(8,128)(2,1)S(1)} %get-tuple-element.28.ml_ref), custom_call_target="tpu_custom_call" | custom-call | flops 679477248 | bytes 5202320 | tf_op jit(solution)/shard_map/pallas_call | solution.py:583
  28.9 0.9 %collective-permute-start.6 = (f32[16,3968]{1,0:T(8,128)S(1)}, f32[16,3968]{1,0:T(8,128)S(1)}, u32[]{:S(2)}, u32[]{:S(2)}) collective-permute-start(f32[16,3968]{1,0:T(8,128)S(1)} %get-tuple-element.30), channel_id=1, source_target_pairs={{0,1},{1,0},{2,3},{3,2},{4,5},{5,4},{6,7},{7,6},{8,9},{9,8},{10,11... | collective-permute-start | bytes 761864 | tf_op jit(solution)/shard_map/ppermute | solution.py:526
  29.8 1.2 %collective-permute-done.6 = f32[16,3968]{1,0:T(8,128)S(1)} collective-permute-done((f32[16,3968]{1,0:T(8,128)S(1)}, f32[16,3968]{1,0:T(8,128)S(1)}, u32[]{:S(2)}, u32[]{:S(2)}) %collective-permute-start.6) | collective-permute-done | bytes 253984 | tf_op jit(solution)/shard_map/ppermute | solution.py:526
  31.0 1.6 %collective-permute-start.7 = (f32[8,3456]{1,0:T(8,128)S(1)}, f32[8,3456]{1,0:T(8,128)S(1)}, u32[]{:S(2)}, u32[]{:S(2)}) collective-permute-start(f32[8,3456]{1,0:T(8,128)S(1)} %slice.17), channel_id=1, source_target_pairs={{0,2},{1,5},{2,0},{3,7},{4,6},{5,1},{6,4},{7,3},{8,10},{9,13},{10,... | collective-permute-start | bytes 331784 | tf_op jit(solution)/shard_map/ppermute | solution.py:526
  32.6 1.3 %collective-permute-start.10 = (f32[8,3456]{1,0:T(8,128)S(1)}, f32[8,3456]{1,0:T(8,128)S(1)}, u32[]{:S(2)}, u32[]{:S(2)}) collective-permute-start(f32[8,3456]{1,0:T(8,128)S(1)} %slice_add_fusion.1), channel_id=1, source_target_pairs={{0,8},{1,17},{2,10},{3,19},{4,12},{5,21},{6,14},{7,23},{8,0},{9,25... | collective-permute-start | bytes 331784 | tf_op jit(solution)/shard_map/ppermute | solution.py:526
  34.0 1.9 %collective-permute-done.7 = f32[8,3456]{1,0:T(8,128)S(1)} collective-permute-done((f32[8,3456]{1,0:T(8,128)S(1)}, f32[8,3456]{1,0:T(8,128)S(1)}, u32[]{:S(2)}, u32[]{:S(2)}) %collective-permute-start.7) | collective-permute-done | bytes 110624 | tf_op jit(solution)/shard_map/ppermute | solution.py:526
  35.8 0.0 slice-start
  35.9 1.3 %collective-permute-start.8 = (f32[8,3456]{1,0:T(8,128)S(1)}, f32[8,3456]{1,0:T(8,128)S(1)}, u32[]{:S(2)}, u32[]{:S(2)}) collective-permute-start(f32[8,3456]{1,0:T(8,128)S(1)} %slice_add_fusion.2), channel_id=1, source_target_pairs={{0,8},{1,17},{2,10},{3,19},{4,12},{5,21},{6,14},{7,23},{8,0},{9,25... | collective-permute-start | bytes 331784 | tf_op jit(solution)/shard_map/ppermute | solution.py:526
  37.2 1.2 %collective-permute-done.10 = f32[8,3456]{1,0:T(8,128)S(1)} collective-permute-done((f32[8,3456]{1,0:T(8,128)S(1)}, f32[8,3456]{1,0:T(8,128)S(1)}, u32[]{:S(2)}, u32[]{:S(2)}) %collective-permute-start.10) | collective-permute-done | bytes 110624 | tf_op jit(solution)/shard_map/ppermute | solution.py:526
  38.4 1.4 %collective-permute-start.11 = (f32[8,3456]{1,0:T(8,128)S(1)}, f32[8,3456]{1,0:T(8,128)S(1)}, u32[]{:S(2)}, u32[]{:S(2)}) collective-permute-start(f32[8,3456]{1,0:T(8,128)S(1)} %add.62), channel_id=1, source_target_pairs={{0,4},{1,3},{2,6},{3,1},{4,0},{5,7},{6,2},{7,5},{8,12},{9,11},{10,... | collective-permute-start | bytes 331784 | tf_op jit(solution)/shard_map/ppermute | solution.py:526
  39.8 1.2 %collective-permute-start.12 = (f32[8,512]{1,0:T(8,128)S(1)}, f32[8,512]{1,0:T(8,128)S(1)}, u32[]{:S(2)}, u32[]{:S(2)}) collective-permute-start(f32[8,512]{1,0:T(8,128)S(1)} %slice.18), channel_id=1, source_target_pairs={{0,2},{1,3},{2,0},{3,1},{4,6},{5,7},{6,4},{7,5},{8,10},{9,11},{10,... | collective-permute-start | bytes 49160 | tf_op jit(solution)/shard_map/ppermute | solution.py:526
  41.0 2.6 %collective-permute-done.12 = f32[8,512]{1,0:T(8,128)S(1)} collective-permute-done((f32[8,512]{1,0:T(8,128)S(1)}, f32[8,512]{1,0:T(8,128)S(1)}, u32[]{:S(2)}, u32[]{:S(2)}) %collective-permute-start.12) | collective-permute-done | bytes 16416 | tf_op jit(solution)/shard_map/ppermute | solution.py:526
  43.6 0.0 collective-permute-done.8
  43.6 0.8 %collective-permute-start.9 = (f32[8,3456]{1,0:T(8,128)S(1)}, f32[8,3456]{1,0:T(8,128)S(1)}, u32[]{:S(2)}, u32[]{:S(2)}) collective-permute-start(f32[8,3456]{1,0:T(8,128)S(1)} %add.59), channel_id=1, source_target_pairs={{0,4},{1,3},{2,6},{3,1},{4,0},{5,7},{6,2},{7,5},{8,12},{9,11},{10,... | collective-permute-start | bytes 331784 | tf_op jit(solution)/shard_map/ppermute | solution.py:526
  44.4 0.0 collective-permute-done.11
  44.4 0.0 slice-start.1
  44.4 0.0 copy-start
  44.4 2.3 %collective-permute-start.14 = (f32[8,3456]{1,0:T(8,128)S(1)}, f32[8,3456]{1,0:T(8,128)S(1)}, u32[]{:S(2)}, u32[]{:S(2)}) collective-permute-start(f32[8,3456]{1,0:T(8,128)S(1)} %add.63), channel_id=1, source_target_pairs={{0,16},{1,9},{2,18},{3,11},{4,20},{5,13},{6,22},{7,15},{8,24},{9,1... | collective-permute-start | bytes 331784 | tf_op jit(solution)/shard_map/ppermute | solution.py:526
  46.7 1.6 %shard_map.97 = (f32[128,128]{1,0:T(8,128)S(1)}, f32[128,128]{1,0:T(8,128)S(1)}, f32[8,128]{1,0:T(8,128)S(1)}) custom-call(f32[8,512]{1,0:T(8,128)S(1)} %add.64.sum_ref), custom_call_target="tpu_custom_call" | custom-call | flops 1500000000 | bytes 200000 | tf_op jit(solution)/shard_map/pallas_call | solution.py:597
  48.3 0.1 collective-permute-done.9
  48.4 2.6 %collective-permute-start.13 = (f32[8,3456]{1,0:T(8,128)S(1)}, f32[8,3456]{1,0:T(8,128)S(1)}, u32[]{:S(2)}, u32[]{:S(2)}) collective-permute-start(f32[8,3456]{1,0:T(8,128)S(1)} %add.60), channel_id=1, source_target_pairs={{0,16},{1,9},{2,18},{3,11},{4,20},{5,13},{6,22},{7,15},{8,24},{9,1... | collective-permute-start | bytes 331784 | tf_op jit(solution)/shard_map/ppermute | solution.py:526
  51.0 0.0 collective-permute-done.14
  51.0 1.6 %collective-permute-start.15 = (f32[8,3456]{1,0:T(8,128)S(1)}, f32[8,3456]{1,0:T(8,128)S(1)}, u32[]{:S(2)}, u32[]{:S(2)}) collective-permute-start(f32[8,3456]{1,0:T(8,128)S(1)} %add.66), channel_id=1, source_target_pairs={{0,2},{1,5},{2,0},{3,7},{4,6},{5,1},{6,4},{7,3},{8,10},{9,13},{10,... | collective-permute-start | bytes 331784 | tf_op jit(solution)/shard_map/ppermute | solution.py:526
  52.6 2.9 %shard_map.98.lhs_ref = bf16[1536,128]{1,0:T(8,128)(2,1)S(1)} custom-call(f32[128,128]{1,0:T(8,128)S(1)} %get-tuple-element.39.gram_ref, f32[128,128]{1,0:T(8,128)S(1)} %get-tuple-element.40.turned_ref, f32[8,128]{1,0:T(8,128)S(1)} %get-tuple-element.41.scale_ref, f32[216,128]{1,0:T(8,128)S(1)} %add.53.top_ref, f32[208,128]{1,0:T(8,128)S(1)} %add.56.low_ref), custom_call_target="tpu_custom_call" | custom-call | flops 1500000000 | bytes 600000 | tf_op jit(solution)/shard_map/pallas_call | solution.py:607
  55.5 0.0 collective-permute-done.13
  55.5 0.3 collective-permute-done.15
  55.8 0.1 collective-permute-start.17
  55.9 0.5 collective-permute-start.16
  56.4 0.8 %collective-permute-done.17.other1_ref = f32[8,3456]{1,0:T(8,128)S(1)} collective-permute-done((f32[8,3456]{1,0:T(8,128)S(1)}, f32[8,3456]{1,0:T(8,128)S(1)}, u32[]{:S(2)}, u32[]{:S(2)}) %collective-permute-start.17) | collective-permute-done | bytes 110624 | tf_op jit(solution)/shard_map/ppermute | solution.py:526
  57.2 0.2 collective-permute-done.16.other0_ref
  57.4 0.0 slice-done
  57.4 0.0 slice-done.1
  57.4 0.0 copy-done
  57.4 6.1 %shard_map.99 = (bf16[1,1300580]{1,0:T(2,128)(2,1)}, f32[1300580]{0:T(1024)}) custom-call(s32[6]{0:T(128)S(1)} %copy-done, f32[8,3456]{1,0:T(8,128)S(1)} %add.65.mine0_ref, f32[8,3456]{1,0:T(8,128)S(1)} %add.67.mine1_ref, f32[8,3456]{1,0:T(8,128)S(1)} %collective-permute-done.16.other0_ref, f32[8,3456]{1,0:T(8,128)S(1)} %collective-permute-done.17.other1_ref, ...), custom_call_target="tpu_custom_call" | custom-call | flops 339738624 | bytes 20809280 | tf_op jit(solution)/shard_map/pallas_call | solution.py:635
  (20 shorter events, 0.3 us)
Async XLA Ops:
  7.7 5.8 %collective-permute-start = (f32[216,128]{1,0:T(8,128)S(1)}, f32[216,128]{1,0:T(8,128)S(1)}, u32[]{:S(2)}, u32[]{:S(2)}) collective-permute-start(f32[216,128]{1,0:T(8,128)S(1)} %get-tuple-element.25), channel_id=1, source_target_pairs={{0,4},{1,17},{2,6},{3,19},{4,0},{5,21},{6,2},{7,23},{8,12},{9,25},... | collective-permute-start | bytes 331784 | tf_op jit(solution)/shard_map/ppermute | solution.py:526
  10.7 4.9 %collective-permute-start.3 = (f32[208,128]{1,0:T(8,128)S(1)}, f32[208,128]{1,0:T(8,128)S(1)}, u32[]{:S(2)}, u32[]{:S(2)}) collective-permute-start(f32[208,128]{1,0:T(8,128)S(1)} %get-tuple-element.26), channel_id=1, source_target_pairs={{0,8},{1,5},{2,10},{3,7},{4,12},{5,1},{6,14},{7,3},{8,0},{9,13},{1... | collective-permute-start | bytes 319496 | tf_op jit(solution)/shard_map/ppermute | solution.py:526
  13.5 5.1 %collective-permute-start.1 = (f32[216,128]{1,0:T(8,128)S(1)}, f32[216,128]{1,0:T(8,128)S(1)}, u32[]{:S(2)}, u32[]{:S(2)}) collective-permute-start(f32[216,128]{1,0:T(8,128)S(1)} %add.51), channel_id=1, source_target_pairs={{0,8},{1,5},{2,10},{3,7},{4,12},{5,1},{6,14},{7,3},{8,0},{9,13},{1... | collective-permute-start | bytes 331784 | tf_op jit(solution)/shard_map/ppermute | solution.py:526
  15.6 6.2 %collective-permute-start.4 = (f32[208,128]{1,0:T(8,128)S(1)}, f32[208,128]{1,0:T(8,128)S(1)}, u32[]{:S(2)}, u32[]{:S(2)}) collective-permute-start(f32[208,128]{1,0:T(8,128)S(1)} %add.54), channel_id=1, source_target_pairs={{0,16},{1,9},{2,18},{3,11},{4,20},{5,13},{6,22},{7,15},{8,24},{9,1... | collective-permute-start | bytes 319496 | tf_op jit(solution)/shard_map/ppermute | solution.py:526
  18.6 8.5 %collective-permute-start.2 = (f32[216,128]{1,0:T(8,128)S(1)}, f32[216,128]{1,0:T(8,128)S(1)}, u32[]{:S(2)}, u32[]{:S(2)}) collective-permute-start(f32[216,128]{1,0:T(8,128)S(1)} %add.52), channel_id=1, source_target_pairs={{0,16},{1,9},{2,18},{3,11},{4,20},{5,13},{6,22},{7,15},{8,24},{9,1... | collective-permute-start | bytes 331784 | tf_op jit(solution)/shard_map/ppermute | solution.py:526
  21.9 4.9 %collective-permute-start.5 = (f32[208,128]{1,0:T(8,128)S(1)}, f32[208,128]{1,0:T(8,128)S(1)}, u32[]{:S(2)}, u32[]{:S(2)}) collective-permute-start(f32[208,128]{1,0:T(8,128)S(1)} %add.55), channel_id=1, source_target_pairs={{0,4},{1,17},{2,6},{3,19},{4,0},{5,21},{6,2},{7,23},{8,12},{9,25},... | collective-permute-start | bytes 319496 | tf_op jit(solution)/shard_map/ppermute | solution.py:526
  28.9 2.1 %collective-permute-start.6 = (f32[16,3968]{1,0:T(8,128)S(1)}, f32[16,3968]{1,0:T(8,128)S(1)}, u32[]{:S(2)}, u32[]{:S(2)}) collective-permute-start(f32[16,3968]{1,0:T(8,128)S(1)} %get-tuple-element.30), channel_id=1, source_target_pairs={{0,1},{1,0},{2,3},{3,2},{4,5},{5,4},{6,7},{7,6},{8,9},{9,8},{10,11... | collective-permute-start | bytes 761864 | tf_op jit(solution)/shard_map/ppermute | solution.py:526
  31.0 4.8 %collective-permute-start.7 = (f32[8,3456]{1,0:T(8,128)S(1)}, f32[8,3456]{1,0:T(8,128)S(1)}, u32[]{:S(2)}, u32[]{:S(2)}) collective-permute-start(f32[8,3456]{1,0:T(8,128)S(1)} %slice.17), channel_id=1, source_target_pairs={{0,2},{1,5},{2,0},{3,7},{4,6},{5,1},{6,4},{7,3},{8,10},{9,13},{10,... | collective-permute-start | bytes 331784 | tf_op jit(solution)/shard_map/ppermute | solution.py:526
  32.6 5.8 %collective-permute-start.10 = (f32[8,3456]{1,0:T(8,128)S(1)}, f32[8,3456]{1,0:T(8,128)S(1)}, u32[]{:S(2)}, u32[]{:S(2)}) collective-permute-start(f32[8,3456]{1,0:T(8,128)S(1)} %slice_add_fusion.1), channel_id=1, source_target_pairs={{0,8},{1,17},{2,10},{3,19},{4,12},{5,21},{6,14},{7,23},{8,0},{9,25... | collective-permute-start | bytes 331784 | tf_op jit(solution)/shard_map/ppermute | solution.py:526
  35.8 21.5 %slice-start = ((s8[5206016]{0:T(1024)(128)(4,1)}), s8[4194304]{0:T(1024)(128)(4,1)S(1)}, s32[]{:S(2)}) async-start(s8[5206016]{0:T(1024)(128)(4,1)} %bitcast.4), calls=%async_computation | async-start | bytes 8388608
  35.9 7.7 %collective-permute-start.8 = (f32[8,3456]{1,0:T(8,128)S(1)}, f32[8,3456]{1,0:T(8,128)S(1)}, u32[]{:S(2)}, u32[]{:S(2)}) collective-permute-start(f32[8,3456]{1,0:T(8,128)S(1)} %slice_add_fusion.2), channel_id=1, source_target_pairs={{0,8},{1,17},{2,10},{3,19},{4,12},{5,21},{6,14},{7,23},{8,0},{9,25... | collective-permute-start | bytes 331784 | tf_op jit(solution)/shard_map/ppermute | solution.py:526
  38.4 5.9 %collective-permute-start.11 = (f32[8,3456]{1,0:T(8,128)S(1)}, f32[8,3456]{1,0:T(8,128)S(1)}, u32[]{:S(2)}, u32[]{:S(2)}) collective-permute-start(f32[8,3456]{1,0:T(8,128)S(1)} %add.62), channel_id=1, source_target_pairs={{0,4},{1,3},{2,6},{3,1},{4,0},{5,7},{6,2},{7,5},{8,12},{9,11},{10,... | collective-permute-start | bytes 331784 | tf_op jit(solution)/shard_map/ppermute | solution.py:526
  39.8 3.7 %collective-permute-start.12 = (f32[8,512]{1,0:T(8,128)S(1)}, f32[8,512]{1,0:T(8,128)S(1)}, u32[]{:S(2)}, u32[]{:S(2)}) collective-permute-start(f32[8,512]{1,0:T(8,128)S(1)} %slice.18), channel_id=1, source_target_pairs={{0,2},{1,3},{2,0},{3,1},{4,6},{5,7},{6,4},{7,5},{8,10},{9,11},{10,... | collective-permute-start | bytes 49160 | tf_op jit(solution)/shard_map/ppermute | solution.py:526
  43.6 4.8 %collective-permute-start.9 = (f32[8,3456]{1,0:T(8,128)S(1)}, f32[8,3456]{1,0:T(8,128)S(1)}, u32[]{:S(2)}, u32[]{:S(2)}) collective-permute-start(f32[8,3456]{1,0:T(8,128)S(1)} %add.59), channel_id=1, source_target_pairs={{0,4},{1,3},{2,6},{3,1},{4,0},{5,7},{6,2},{7,5},{8,12},{9,11},{10,... | collective-permute-start | bytes 331784 | tf_op jit(solution)/shard_map/ppermute | solution.py:526
  44.4 13.0 %slice-start.1 = ((s8[5206016]{0:T(1024)(128)(4,1)}), s8[1011712]{0:T(1024)(128)(4,1)S(1)}, s32[]{:S(2)}) async-start(s8[5206016]{0:T(1024)(128)(4,1)} %bitcast.4), calls=%async_computation.1 | async-start | bytes 2023424
  44.4 13.0 %copy-start = (s32[6]{0:T(128)S(1)}, s32[6]{0:T(128)}, u32[]{:S(2)}) copy-start(s32[6]{0:T(128)} %order_ref.1) | copy-start | bytes 76
  44.4 6.6 %collective-permute-start.14 = (f32[8,3456]{1,0:T(8,128)S(1)}, f32[8,3456]{1,0:T(8,128)S(1)}, u32[]{:S(2)}, u32[]{:S(2)}) collective-permute-start(f32[8,3456]{1,0:T(8,128)S(1)} %add.63), channel_id=1, source_target_pairs={{0,16},{1,9},{2,18},{3,11},{4,20},{5,13},{6,22},{7,15},{8,24},{9,1... | collective-permute-start | bytes 331784 | tf_op jit(solution)/shard_map/ppermute | solution.py:526
  48.4 7.1 %collective-permute-start.13 = (f32[8,3456]{1,0:T(8,128)S(1)}, f32[8,3456]{1,0:T(8,128)S(1)}, u32[]{:S(2)}, u32[]{:S(2)}) collective-permute-start(f32[8,3456]{1,0:T(8,128)S(1)} %add.60), channel_id=1, source_target_pairs={{0,16},{1,9},{2,18},{3,11},{4,20},{5,13},{6,22},{7,15},{8,24},{9,1... | collective-permute-start | bytes 331784 | tf_op jit(solution)/shard_map/ppermute | solution.py:526
  51.0 4.8 %collective-permute-start.15 = (f32[8,3456]{1,0:T(8,128)S(1)}, f32[8,3456]{1,0:T(8,128)S(1)}, u32[]{:S(2)}, u32[]{:S(2)}) collective-permute-start(f32[8,3456]{1,0:T(8,128)S(1)} %add.66), channel_id=1, source_target_pairs={{0,2},{1,5},{2,0},{3,7},{4,6},{5,1},{6,4},{7,3},{8,10},{9,13},{10,... | collective-permute-start | bytes 331784 | tf_op jit(solution)/shard_map/ppermute | solution.py:526
  55.8 1.4 %collective-permute-start.17 = (f32[8,3456]{1,0:T(8,128)S(1)}, f32[8,3456]{1,0:T(8,128)S(1)}, u32[]{:S(2)}, u32[]{:S(2)}) collective-permute-start(f32[8,3456]{1,0:T(8,128)S(1)} %add.67.mine1_ref), channel_id=1, source_target_pairs={{0,1},{1,0},{2,3},{3,2},{4,5},{5,4},{6,7},{7,6},{8,9},{9,8},{10,11... | collective-permute-start | bytes 331784 | tf_op jit(solution)/shard_map/ppermute | solution.py:526
  55.9 1.5 %collective-permute-start.16 = (f32[8,3456]{1,0:T(8,128)S(1)}, f32[8,3456]{1,0:T(8,128)S(1)}, u32[]{:S(2)}, u32[]{:S(2)}) collective-permute-start(f32[8,3456]{1,0:T(8,128)S(1)} %add.65.mine0_ref), channel_id=1, source_target_pairs={{0,1},{1,0},{2,3},{3,2},{4,5},{5,4},{6,7},{7,6},{8,9},{9,8},{10,11... | collective-permute-start | bytes 331784 | tf_op jit(solution)/shard_map/ppermute | solution.py:526
